TPU v7x, 512 devices: a whole 4x4x16 slice. The times are simulated.
512 devices in a mesh: row: 16 (over z), col: 32 (over y, x, core).
Axes of the slice: x: 4, y: 4, z: 16, core: 2. Of those that a mesh axis runs over, the one named last changes fastest.
Arguments:
- flow_state: bfloat16 [131072, 256], P(('col', 'row')), may hold values from -6 to 6
- link_state: bfloat16 [65536, 256], P(('row', 'col')), may hold values from -6 to 6
- incidence: bfloat16 [16, 32, 24, 128, 128], P('row', 'col'), may hold values from -0.29882812 to 0.29882812
- tile_flow: int32 [16, 32, 24], P('row', 'col'), may hold values from 0 to 31
- tile_link: int32 [16, 32, 24], P('row', 'col'), may hold values from 0 to 31
- tile_live: int32 [16, 32, 24], P('row', 'col'), may hold values from 0 to 1, as said below
- link_gain: float32 [256], replicated, may hold values from 0.5 to 2
- link_agg_weight: bfloat16 [256, 256], replicated, may hold values from -0.375 to 0.375
- link_self_weight: bfloat16 [256, 256], replicated, may hold values from -0.375 to 0.375
- link_out_weight: bfloat16 [256, 256], replicated, may hold values from -0.375 to 0.375
- flow_gain: float32 [256], replicated, may hold values from 0.5 to 2
- flow_agg_weight: bfloat16 [256, 256], replicated, may hold values from -0.375 to 0.375
- flow_self_weight: bfloat16 [256, 256], replicated, may hold values from -0.375 to 0.375
- flow_out_weight: bfloat16 [256, 256], replicated, may hold values from -0.375 to 0.375
Outputs:
- link_next: bfloat16 [65536, 256], P(('row', 'col'))
- flow_next: bfloat16 [131072, 256], P(('col', 'row'))
Inputs may be any that keep to these rules, and one draw needn't show every extreme that they name: `tile_live`: in every draw some group pair has all 24 slots live; the number of live slots differs from pair to pair.
All inputs are finite; a program needn't handle non-finite values.
Results may differ from a plain program's by a relative error of at most 0.018.
Values may be sent and summed in bfloat16 or wider, within the bound.
No kernel may reach another device: no remote copies, remote signals or barrier semaphores. Data moves between devices by JAX's collectives and lax.ppermute only.
A program may use at most 64 MiB of HBM per device.

v0:
```python
import jax
import jax.numpy as jnp
from jax import lax
from jax.sharding import PartitionSpec as P

H = 256
BS = 128


def state_update(totals, state, gain, agg_weight, self_weight, out_weight):
    scale = lax.rsqrt(jnp.mean(totals * totals, axis=-1, keepdims=True) + 1e-05)
    normed = (totals * scale * gain).astype(jnp.bfloat16)
    before = jnp.dot(normed, agg_weight, preferred_element_type=jnp.float32) + jnp.dot(
        state, self_weight, preferred_element_type=jnp.float32
    )
    hidden = jax.nn.silu(before).astype(jnp.bfloat16)
    return (
        state.astype(jnp.float32) + jnp.dot(hidden, out_weight, preferred_element_type=jnp.float32)
    ).astype(jnp.bfloat16)


def selector(targets, live_slots, block_count):
    select = (targets[None, :] == jnp.arange(block_count, dtype=jnp.int32)[:, None]).astype(
        jnp.float32
    )
    return select * live_slots.astype(jnp.float32)[None, :]


def on_device(
    flow_state,
    link_state,
    incidence,
    tile_flow,
    tile_link,
    tile_live,
    link_gain,
    link_agg_weight,
    link_self_weight,
    link_out_weight,
    flow_gain,
    flow_agg_weight,
    flow_self_weight,
    flow_out_weight,
):
    coefs = incidence[0, 0]
    flow_slots = tile_flow[0, 0]
    link_slots = tile_link[0, 0]
    live_slots = tile_live[0, 0]
    slot_count = coefs.shape[0]
    flow_blocks_here = flow_state.shape[0] // BS
    link_blocks_here = link_state.shape[0] // BS
    link_blocks = link_blocks_here * lax.axis_size("col")
    flow_group = lax.all_gather(flow_state, "row", axis=0, tiled=True)
    flow_blocks = flow_group.shape[0] // BS
    flow_pieces = jnp.take(flow_group.reshape(flow_blocks, BS, H), flow_slots, axis=0)
    link_terms = jnp.einsum(
        "tij,tih->tjh", coefs, flow_pieces, preferred_element_type=jnp.float32
    ).reshape(slot_count, BS * H)
    link_select = selector(link_slots, live_slots, link_blocks)
    chosen = link_select
    link_sum = lax.psum_scatter(
        jnp.dot(chosen, link_terms, precision=lax.Precision.HIGHEST).astype(jnp.bfloat16),
        "col",
        scatter_dimension=0,
        tiled=True,
    ).astype(jnp.float32)
    link_next = state_update(
        link_sum.reshape(link_blocks_here * BS, H),
        link_state,
        link_gain,
        link_agg_weight,
        link_self_weight,
        link_out_weight,
    )
    link_group = lax.all_gather(link_next, "col", axis=0, tiled=True)
    link_pieces = jnp.take(link_group.reshape(link_blocks, BS, H), link_slots, axis=0)
    flow_terms = jnp.einsum(
        "tij,tjh->tih", coefs, link_pieces, preferred_element_type=jnp.float32
    ).reshape(slot_count, BS * H)
    flow_select = selector(flow_slots, live_slots, flow_blocks)
    chosen = flow_select
    flow_sum = lax.psum_scatter(
        jnp.dot(chosen, flow_terms, precision=lax.Precision.HIGHEST).astype(jnp.bfloat16),
        "row",
        scatter_dimension=0,
        tiled=True,
    ).astype(jnp.float32)
    flow_next = state_update(
        flow_sum.reshape(flow_blocks_here * BS, H),
        flow_state,
        flow_gain,
        flow_agg_weight,
        flow_self_weight,
        flow_out_weight,
    )
    return (link_next, flow_next)


def solution(mesh):
    return jax.shard_map(
        on_device,
        mesh=mesh,
        in_specs=(
            P(("col", "row"), None),
            P(("row", "col"), None),
            P("row", "col", None, None, None),
            P("row", "col", None),
            P("row", "col", None),
            P("row", "col", None),
            P(),
            P(),
            P(),
            P(),
            P(),
            P(),
            P(),
            P(),
        ),
        out_specs=(P(("row", "col"), None), P(("col", "row"), None)),
        check_vma=False,
    )
```

profile of v0, /device:TPU:2, one launch (start us, length us, event | category | flops | bytes accessed | tf_op | source)
XLA Modules:
  0.0 468.4 jit_solution(17944627231696059716)
XLA Ops:
  7.2 0.0 all-gather.3.cloned.1.call-start
  7.2 0.7 all-gather.3.cloned.1.call-update
  7.9 0.0 all-reduce.5.cloned.1.call-start
  8.0 0.7 compare_select_fusion.1
  8.6 0.7 compare_and_fusion.1
  9.3 0.7 convert_bitcast_fusion
  9.9 77.7 %all-gather.3.cloned.1.call-done = bf16[4096,256]{1,0:T(8,128)(2,1)} async-done(((bf16[256,256]{1,0:T(8,128)(2,1)}), bf16[4096,256]{1,0:T(8,128)(2,1)}) %all-gather.3.cloned.1.call-update) | async-done | bytes 2097168 | tf_op jit(solution)/shard_map/all_gather | solution.py:53
  87.7 2.2 gather_fusion
  89.9 2.4 convolution_bitcast_fusion.1
  92.3 3.6 copy.26
  95.9 6.7 %convolution_convert_fusion.1 = bf16[32,32768]{1,0:T(8,128)(2,1)} fusion(f32[24,32768]{1,0:T(8,128)} %bitcast.40, f32[24]{0:T(128)S(1)} %convert_bitcast_fusion, s32[24]{0:T(128)S(1)} %bitcast.45), kind=kOutput, calls=%fused_computation.3 | convolution fusion | flops 303040000 | bytes 5243072 | tf_op jit(solution)/shard_map/dot_general | solution.py:62
  102.6 0.0 all-reduce.5.cloned.1.call-update
  102.6 0.0 all-gather.5.cloned.1.call-start
  102.6 1.4 dynamic-slice
  104.0 133.2 %all-reduce.5.cloned.1.call-done = bf16[32,32768]{1,0:T(8,128)(2,1)} async-done(((bf16[32,32768]{1,0:T(8,128)(2,1)}), bf16[32,32768]{1,0:T(8,128)(2,1)}) %all-reduce.5.cloned.1.call-update) | async-done | bytes 2097168
  237.2 2.1 fusion.11
  239.4 0.1 multiply_reduce_fusion.1
  239.5 0.2 fusion.15
  239.7 0.9 fusion.5
  240.7 0.0 all-reduce.7.cloned.1.call-start
  240.8 59.3 %all-gather.5.cloned.1.call-done = bf16[4096,256]{1,0:T(8,128)(2,1)} async-done(((bf16[128,256]{1,0:T(8,128)(2,1)}), bf16[4096,256]{1,0:T(8,128)(2,1)}) %all-gather.5.cloned.1.call-update) | async-done | bytes 2097168 | tf_op jit(solution)/shard_map/all_gather | solution.py:75
  300.1 2.2 gather_fusion.1
  302.3 2.4 convolution_bitcast_fusion
  304.7 3.6 copy.27
  308.3 6.7 %convolution_convert_fusion = bf16[32,32768]{1,0:T(8,128)(2,1)} fusion(f32[24,32768]{1,0:T(8,128)} %bitcast.39, s32[24]{0:T(128)S(1)} %bitcast.46, f32[24]{0:T(128)S(1)} %convert_bitcast_fusion), kind=kOutput, calls=%fused_computation.2 | convolution fusion | flops 303040000 | bytes 5243072 | tf_op jit(solution)/shard_map/dot_general | solution.py:83
  315.0 1.4 dynamic-slice.2
  317.0 142.1 %all-reduce.7.cloned.1.call-done = bf16[32,32768]{1,0:T(8,128)(2,1)} async-done(((bf16[32,32768]{1,0:T(8,128)(2,1)}), bf16[32,32768]{1,0:T(8,128)(2,1)}) %all-reduce.7.cloned.1.call-update) | async-done | bytes 2097168
  459.0 1.1 dynamic-slice_convert_fusion
  460.2 0.2 reshape.70
  460.4 0.1 multiply_reduce_fusion
  460.6 0.2 fusion.10
  460.8 1.0 fusion.4
  (35 shorter events, 0.2 us)
Async XLA Ops:
  7.2 82.8 %copy-start = (bf16[1,1,24,128,128]{4,3,2,1,0:T(8,128)(2,1)S(1)}, bf16[1,1,24,128,128]{4,3,2,1,0:T(8,128)(2,1)}, u32[]{:S(2)}) copy-start(bf16[1,1,24,128,128]{4,3,2,1,0:T(8,128)(2,1)} %param.18) | copy-start | bytes 2359300
  7.2 80.5 %all-gather.3.cloned.1.call-start = ((), (), s32[]{:S(2)}) async-start(), calls=%async_computation | async-start | bytes 2228224 | tf_op jit(solution)/shard_map/all_gather | solution.py:53
  7.9 229.3 %all-reduce.5.cloned.1.call-start = ((), (), s32[]{:S(2)}) async-start(), calls=%async_computation.2 | async-start | bytes 4194304
  92.3 3.6 copy-start.6
  102.5 136.9 %copy-start.2 = (bf16[256,256]{1,0:T(8,128)(2,1)S(1)}, bf16[256,256]{1,0:T(8,128)(2,1)}, u32[]{:S(2)}) copy-start(bf16[256,256]{1,0:T(8,128)(2,1)} %param.23) | copy-start | bytes 393220
  102.5 137.0 %copy-start.4 = (f32[256]{0:T(256)S(1)}, f32[256]{0:T(256)}, u32[]{:S(2)}) copy-start(f32[256]{0:T(256)} %param.22) | copy-start | bytes 3076
  102.5 137.2 %copy-start.8 = (bf16[256,256]{1,0:T(8,128)(2,1)S(1)}, bf16[256,256]{1,0:T(8,128)(2,1)}, u32[]{:S(2)}) copy-start(bf16[256,256]{1,0:T(8,128)(2,1)} %param.25) | copy-start | bytes 393220
  102.5 137.2 %copy-start.9 = (bf16[256,256]{1,0:T(8,128)(2,1)S(1)}, bf16[256,256]{1,0:T(8,128)(2,1)}, u32[]{:S(2)}) copy-start(bf16[256,256]{1,0:T(8,128)(2,1)} %param.24) | copy-start | bytes 393220
  102.5 137.2 %copy-start.12 = (bf16[128,256]{1,0:T(8,128)(2,1)S(1)}, bf16[128,256]{1,0:T(8,128)(2,1)}, u32[]{:S(2)}) copy-start(bf16[128,256]{1,0:T(8,128)(2,1)} %param.17) | copy-start | bytes 196612
  102.6 197.5 %all-gather.5.cloned.1.call-start = ((), (), s32[]{:S(2)}) async-start(), calls=%async_computation.1 | async-start | bytes 2162688 | tf_op jit(solution)/shard_map/all_gather | solution.py:75
  240.7 218.3 %all-reduce.7.cloned.1.call-start = ((), (), s32[]{:S(2)}) async-start(), calls=%async_computation.3 | async-start | bytes 4194304
  304.7 3.6 copy-start.7
  314.9 145.6 %copy-start.1 = (bf16[256,256]{1,0:T(8,128)(2,1)S(1)}, bf16[256,256]{1,0:T(8,128)(2,1)}, u32[]{:S(2)}) copy-start(bf16[256,256]{1,0:T(8,128)(2,1)} %param.27) | copy-start | bytes 393220
  314.9 145.6 %copy-start.5 = (f32[256]{0:T(256)S(1)}, f32[256]{0:T(256)}, u32[]{:S(2)}) copy-start(f32[256]{0:T(256)} %param.26) | copy-start | bytes 3076
  314.9 145.9 %copy-start.3 = (bf16[256,256]{1,0:T(8,128)(2,1)S(1)}, bf16[256,256]{1,0:T(8,128)(2,1)}, u32[]{:S(2)}) copy-start(bf16[256,256]{1,0:T(8,128)(2,1)} %param.16) | copy-start | bytes 393220
  314.9 145.9 %copy-start.10 = (bf16[256,256]{1,0:T(8,128)(2,1)S(1)}, bf16[256,256]{1,0:T(8,128)(2,1)}, u32[]{:S(2)}) copy-start(bf16[256,256]{1,0:T(8,128)(2,1)} %param.29) | copy-start | bytes 393220
  314.9 145.9 %copy-start.11 = (bf16[256,256]{1,0:T(8,128)(2,1)S(1)}, bf16[256,256]{1,0:T(8,128)(2,1)}, u32[]{:S(2)}) copy-start(bf16[256,256]{1,0:T(8,128)(2,1)} %param.28) | copy-start | bytes 393220
Sparse Core Ops, SparseCore 0:
  10.1 77.5 all-gather.2
  102.7 134.4 all-reduce.4
  240.9 59.1 all-gather.4
  315.1 143.8 all-reduce.6
where the time goes:
time: 469 us; the launch traced here: 468 us
  waiting for transfers between devices  413 us (88%)
  matrix products  20.5 us (4%)
  local copies, waits for them, and re-layouts  14.7 us (3%)
  between operations  14.6 us (3%)
  other arithmetic  5.46 us (1%)
    unnamed x6, waiting for transfers between devices  276 us
    all_gather x1, waiting for transfers between devices, on_device(): flow_group = lax.all_gather(flow_state, 'row', axis=0, tiled=True)  77.7 us
    all_gather x1, waiting for transfers between devices, on_device(): link_group = lax.all_gather(link_next, 'col', axis=0, tiled=True)  59.3 us
    unnamed x30, local copies, waits for them, and re-layouts  9.94 us
  transfers between devices with their start and end apart: 4, of which 4 were waited for; matrix products, arithmetic and copies ran while one was open for 1% of the time, Pallas kernels for 0%

commit v1 on v0

v1 whole, which is shorter than its diff:
```python
import functools
import jax
import jax.numpy as jnp
from jax import lax
from jax.experimental import pallas as pl
from jax.experimental.pallas import tpu as pltpu
from jax.sharding import PartitionSpec as P

H = 256
BS = 128
VMEM = pl.BlockSpec(memory_space=pltpu.VMEM)
SMEM = pl.BlockSpec(memory_space=pltpu.SMEM)


def products_kernel(to_links, take_ref, put_ref, live_ref, coefs_ref, pieces_ref, out_ref, acc_ref):
    blocks = out_ref.shape[0]
    acc_ref[...] = jnp.zeros_like(acc_ref)
    for slot in range(coefs_ref.shape[0]):
        put = jnp.where(live_ref[0, 0, slot] == 1, put_ref[0, 0, slot], blocks)
        term = lax.dot_general(
            coefs_ref[slot],
            pieces_ref[take_ref[0, 0, slot]],
            (((0 if to_links else 1,), (0,)), ((), ())),
            preferred_element_type=jnp.float32,
        )
        acc_ref[put] += term
    out_ref[...] = acc_ref[:blocks].astype(out_ref.dtype)


def products(to_links, take, put, live, coefs, pieces, blocks):
    width = pieces.shape[-1]
    return pl.pallas_call(
        functools.partial(products_kernel, to_links),
        out_shape=jax.ShapeDtypeStruct((blocks, BS, width), jnp.bfloat16),
        in_specs=[SMEM, SMEM, SMEM, VMEM, VMEM],
        out_specs=VMEM,
        scratch_shapes=[pltpu.VMEM((blocks + 1, BS, width), jnp.float32)],
        compiler_params=pltpu.CompilerParams(vmem_limit_bytes=32 << 20),
        name="link_products" if to_links else "flow_products",
    )(take, put, live, coefs, pieces)


def update_kernel(parts_ref, state_ref, gain_ref, agg_ref, self_ref, out_w_ref, *out_refs):
    totals = jnp.sum(parts_ref[...].astype(jnp.float32), axis=0)
    scale = lax.rsqrt(jnp.mean(totals * totals, axis=-1, keepdims=True) + 1e-05)
    normed = (totals * scale * gain_ref[...]).astype(jnp.bfloat16)
    before = jnp.dot(normed, agg_ref[...], preferred_element_type=jnp.float32) + jnp.dot(
        state_ref[...], self_ref[...], preferred_element_type=jnp.float32
    )
    hidden = jax.nn.silu(before).astype(jnp.bfloat16)
    result = (
        state_ref[...].astype(jnp.float32)
        + jnp.dot(hidden, out_w_ref[...], preferred_element_type=jnp.float32)
    ).astype(jnp.bfloat16)
    out_refs[0][...] = result
    if len(out_refs) > 1:
        for copy in range(out_refs[1].shape[0]):
            out_refs[1][copy] = result


def update(parts, state, gain, agg_weight, self_weight, out_weight, copies):
    shapes = [jax.ShapeDtypeStruct(state.shape, jnp.bfloat16)]
    if copies:
        shapes.append(jax.ShapeDtypeStruct((copies,) + state.shape, jnp.bfloat16))
    return pl.pallas_call(
        update_kernel,
        out_shape=shapes,
        in_specs=[VMEM] * 6,
        out_specs=[VMEM] * len(shapes),
        compiler_params=pltpu.CompilerParams(vmem_limit_bytes=32 << 20),
        name="link_update" if copies else "flow_update",
    )(parts, state, gain.reshape(1, H), agg_weight, self_weight, out_weight)


def on_device(
    flow_state,
    link_state,
    incidence,
    tile_flow,
    tile_link,
    tile_live,
    link_gain,
    link_agg_weight,
    link_self_weight,
    link_out_weight,
    flow_gain,
    flow_agg_weight,
    flow_self_weight,
    flow_out_weight,
):
    coefs = incidence[0, 0]
    cols = lax.axis_size("col")
    rows = lax.axis_size("row")
    flow_group = lax.all_gather(flow_state, "row", axis=0, tiled=True)
    flow_blocks = flow_state.shape[0] // BS * rows
    link_blocks = link_state.shape[0] // BS * cols
    link_part = products(
        True, tile_flow, tile_link, tile_live, coefs,
        flow_group.reshape(flow_blocks, BS, H), link_blocks,
    )
    link_parts = lax.all_to_all(link_part, "col", 0, 0, tiled=True)
    link_next, link_copies = update(
        link_parts, link_state, link_gain, link_agg_weight, link_self_weight, link_out_weight, cols
    )
    link_group = lax.all_to_all(link_copies, "col", 0, 0, tiled=True)
    flow_part = products(
        False, tile_link, tile_flow, tile_live, coefs, link_group, flow_blocks
    )
    flow_sum = lax.psum_scatter(
        flow_part.reshape(flow_blocks * BS, H), "row", scatter_dimension=0, tiled=True
    )
    (flow_next,) = update(
        flow_sum[None], flow_state, flow_gain, flow_agg_weight, flow_self_weight, flow_out_weight, 0
    )
    return (link_next, flow_next)


def solution(mesh):
    return jax.shard_map(
        on_device,
        mesh=mesh,
        in_specs=(
            P(("col", "row"), None),
            P(("row", "col"), None),
            P("row", "col", None, None, None),
            P("row", "col", None),
            P("row", "col", None),
            P("row", "col", None),
            P(),
            P(),
            P(),
            P(),
            P(),
            P(),
            P(),
            P(),
        ),
        out_specs=(P(("row", "col"), None), P(("col", "row"), None)),
        check_vma=False,
    )
```

time: 469 us -> 242 us (0.52)
  waiting for transfers between devices: 413 us -> 148 us
  blocking collectives: 0 us -> 66.8 us
  matrix products: 20.5 us -> 0 us
  local copies, waits for them, and re-layouts: 14.7 us -> 5.65 us
  Pallas kernels: 0 us -> 7 us
  other arithmetic: 5.46 us -> 0 us
    unnamed x6 -> x2, waiting for transfers between devices: 276 us -> 0.7 us
    reduce_scatter x0 -> x1, waiting for transfers between devices: none -> 68 us  [on_device(): lax.psum_scatter(flow_part.reshape(flow_blocks * BS, H), 'row', scatter_d...]
    all_to_all x0 -> x2, blocking collectives: none -> 66.8 us  [the longest x1 34.7 us: on_device(): link_parts = lax.all_to_all(link_part, 'col', 0, 0, tiled=True)]
    all_gather x1 -> x0, waiting for transfers between devices: 59.3 us -> none  [on_device(): link_group = lax.all_gather(link_next, 'col', axis=0, tiled=True)]
    dot_general x8 -> x0, matrix products: 20.5 us -> none  [the longest x1 6.66 us: on_device(): jnp.dot(chosen, link_terms, precision=lax.Precision.HIGHEST)]
    pallas_call x0 -> x4, Pallas kernels: none -> 7 us  [the longest x2 4.51 us: products(): pl.pallas_call(functools.partial(products_kernel, to_links), out_shape=ja...]
    unnamed x30 -> x40, local copies, waits for them, and re-layouts: 9.94 us -> 5.65 us
  transfers between devices with their start and end apart: 4 -> 2, of which waited for: 4 -> 2; matrix products, arithmetic and copies ran while one was open for 1% -> 0% of each run, Pallas kernels for 0% -> 0%
where the time goes in v1:
time: 242 us
  waiting for transfers between devices  148 us (61%)
  blocking collectives  66.8 us (28%)
  between operations  14.2 us (6%)
  Pallas kernels  7 us (3%)
  local copies, waits for them, and re-layouts  5.65 us (2%)
    all_gather x1, waiting for transfers between devices, on_device(): flow_group = lax.all_gather(flow_state, 'row', axis=0, tiled=True)  79.7 us
    reduce_scatter x1, waiting for transfers between devices, on_device(): lax.psum_scatter(flow_part.reshape(flow_blocks * BS, H), 'row', scatter_d...  68 us
    all_to_all x1, blocking collectives, on_device(): link_parts = lax.all_to_all(link_part, 'col', 0, 0, tiled=True)  34.7 us
    all_to_all x1, blocking collectives, on_device(): link_group = lax.all_to_all(link_copies, 'col', 0, 0, tiled=True)  32.1 us
    unnamed x40, local copies, waits for them, and re-layouts  5.65 us
  transfers between devices with their start and end apart: 2, of which 2 were waited for; matrix products, arithmetic and copies ran while one was open for 0% of the time, Pallas kernels for 0%

profile of v1, /device:TPU:2, one launch (start us, length us, event | category | flops | bytes accessed | tf_op | source)
XLA Modules:
  0.0 242.1 jit_solution(6487907920033924353)
XLA Ops:
  7.2 0.0 all-gather.2.cloned.1.call-start
  7.2 0.7 all-gather.2.cloned.1.call-update
  7.9 0.0 reduce-scatter.2.cloned.1.call-start
  7.9 79.7 %all-gather.2.cloned.1.call-done = bf16[4096,256]{1,0:T(8,128)(2,1)} async-done(((bf16[256,256]{1,0:T(8,128)(2,1)}), bf16[4096,256]{1,0:T(8,128)(2,1)}) %all-gather.2.cloned.1.call-update) | async-done | bytes 2097168 | tf_op jit(solution)/shard_map/all_gather | solution.py:94
  87.7 1.1 copy-done
  88.8 1.6 copy-done.2
  90.4 0.7 copy-done.12
  91.0 0.7 copy-done.14
  91.7 0.7 copy-done.16
  92.4 1.6 link_products.1
  94.0 0.0 copy-start.4
  94.0 0.0 copy-start.5
  94.0 0.0 copy-start.6
  94.0 0.0 copy-start.11
  94.0 0.0 copy-start.18
  94.0 34.7 %all_to_all.10.parts_ref = bf16[32,128,256]{2,1,0:T(8,128)(2,1)S(1)} all-to-all(bf16[32,128,256]{2,1,0:T(8,128)(2,1)S(1)} %link_products.1), channel_id=1, replica_groups=mesh['row'=16,'col'=32] {'col'}, dimensions={0} | all-to-all | bytes 4194304 | tf_op jit(solution)/shard_map/all_to_all | solution.py:101
  128.7 0.0 copy-done.4
  128.7 0.0 copy-done.5
  128.7 0.0 copy-done.6
  128.7 0.0 copy-done.11
  128.8 0.0 copy-done.18
  128.8 1.4 link_update.1
  130.2 32.1 %all_to_all.11.pieces_ref = bf16[32,128,256]{2,1,0:T(8,128)(2,1)S(1)} all-to-all(bf16[32,128,256]{2,1,0:T(8,128)(2,1)S(1)} %get-tuple-element.5), channel_id=1, replica_groups=mesh['row'=16,'col'=32] {'col'}, dimensions={0} | all-to-all | bytes 4194304 | tf_op jit(solution)/shard_map/all_to_all | solution.py:105
  162.3 0.0 copy-done.1
  162.3 0.0 copy-done.13
  162.3 0.0 copy-done.15
  162.3 2.9 %flow_products.1 = bf16[32,128,256]{2,1,0:T(8,128)(2,1)} custom-call(s32[1,1,24]{2,1,0:T(1,128)S(1)} %copy-done.15, s32[1,1,24]{2,1,0:T(1,128)S(1)} %copy-done.13, s32[1,1,24]{2,1,0:T(1,128)S(1)} %copy-done.17, bf16[24,128,128]{2,1,0:T(8,128)(2,1)S(1)} %bitcast.7, bf16[32,128,256]{2,1,0:T(8,128)(2,1)S(1)} %all_to_all.11.pieces_ref), custom_call_target="tpu_custom_call" | custom-call | tf_op jit(solution)/shard_map/flow_products/pallas_call | solution.py:32
  165.2 0.0 copy-start.19
  165.2 0.0 reduce-scatter.2.cloned.1.call-update
  165.2 68.0 %reduce-scatter.2.cloned.1.call-done = bf16[256,256]{1,0:T(8,128)(2,1)} async-done(((bf16[4096,256]{1,0:T(8,128)(2,1)}), bf16[256,256]{1,0:T(8,128)(2,1)}) %reduce-scatter.2.cloned.1.call-update) | async-done | bytes 131088 | tf_op jit(solution)/shard_map/reduce_scatter | solution.py:109
  233.3 0.9 copy-done.10
  234.2 1.1 flow_update.1
  (20 shorter events, 0.0 us)
Async XLA Ops:
  7.2 80.5 %all-gather.2.cloned.1.call-start = ((), (), s32[]{:S(2)}) async-start(), calls=%async_computation.3 | async-start | bytes 2228224 | tf_op jit(solution)/shard_map/all_gather | solution.py:94
  7.9 225.3 %reduce-scatter.2.cloned.1.call-start = ((), (), s32[]{:S(2)}) async-start(), calls=%async_computation.4 | async-start | bytes 2228224 | tf_op jit(solution)/shard_map/reduce_scatter | solution.py:109
  87.7 1.1 copy-start
  88.8 1.6 copy-start.2
  90.4 0.7 copy-start.12
  91.0 0.7 copy-start.14
  91.7 0.7 copy-start.16
  94.0 34.8 %copy-start.4 = (bf16[256,256]{1,0:T(8,128)(2,1)S(1)}, bf16[256,256]{1,0:T(8,128)(2,1)}, u32[]{:S(2)}) copy-start(bf16[256,256]{1,0:T(8,128)(2,1)} %agg_ref.2) | copy-start | bytes 393220
  94.0 34.7 %copy-start.5 = (bf16[256,256]{1,0:T(8,128)(2,1)S(1)}, bf16[256,256]{1,0:T(8,128)(2,1)}, u32[]{:S(2)}) copy-start(bf16[256,256]{1,0:T(8,128)(2,1)} %self_ref.2) | copy-start | bytes 393220
  94.0 34.7 %copy-start.6 = (bf16[256,256]{1,0:T(8,128)(2,1)S(1)}, bf16[256,256]{1,0:T(8,128)(2,1)}, u32[]{:S(2)}) copy-start(bf16[256,256]{1,0:T(8,128)(2,1)} %out_w_ref.2) | copy-start | bytes 393220
  94.0 34.7 %copy-start.11 = (bf16[128,256]{1,0:T(8,128)(2,1)S(1)}, bf16[128,256]{1,0:T(8,128)(2,1)}, u32[]{:S(2)}) copy-start(bf16[128,256]{1,0:T(8,128)(2,1)} %state_ref.2) | copy-start | bytes 196612
  94.0 34.7 %copy-start.18 = (f32[256]{0:T(256)S(1)}, f32[256]{0:T(256)}, u32[]{:S(2)}) copy-start(f32[256]{0:T(256)} %param.20) | copy-start | bytes 3076
  130.2 32.1 %copy-start.1 = (bf16[1,1,24,128,128]{4,3,2,1,0:T(8,128)(2,1)S(1)}, bf16[1,1,24,128,128]{4,3,2,1,0:T(8,128)(2,1)}, u32[]{:S(2)}) copy-start(bf16[1,1,24,128,128]{4,3,2,1,0:T(8,128)(2,1)} %param.16) | copy-start | bytes 2359300
  130.2 32.1 %copy-start.13 = (s32[1,1,24]{2,1,0:T(1,128)S(1)}, s32[1,1,24]{2,1,0:T(1,128)}, u32[]{:S(2)}) copy-start(s32[1,1,24]{2,1,0:T(1,128)} %put_ref.3) | copy-start | bytes 292
  130.2 32.1 %copy-start.15 = (s32[1,1,24]{2,1,0:T(1,128)S(1)}, s32[1,1,24]{2,1,0:T(1,128)}, u32[]{:S(2)}) copy-start(s32[1,1,24]{2,1,0:T(1,128)} %take_ref.3) | copy-start | bytes 292
  130.2 32.1 %copy-start.17 = (s32[1,1,24]{2,1,0:T(1,128)S(1)}, s32[1,1,24]{2,1,0:T(1,128)}, u32[]{:S(2)}) copy-start(s32[1,1,24]{2,1,0:T(1,128)} %live_ref.3) | copy-start | bytes 292
  165.2 68.1 %copy-start.3 = (bf16[256,256]{1,0:T(8,128)(2,1)S(1)}, bf16[256,256]{1,0:T(8,128)(2,1)}, u32[]{:S(2)}) copy-start(bf16[256,256]{1,0:T(8,128)(2,1)} %state_ref.3) | copy-start | bytes 393220
  165.2 68.1 %copy-start.7 = (bf16[256,256]{1,0:T(8,128)(2,1)S(1)}, bf16[256,256]{1,0:T(8,128)(2,1)}, u32[]{:S(2)}) copy-start(bf16[256,256]{1,0:T(8,128)(2,1)} %agg_ref.3) | copy-start | bytes 393220
  165.2 68.1 %copy-start.8 = (bf16[256,256]{1,0:T(8,128)(2,1)S(1)}, bf16[256,256]{1,0:T(8,128)(2,1)}, u32[]{:S(2)}) copy-start(bf16[256,256]{1,0:T(8,128)(2,1)} %self_ref.3) | copy-start | bytes 393220
  165.2 68.1 %copy-start.9 = (bf16[256,256]{1,0:T(8,128)(2,1)S(1)}, bf16[256,256]{1,0:T(8,128)(2,1)}, u32[]{:S(2)}) copy-start(bf16[256,256]{1,0:T(8,128)(2,1)} %out_w_ref.3) | copy-start | bytes 393220
  165.2 68.1 %copy-start.19 = (f32[256]{0:T(256)S(1)}, f32[256]{0:T(256)}, u32[]{:S(2)}) copy-start(f32[256]{0:T(256)} %param.24) | copy-start | bytes 3076
  233.3 0.9 copy-start.10
Sparse Core Ops, SparseCore 0:
  10.1 77.5 all-gather.1
  165.3 67.8 reduce-scatter.1

commit v2 on v1

v2 whole, which is shorter than its diff:
```python
import functools
import jax
import jax.numpy as jnp
from jax import lax
from jax.experimental import pallas as pl
from jax.experimental.pallas import tpu as pltpu
from jax.sharding import PartitionSpec as P

H = 256
BS = 128
VMEM = pl.BlockSpec(memory_space=pltpu.VMEM)
SMEM = pl.BlockSpec(memory_space=pltpu.SMEM)
PARAMS = pltpu.CompilerParams(vmem_limit_bytes=40 << 20)
F32 = jnp.float32
BF16 = jnp.bfloat16
SCALE = 8192.0


def link_products_kernel(
    me_ref, flow_ref, link_ref, live_ref, coefs_ref, pieces_ref, own_ref, other_ref, acc_ref
):
    blocks = acc_ref.shape[0] - 1
    half = blocks // 2
    acc_ref[...] = jnp.zeros_like(acc_ref)
    for slot in range(coefs_ref.shape[0]):
        block = link_ref[0, 0, slot]
        place = ((block + me_ref[1]) % 2) * half + block // 2
        place = jnp.where(live_ref[0, 0, slot] == 1, place, blocks)
        acc_ref[place] += lax.dot_general(
            coefs_ref[slot],
            pieces_ref[flow_ref[0, 0, slot]],
            (((0,), (0,)), ((), ())),
            preferred_element_type=F32,
        )
    own_ref[...] = acc_ref[:half].astype(BF16)
    other_ref[...] = acc_ref[half : 2 * half].astype(BF16)


def link_products(me, flow, link, live, coefs, pieces, blocks):
    shape = jax.ShapeDtypeStruct((blocks // 2, BS, H), BF16)
    return pl.pallas_call(
        link_products_kernel,
        out_shape=[shape, shape],
        in_specs=[SMEM, SMEM, SMEM, SMEM, VMEM, VMEM],
        out_specs=[VMEM, VMEM],
        scratch_shapes=[pltpu.VMEM((blocks + 1, BS, H), F32)],
        compiler_params=PARAMS,
        name="link_products",
    )(me, flow, link, live, coefs, pieces)


def flow_products_kernel(
    me_ref, flow_ref, link_ref, live_ref, coefs_ref, own_ref, other_ref,
    same_ref, next_ref, far_up_ref, far_down_ref, prev_ref, acc_ref, pieces_ref,
):
    blocks = acc_ref.shape[0] - 1
    quarter = blocks // 4
    half = own_ref.shape[0]
    pieces_ref[:half] = own_ref[...]
    pieces_ref[half:] = other_ref[...]
    acc_ref[...] = jnp.zeros_like(acc_ref)
    for slot in range(coefs_ref.shape[0]):
        block = flow_ref[0, 0, slot]
        row = block // 2
        place = ((row - me_ref[0] + 16) % 4) * quarter + (row // 4) * 2 + block % 2
        place = jnp.where(live_ref[0, 0, slot] == 1, place, blocks)
        piece = link_ref[0, 0, slot]
        piece = ((piece + me_ref[1]) % 2) * half + piece // 2
        acc_ref[place] += jnp.dot(
            coefs_ref[slot], pieces_ref[piece], preferred_element_type=F32
        )
    low = quarter // 2
    same_ref[...] = acc_ref[:quarter].astype(BF16)
    next_ref[...] = acc_ref[quarter : 2 * quarter].astype(BF16)
    far_up_ref[...] = acc_ref[2 * quarter : 2 * quarter + low].astype(BF16)
    far_down_ref[...] = acc_ref[2 * quarter + low : 3 * quarter].astype(BF16)
    prev_ref[...] = acc_ref[3 * quarter : 4 * quarter].astype(BF16)


def flow_products(me, flow, link, live, coefs, own, other, blocks):
    whole = jax.ShapeDtypeStruct((blocks // 4, BS, H), BF16)
    part = jax.ShapeDtypeStruct((blocks // 8, BS, H), BF16)
    return pl.pallas_call(
        flow_products_kernel,
        out_shape=[whole, whole, part, part, whole],
        in_specs=[SMEM, SMEM, SMEM, SMEM, VMEM, VMEM, VMEM],
        out_specs=[VMEM] * 5,
        scratch_shapes=[
            pltpu.VMEM((blocks + 1, BS, H), F32),
            pltpu.VMEM((2 * own.shape[0], BS, H), BF16),
        ],
        compiler_params=PARAMS,
        name="flow_products",
    )(me, flow, link, live, coefs, own, other)


def add_kernel(a_ref, b_ref, out_ref):
    out_ref[...] = (a_ref[...].astype(F32) + b_ref[...].astype(F32)).astype(BF16)


def add_two(a, b):
    return pl.pallas_call(
        add_kernel,
        out_shape=jax.ShapeDtypeStruct(a.shape, BF16),
        in_specs=[VMEM, VMEM],
        out_specs=VMEM,
        compiler_params=PARAMS,
        name="add_two",
    )(a, b)


def relay_kernel(up_ref, low_ref, down_ref, high_ref, up_out_ref, down_out_ref):
    half = low_ref.shape[0]
    up_out_ref[:half] = (up_ref[:half].astype(F32) + low_ref[...].astype(F32)).astype(BF16)
    up_out_ref[half:] = up_ref[half:]
    down_out_ref[:half] = down_ref[:half]
    down_out_ref[half:] = (down_ref[half:].astype(F32) + high_ref[...].astype(F32)).astype(BF16)


def relay(up, low, down, high):
    return pl.pallas_call(
        relay_kernel,
        out_shape=[jax.ShapeDtypeStruct(up.shape, BF16)] * 2,
        in_specs=[VMEM] * 4,
        out_specs=[VMEM] * 2,
        compiler_params=PARAMS,
        name="relay",
    )(up, low, down, high)


def add_three_kernel(a_ref, b_ref, c_ref, out_ref):
    out_ref[...] = (
        a_ref[...].astype(F32) + b_ref[...].astype(F32) + c_ref[...].astype(F32)
    ).astype(BF16)


def add_three(a, b, c):
    return pl.pallas_call(
        add_three_kernel,
        out_shape=jax.ShapeDtypeStruct(a.shape, BF16),
        in_specs=[VMEM] * 3,
        out_specs=VMEM,
        compiler_params=PARAMS,
        name="add_three",
    )(a, b, c)


def update_kernel(parts_ref, state_ref, gain_ref, agg_ref, self_ref, out_w_ref, *out_refs):
    totals = jnp.sum(parts_ref[...].astype(F32), axis=0)
    scale = lax.rsqrt(jnp.mean(totals * totals, axis=-1, keepdims=True) + 1e-05)
    normed = (totals * scale * gain_ref[...]).astype(BF16)
    before = jnp.dot(normed, agg_ref[...], preferred_element_type=F32) + jnp.dot(
        state_ref[...], self_ref[...], preferred_element_type=F32
    )
    hidden = jax.nn.silu(before).astype(BF16)
    result = (
        state_ref[...].astype(F32)
        + jnp.dot(hidden, out_w_ref[...], preferred_element_type=F32)
    ).astype(BF16)
    out_refs[0][...] = result
    if len(out_refs) > 1:
        for copy in range(out_refs[1].shape[0]):
            out_refs[1][copy] = result


def update(parts, state, gain, agg_weight, self_weight, out_weight, copies):
    shapes = [jax.ShapeDtypeStruct(state.shape, BF16)]
    if copies:
        shapes.append(jax.ShapeDtypeStruct((copies,) + state.shape, BF16))
    return pl.pallas_call(
        update_kernel,
        out_shape=shapes,
        in_specs=[VMEM] * 6,
        out_specs=[VMEM] * len(shapes),
        compiler_params=PARAMS,
        name="link_update" if copies else "flow_update",
    )(parts, state, gain.reshape(1, H), agg_weight, self_weight, out_weight)


def on_device(
    flow_state,
    link_state,
    incidence,
    tile_flow,
    tile_link,
    tile_live,
    link_gain,
    link_agg_weight,
    link_self_weight,
    link_out_weight,
    flow_gain,
    flow_agg_weight,
    flow_self_weight,
    flow_out_weight,
):
    coefs = incidence[0, 0]
    cols = lax.axis_size("col")
    rows = lax.axis_size("row")
    pairs = cols // 2
    flow_blocks = flow_state.shape[0] // BS * rows
    me = jnp.stack([lax.axis_index("row"), lax.axis_index("col") % 2]).astype(jnp.int32)
    sibling = [(i, i ^ 1) for i in range(cols)]
    same_core = [[2 * i + core for i in range(pairs)] for core in range(2)]
    up = [(i, (i + 1) % rows) for i in range(rows)]
    down = [(i, (i - 1) % rows) for i in range(rows)]
    far = [[4 * a + b for a in range(rows // 4)] for b in range(4)]

    flow_group = gather_rows(flow_state)
    own, other = link_products(
        me, tile_flow, tile_link, tile_live, coefs,
        flow_group.reshape(flow_blocks, BS, H), cols,
    )
    own = add_two(own, lax.ppermute(other, "col", sibling))
    link_parts = lax.all_to_all(own, "col", 0, 0, tiled=True, axis_index_groups=same_core)
    link_next, link_copies = update(
        link_parts, link_state, link_gain, link_agg_weight, link_self_weight, link_out_weight, pairs
    )
    own = lax.all_to_all(link_copies, "col", 0, 0, tiled=True, axis_index_groups=same_core)
    other = lax.ppermute(own, "col", sibling)
    same, nxt, low, high, prev = flow_products(
        me, tile_flow, tile_link, tile_live, coefs, own, other, flow_blocks
    )
    low = lax.ppermute(low, "row", up)
    high = lax.ppermute(high, "row", down)
    nxt, prev = relay(nxt, low, prev, high)
    nxt = lax.ppermute(nxt, "row", up)
    prev = lax.ppermute(prev, "row", down)
    same = add_three(same, nxt, prev)
    per = flow_state.shape[0]
    flow_parts = lax.all_to_all(
        same.reshape(rows // 4, per, H), "row", 0, 0, tiled=True, axis_index_groups=far
    )
    (flow_next,) = update(
        flow_parts, flow_state, flow_gain, flow_agg_weight, flow_self_weight, flow_out_weight, 0
    )
    return (link_next, flow_next)


def gather_rows(state):
    sent = (state.astype(F32) * SCALE).astype(jnp.float16)
    got = lax.all_gather(sent, "row", axis=0, tiled=True)
    return (got.astype(F32) * (1 / SCALE)).astype(BF16)


def solution(mesh):
    return jax.shard_map(
        on_device,
        mesh=mesh,
        in_specs=(
            P(("col", "row"), None),
            P(("row", "col"), None),
            P("row", "col", None, None, None),
            P("row", "col", None),
            P("row", "col", None),
            P("row", "col", None),
            P(),
            P(),
            P(),
            P(),
            P(),
            P(),
            P(),
            P(),
        ),
        out_specs=(P(("row", "col"), None), P(("col", "row"), None)),
        check_vma=False,
    )
```

time: 242 us -> 179 us (0.74)
  the two profiles are of different devices: /device:TPU:2 before, /device:TPU:32 now
where the time goes in v2:
time: 179 us
  blocking collectives  130 us (73%)
  waiting for transfers between devices  24.5 us (14%)
  starting transfers between devices  15.6 us (9%)
  Pallas kernels  6.23 us (3%)
    all_gather x1, blocking collectives, gather_rows(): got = lax.all_gather(sent, 'row', axis=0, tiled=True)  47.7 us
    all_to_all x1, blocking collectives, on_device(): lax.all_to_all(same.reshape(rows // 4, per, H), 'row', 0, 0, tiled=True,...  38.1 us
    all_to_all x1, blocking collectives, on_device(): lax.all_to_all(own, 'col', 0, 0, tiled=True, axis_index_groups=same_core)  24.3 us
    all_to_all x1, blocking collectives, on_device(): lax.all_to_all(link_copies, 'col', 0, 0, tiled=True, axis_index_groups=sa...  19.6 us
    ppermute x1, waiting for transfers between devices, on_device(): nxt = lax.ppermute(nxt, 'row', up)  9.06 us
    ppermute x1, waiting for transfers between devices, on_device(): low = lax.ppermute(low, 'row', up)  4.37 us
    ppermute x1, waiting for transfers between devices, on_device(): prev = lax.ppermute(prev, 'row', down)  3.63 us
  transfers between devices with their start and end apart: 6, of which 6 were waited for; matrix products, arithmetic and copies ran while one was open for 0% of the time, Pallas kernels for 0%

profile of v2, /device:TPU:32, one launch (start us, length us, event | category | flops | bytes accessed | tf_op | source)
XLA Modules:
  0.0 179.0 jit_solution(2871067766306275019)
XLA Ops:
  0.6 0.9 multiply_convert_fusion.1
  1.6 47.7 %all-gather.1 = f16[4096,256]{1,0:T(8,128)(2,1)S(1)} all-gather(f16[256,256]{1,0:T(8,128)(2,1)S(1)} %multiply_convert_fusion.1), channel_id=1, replica_groups=mesh['row'=16,'col'=32] {'row'}, dimensions={0}, use_global_device_ids=true | all-gather | bytes 2228224 | tf_op jit(solution)/shard_map/all_gather | solution.py:241
  49.3 0.6 multiply_convert_fusion
  49.9 0.1 pad_add_fusion.me_ref
  50.0 0.5 copy-done
  50.4 0.0 copy-done.11
  50.4 1.6 link_products.1
  52.0 1.9 %collective-permute-start = (bf16[16,128,256]{2,1,0:T(8,128)(2,1)S(1)}, bf16[16,128,256]{2,1,0:T(8,128)(2,1)S(1)}, u32[]{:S(2)}, u32[]{:S(2)}) collective-permute-start(bf16[16,128,256]{2,1,0:T(8,128)(2,1)S(1)} %get-tuple-element.14), channel_id=1, source_target_pairs={{0,1},{1,0},{2,3},{3,2},{4,5},{5,4},{6,7},{7,6},{8,9},{9,8},{10,11... | collective-permute-start | bytes 3145736 | tf_op jit(solution)/shard_map/ppermute | solution.py:213
  54.0 2.6 %collective-permute-done.b_ref = bf16[16,128,256]{2,1,0:T(8,128)(2,1)S(1)} collective-permute-done((bf16[16,128,256]{2,1,0:T(8,128)(2,1)S(1)}, bf16[16,128,256]{2,1,0:T(8,128)(2,1)S(1)}, u32[]{:S(2)}, u32[]{:S(2)}) %collective-permute-start) | collective-permute-done | bytes 1048608 | tf_op jit(solution)/shard_map/ppermute | solution.py:213
  56.6 0.0 copy-start.12
  56.6 0.2 add_two.1
  56.9 24.3 %all_to_all.15.parts_ref = bf16[16,128,256]{2,1,0:T(8,128)(2,1)S(1)} all-to-all(bf16[16,128,256]{2,1,0:T(8,128)(2,1)S(1)} %add_two.1), channel_id=1, replica_groups={{0,2,4,6,8,10,12,14,16,18,20,22,24,26,28,30},{1,3,5,7,9,11,13,15,17,19,..., dimensions={0} | all-to-all | bytes 2097152 | tf_op jit(solution)/shard_map/all_to_all | solution.py:214
  81.2 0.0 copy-done.3
  81.2 1.2 link_update.1
  82.3 19.6 %all_to_all.16.own_ref = bf16[16,128,256]{2,1,0:T(8,128)(2,1)S(1)} all-to-all(bf16[16,128,256]{2,1,0:T(8,128)(2,1)S(1)} %get-tuple-element.16), channel_id=1, replica_groups={{0,2,4,6,8,10,12,14,16,18,20,22,24,26,28,30},{1,3,5,7,9,11,13,15,17,19,..., dimensions={0} | all-to-all | bytes 2097152 | tf_op jit(solution)/shard_map/all_to_all | solution.py:218
  101.9 1.9 %collective-permute-start.1 = (bf16[16,128,256]{2,1,0:T(8,128)(2,1)S(1)}, bf16[16,128,256]{2,1,0:T(8,128)(2,1)S(1)}, u32[]{:S(2)}, u32[]{:S(2)}) collective-permute-start(bf16[16,128,256]{2,1,0:T(8,128)(2,1)S(1)} %all_to_all.16.own_ref), channel_id=1, source_target_pairs={{0,1},{1,0},{2,3},{3,2},{4,5},{5,4},{6,7},{7,6},{8,9},{9,8},{10,11... | collective-permute-start | bytes 3145736 | tf_op jit(solution)/shard_map/ppermute | solution.py:219
  103.8 2.6 %collective-permute-done.1.other_ref = bf16[16,128,256]{2,1,0:T(8,128)(2,1)S(1)} collective-permute-done((bf16[16,128,256]{2,1,0:T(8,128)(2,1)S(1)}, bf16[16,128,256]{2,1,0:T(8,128)(2,1)S(1)}, u32[]{:S(2)}, u32[]{:S(2)}) %collective-permute-start.1) | collective-permute-done | bytes 1048608 | tf_op jit(solution)/shard_map/ppermute | solution.py:219
  106.5 1.8 %flow_products.1 = (bf16[8,128,256]{2,1,0:T(8,128)(2,1)S(1)}, bf16[8,128,256]{2,1,0:T(8,128)(2,1)S(1)}, bf16[4,128,256]{2,1,0:T(8,128)(2,1)S(1)}, bf16[4,128,256...) custom-call(s32[2]{0:T(128)S(1)} %pad_add_fusion.me_ref, s32[1,1,24]{2,1,0:T(1,128)S(1)} %copy-done.9, ...), custom_call_target="tpu_custom_call" | custom-call | tf_op jit(solution)/shard_map/flow_products/pallas_call | solution.py:83
  108.3 2.4 %collective-permute-start.2 = (bf16[4,128,256]{2,1,0:T(8,128)(2,1)S(1)}, bf16[4,128,256]{2,1,0:T(8,128)(2,1)S(1)}, u32[]{:S(2)}, u32[]{:S(2)}) collective-permute-start(bf16[4,128,256]{2,1,0:T(8,128)(2,1)S(1)} %get-tuple-element.19), channel_id=1, source_target_pairs={{0,32},{32,64},{64,96},{96,128},{128,160},{160,192},{192,224},{224... | collective-permute-start | bytes 786440 | tf_op jit(solution)/shard_map/ppermute | solution.py:223
  110.7 3.4 %collective-permute-start.3 = (bf16[4,128,256]{2,1,0:T(8,128)(2,1)S(1)}, bf16[4,128,256]{2,1,0:T(8,128)(2,1)S(1)}, u32[]{:S(2)}, u32[]{:S(2)}) collective-permute-start(bf16[4,128,256]{2,1,0:T(8,128)(2,1)S(1)} %get-tuple-element.21), channel_id=1, source_target_pairs={{0,480},{32,0},{64,32},{96,64},{128,96},{160,128},{192,160},{224,1... | collective-permute-start | bytes 786440 | tf_op jit(solution)/shard_map/ppermute | solution.py:224
  114.2 4.4 %collective-permute-done.2.low_ref = bf16[4,128,256]{2,1,0:T(8,128)(2,1)S(1)} collective-permute-done((bf16[4,128,256]{2,1,0:T(8,128)(2,1)S(1)}, bf16[4,128,256]{2,1,0:T(8,128)(2,1)S(1)}, u32[]{:S(2)}, u32[]{:S(2)}) %collective-permute-start.2) | collective-permute-done | bytes 262176 | tf_op jit(solution)/shard_map/ppermute | solution.py:223
  118.5 2.2 %collective-permute-done.3.high_ref = bf16[4,128,256]{2,1,0:T(8,128)(2,1)S(1)} collective-permute-done((bf16[4,128,256]{2,1,0:T(8,128)(2,1)S(1)}, bf16[4,128,256]{2,1,0:T(8,128)(2,1)S(1)}, u32[]{:S(2)}, u32[]{:S(2)}) %collective-permute-start.3) | collective-permute-done | bytes 262176 | tf_op jit(solution)/shard_map/ppermute | solution.py:224
  120.7 0.0 copy-start.13
  120.7 0.1 relay.1
  120.9 3.0 %collective-permute-start.4 = (bf16[8,128,256]{2,1,0:T(8,128)(2,1)S(1)}, bf16[8,128,256]{2,1,0:T(8,128)(2,1)S(1)}, u32[]{:S(2)}, u32[]{:S(2)}) collective-permute-start(bf16[8,128,256]{2,1,0:T(8,128)(2,1)S(1)} %get-tuple-element.22), channel_id=1, source_target_pairs={{0,32},{32,64},{64,96},{96,128},{128,160},{160,192},{192,224},{224... | collective-permute-start | bytes 1572872 | tf_op jit(solution)/shard_map/ppermute | solution.py:226
  123.9 2.9 %collective-permute-start.5 = (bf16[8,128,256]{2,1,0:T(8,128)(2,1)S(1)}, bf16[8,128,256]{2,1,0:T(8,128)(2,1)S(1)}, u32[]{:S(2)}, u32[]{:S(2)}) collective-permute-start(bf16[8,128,256]{2,1,0:T(8,128)(2,1)S(1)} %get-tuple-element.23), channel_id=1, source_target_pairs={{0,480},{32,0},{64,32},{96,64},{128,96},{160,128},{192,160},{224,1... | collective-permute-start | bytes 1572872 | tf_op jit(solution)/shard_map/ppermute | solution.py:227
  126.9 9.1 %collective-permute-done.4.b_ref = bf16[8,128,256]{2,1,0:T(8,128)(2,1)S(1)} collective-permute-done((bf16[8,128,256]{2,1,0:T(8,128)(2,1)S(1)}, bf16[8,128,256]{2,1,0:T(8,128)(2,1)S(1)}, u32[]{:S(2)}, u32[]{:S(2)}) %collective-permute-start.4) | collective-permute-done | bytes 524320 | tf_op jit(solution)/shard_map/ppermute | solution.py:226
  135.9 3.6 %collective-permute-done.5.c_ref = bf16[8,128,256]{2,1,0:T(8,128)(2,1)S(1)} collective-permute-done((bf16[8,128,256]{2,1,0:T(8,128)(2,1)S(1)}, bf16[8,128,256]{2,1,0:T(8,128)(2,1)S(1)}, u32[]{:S(2)}, u32[]{:S(2)}) %collective-permute-start.5) | collective-permute-done | bytes 524320 | tf_op jit(solution)/shard_map/ppermute | solution.py:227
  139.6 0.2 add_three.1
  139.8 38.1 %all_to_all.17.parts_ref = bf16[4,256,256]{2,1,0:T(8,128)(2,1)S(1)} all-to-all(bf16[4,256,256]{2,1,0:T(8,128)(2,1)S(1)} %bitcast.10), channel_id=1, replica_groups={{0,128,256,384},{32,160,288,416},{64,192,320,448},{96,224,352,480},{1,1..., dimensions={0} | all-to-all | bytes 1048576 | tf_op jit(solution)/shard_map/all_to_all | solution.py:230
  177.9 0.0 copy-done.5
  177.9 1.1 flow_update.1
  (22 shorter events, 0.0 us)
Async XLA Ops:
  49.3 1.1 copy-start
  49.3 1.1 copy-start.9
  49.3 1.1 copy-start.10
  49.3 1.1 copy-start.11
  52.0 4.6 %collective-permute-start = (bf16[16,128,256]{2,1,0:T(8,128)(2,1)S(1)}, bf16[16,128,256]{2,1,0:T(8,128)(2,1)S(1)}, u32[]{:S(2)}, u32[]{:S(2)}) collective-permute-start(bf16[16,128,256]{2,1,0:T(8,128)(2,1)S(1)} %get-tuple-element.14), channel_id=1, source_target_pairs={{0,1},{1,0},{2,3},{3,2},{4,5},{5,4},{6,7},{7,6},{8,9},{9,8},{10,11... | collective-permute-start | bytes 3145736 | tf_op jit(solution)/shard_map/ppermute | solution.py:213
  56.6 24.6 %copy-start.2 = (bf16[256,256]{1,0:T(8,128)(2,1)S(1)}, bf16[256,256]{1,0:T(8,128)(2,1)}, u32[]{:S(2)}) copy-start(bf16[256,256]{1,0:T(8,128)(2,1)} %agg_ref.2) | copy-start | bytes 393220
  56.6 24.6 %copy-start.3 = (bf16[256,256]{1,0:T(8,128)(2,1)S(1)}, bf16[256,256]{1,0:T(8,128)(2,1)}, u32[]{:S(2)}) copy-start(bf16[256,256]{1,0:T(8,128)(2,1)} %self_ref.2) | copy-start | bytes 393220
  56.6 24.6 %copy-start.4 = (bf16[256,256]{1,0:T(8,128)(2,1)S(1)}, bf16[256,256]{1,0:T(8,128)(2,1)}, u32[]{:S(2)}) copy-start(bf16[256,256]{1,0:T(8,128)(2,1)} %out_w_ref.2) | copy-start | bytes 393220
  56.6 24.6 %copy-start.8 = (bf16[128,256]{1,0:T(8,128)(2,1)S(1)}, bf16[128,256]{1,0:T(8,128)(2,1)}, u32[]{:S(2)}) copy-start(bf16[128,256]{1,0:T(8,128)(2,1)} %state_ref.2) | copy-start | bytes 196612
  56.6 24.6 %copy-start.12 = (f32[256]{0:T(256)S(1)}, f32[256]{0:T(256)}, u32[]{:S(2)}) copy-start(f32[256]{0:T(256)} %param.20) | copy-start | bytes 3076
  101.9 4.5 %collective-permute-start.1 = (bf16[16,128,256]{2,1,0:T(8,128)(2,1)S(1)}, bf16[16,128,256]{2,1,0:T(8,128)(2,1)S(1)}, u32[]{:S(2)}, u32[]{:S(2)}) collective-permute-start(bf16[16,128,256]{2,1,0:T(8,128)(2,1)S(1)} %all_to_all.16.own_ref), channel_id=1, source_target_pairs={{0,1},{1,0},{2,3},{3,2},{4,5},{5,4},{6,7},{7,6},{8,9},{9,8},{10,11... | collective-permute-start | bytes 3145736 | tf_op jit(solution)/shard_map/ppermute | solution.py:219
  108.3 10.2 %collective-permute-start.2 = (bf16[4,128,256]{2,1,0:T(8,128)(2,1)S(1)}, bf16[4,128,256]{2,1,0:T(8,128)(2,1)S(1)}, u32[]{:S(2)}, u32[]{:S(2)}) collective-permute-start(bf16[4,128,256]{2,1,0:T(8,128)(2,1)S(1)} %get-tuple-element.19), channel_id=1, source_target_pairs={{0,32},{32,64},{64,96},{96,128},{128,160},{160,192},{192,224},{224... | collective-permute-start | bytes 786440 | tf_op jit(solution)/shard_map/ppermute | solution.py:223
  110.7 10.0 %collective-permute-start.3 = (bf16[4,128,256]{2,1,0:T(8,128)(2,1)S(1)}, bf16[4,128,256]{2,1,0:T(8,128)(2,1)S(1)}, u32[]{:S(2)}, u32[]{:S(2)}) collective-permute-start(bf16[4,128,256]{2,1,0:T(8,128)(2,1)S(1)} %get-tuple-element.21), channel_id=1, source_target_pairs={{0,480},{32,0},{64,32},{96,64},{128,96},{160,128},{192,160},{224,1... | collective-permute-start | bytes 786440 | tf_op jit(solution)/shard_map/ppermute | solution.py:224
  120.7 57.1 %copy-start.1 = (bf16[256,256]{1,0:T(8,128)(2,1)S(1)}, bf16[256,256]{1,0:T(8,128)(2,1)}, u32[]{:S(2)}) copy-start(bf16[256,256]{1,0:T(8,128)(2,1)} %state_ref.3) | copy-start | bytes 393220
  120.7 57.1 %copy-start.5 = (bf16[256,256]{1,0:T(8,128)(2,1)S(1)}, bf16[256,256]{1,0:T(8,128)(2,1)}, u32[]{:S(2)}) copy-start(bf16[256,256]{1,0:T(8,128)(2,1)} %agg_ref.3) | copy-start | bytes 393220
  120.7 57.1 %copy-start.6 = (bf16[256,256]{1,0:T(8,128)(2,1)S(1)}, bf16[256,256]{1,0:T(8,128)(2,1)}, u32[]{:S(2)}) copy-start(bf16[256,256]{1,0:T(8,128)(2,1)} %self_ref.3) | copy-start | bytes 393220
  120.7 57.2 %copy-start.7 = (bf16[256,256]{1,0:T(8,128)(2,1)S(1)}, bf16[256,256]{1,0:T(8,128)(2,1)}, u32[]{:S(2)}) copy-start(bf16[256,256]{1,0:T(8,128)(2,1)} %out_w_ref.3) | copy-start | bytes 393220
  120.7 57.2 %copy-start.13 = (f32[256]{0:T(256)S(1)}, f32[256]{0:T(256)}, u32[]{:S(2)}) copy-start(f32[256]{0:T(256)} %param.24) | copy-start | bytes 3076
  120.9 15.1 %collective-permute-start.4 = (bf16[8,128,256]{2,1,0:T(8,128)(2,1)S(1)}, bf16[8,128,256]{2,1,0:T(8,128)(2,1)S(1)}, u32[]{:S(2)}, u32[]{:S(2)}) collective-permute-start(bf16[8,128,256]{2,1,0:T(8,128)(2,1)S(1)} %get-tuple-element.22), channel_id=1, source_target_pairs={{0,32},{32,64},{64,96},{96,128},{128,160},{160,192},{192,224},{224... | collective-permute-start | bytes 1572872 | tf_op jit(solution)/shard_map/ppermute | solution.py:226
  123.9 15.6 %collective-permute-start.5 = (bf16[8,128,256]{2,1,0:T(8,128)(2,1)S(1)}, bf16[8,128,256]{2,1,0:T(8,128)(2,1)S(1)}, u32[]{:S(2)}, u32[]{:S(2)}) collective-permute-start(bf16[8,128,256]{2,1,0:T(8,128)(2,1)S(1)} %get-tuple-element.23), channel_id=1, source_target_pairs={{0,480},{32,0},{64,32},{96,64},{128,96},{160,128},{192,160},{224,1... | collective-permute-start | bytes 1572872 | tf_op jit(solution)/shard_map/ppermute | solution.py:227

commit v3 on v2

--- a/solution.py
+++ b/solution.py
@@ -50,41 +50,45 @@
 
 
 def flow_products_kernel(
-    me_ref, flow_ref, link_ref, live_ref, coefs_ref, own_ref, other_ref,
-    same_ref, next_ref, far_up_ref, far_down_ref, prev_ref, acc_ref, pieces_ref,
+    me_ref, flow_ref, link_ref, live_ref, coefs_ref, own_ref, other_ref, *rest
 ):
+    *out_refs, acc_ref, pieces_ref = rest
     blocks = acc_ref.shape[0] - 1
-    quarter = blocks // 4
+    rows = blocks // 2
     half = own_ref.shape[0]
     pieces_ref[:half] = own_ref[...]
     pieces_ref[half:] = other_ref[...]
     acc_ref[...] = jnp.zeros_like(acc_ref)
     for slot in range(coefs_ref.shape[0]):
         block = flow_ref[0, 0, slot]
-        row = block // 2
-        place = ((row - me_ref[0] + 16) % 4) * quarter + (row // 4) * 2 + block % 2
+        ahead = (block // 2 - me_ref[0] + rows) % rows
+        upward = ahead < rows // 2
+        steps = jnp.where(upward, ahead, (rows - ahead) % (rows // 2))
+        odd = me_ref[0] % 2
+        second = jnp.where(steps == 0, jnp.where(ahead == 0, 0, 1), jnp.where(upward, odd, 1 - odd))
+        place = second * rows + steps * 2 + block % 2
         place = jnp.where(live_ref[0, 0, slot] == 1, place, blocks)
         piece = link_ref[0, 0, slot]
         piece = ((piece + me_ref[1]) % 2) * half + piece // 2
         acc_ref[place] += jnp.dot(
             coefs_ref[slot], pieces_ref[piece], preferred_element_type=F32
         )
-    low = quarter // 2
-    same_ref[...] = acc_ref[:quarter].astype(BF16)
-    next_ref[...] = acc_ref[quarter : 2 * quarter].astype(BF16)
-    far_up_ref[...] = acc_ref[2 * quarter : 2 * quarter + low].astype(BF16)
-    far_down_ref[...] = acc_ref[2 * quarter + low : 3 * quarter].astype(BF16)
-    prev_ref[...] = acc_ref[3 * quarter : 4 * quarter].astype(BF16)
+    start = 0
+    for out_ref in out_refs:
+        count = out_ref.shape[0]
+        out_ref[...] = acc_ref[start : start + count].astype(BF16)
+        start += count
 
 
 def flow_products(me, flow, link, live, coefs, own, other, blocks):
-    whole = jax.ShapeDtypeStruct((blocks // 4, BS, H), BF16)
-    part = jax.ShapeDtypeStruct((blocks // 8, BS, H), BF16)
-    return pl.pallas_call(
+    row = jax.ShapeDtypeStruct((2, BS, H), BF16)
+    half_row = jax.ShapeDtypeStruct((1, BS, H), BF16)
+    shapes = [row] * (blocks // 4) + [half_row] * 2 + [row] * (blocks // 4 - 1)
+    outs = pl.pallas_call(
         flow_products_kernel,
-        out_shape=[whole, whole, part, part, whole],
+        out_shape=shapes,
         in_specs=[SMEM, SMEM, SMEM, SMEM, VMEM, VMEM, VMEM],
-        out_specs=[VMEM] * 5,
+        out_specs=[VMEM] * len(shapes),
         scratch_shapes=[
             pltpu.VMEM((blocks + 1, BS, H), F32),
             pltpu.VMEM((2 * own.shape[0], BS, H), BF16),
@@ -92,6 +96,29 @@
         compiler_params=PARAMS,
         name="flow_products",
     )(me, flow, link, live, coefs, own, other)
+    side = blocks // 4
+    return outs[0], outs[1:side], outs[side], outs[side + 1], outs[side + 2 :]
+
+
+def add(a, b):
+    return (a.astype(F32) + b.astype(F32)).astype(BF16)
+
+
+def sum_over_rows(mine, for_a, half_a, half_b, for_b, rows):
+    swap_a = [(i, i ^ 1) for i in range(rows)]
+    swap_b = [(i, ((i - 1) ^ 1) + 1 if i % rows else rows - 1) for i in range(rows)]
+    swap_b = [(i, j % rows) for i, j in swap_b]
+    got_a = lax.ppermute(half_a, "row", swap_a)
+    got_b = lax.ppermute(half_b, "row", swap_b)
+    a = jnp.concatenate([for_a[-1][:1], add(for_a[-1][1:], got_b)], axis=0)
+    b = jnp.concatenate([add(for_b[-1][:1], got_a), for_b[-1][1:]], axis=0)
+    for step in range(len(for_a) - 2, -2, -1):
+        got_a = lax.ppermute(a, "row", swap_a)
+        got_b = lax.ppermute(b, "row", swap_b)
+        if step >= 0:
+            b = add(for_b[step], got_a)
+            a = add(for_a[step], got_b)
+    return jnp.stack([x.reshape(2 * BS, H) for x in (mine, got_a, got_b)])
 
 
 def add_kernel(a_ref, b_ref, out_ref):
@@ -107,42 +134,6 @@
         compiler_params=PARAMS,
         name="add_two",
     )(a, b)
-
-
-def relay_kernel(up_ref, low_ref, down_ref, high_ref, up_out_ref, down_out_ref):
-    half = low_ref.shape[0]
-    up_out_ref[:half] = (up_ref[:half].astype(F32) + low_ref[...].astype(F32)).astype(BF16)
-    up_out_ref[half:] = up_ref[half:]
-    down_out_ref[:half] = down_ref[:half]
-    down_out_ref[half:] = (down_ref[half:].astype(F32) + high_ref[...].astype(F32)).astype(BF16)
-
-
-def relay(up, low, down, high):
-    return pl.pallas_call(
-        relay_kernel,
-        out_shape=[jax.ShapeDtypeStruct(up.shape, BF16)] * 2,
-        in_specs=[VMEM] * 4,
-        out_specs=[VMEM] * 2,
-        compiler_params=PARAMS,
-        name="relay",
-    )(up, low, down, high)
-
-
-def add_three_kernel(a_ref, b_ref, c_ref, out_ref):
-    out_ref[...] = (
-        a_ref[...].astype(F32) + b_ref[...].astype(F32) + c_ref[...].astype(F32)
-    ).astype(BF16)
-
-
-def add_three(a, b, c):
-    return pl.pallas_call(
-        add_three_kernel,
-        out_shape=jax.ShapeDtypeStruct(a.shape, BF16),
-        in_specs=[VMEM] * 3,
-        out_specs=VMEM,
-        compiler_params=PARAMS,
-        name="add_three",
-    )(a, b, c)
 
 
 def update_kernel(parts_ref, state_ref, gain_ref, agg_ref, self_ref, out_w_ref, *out_refs):
@@ -201,9 +192,6 @@
     me = jnp.stack([lax.axis_index("row"), lax.axis_index("col") % 2]).astype(jnp.int32)
     sibling = [(i, i ^ 1) for i in range(cols)]
     same_core = [[2 * i + core for i in range(pairs)] for core in range(2)]
-    up = [(i, (i + 1) % rows) for i in range(rows)]
-    down = [(i, (i - 1) % rows) for i in range(rows)]
-    far = [[4 * a + b for a in range(rows // 4)] for b in range(4)]
 
     flow_group = gather_rows(flow_state)
     own, other = link_products(
@@ -217,19 +205,10 @@
     )
     own = lax.all_to_all(link_copies, "col", 0, 0, tiled=True, axis_index_groups=same_core)
     other = lax.ppermute(own, "col", sibling)
-    same, nxt, low, high, prev = flow_products(
+    mine, for_a, half_a, half_b, for_b = flow_products(
         me, tile_flow, tile_link, tile_live, coefs, own, other, flow_blocks
     )
-    low = lax.ppermute(low, "row", up)
-    high = lax.ppermute(high, "row", down)
-    nxt, prev = relay(nxt, low, prev, high)
-    nxt = lax.ppermute(nxt, "row", up)
-    prev = lax.ppermute(prev, "row", down)
-    same = add_three(same, nxt, prev)
-    per = flow_state.shape[0]
-    flow_parts = lax.all_to_all(
-        same.reshape(rows // 4, per, H), "row", 0, 0, tiled=True, axis_index_groups=far
-    )
+    flow_parts = sum_over_rows(mine, for_a, half_a, half_b, for_b, rows)
     (flow_next,) = update(
         flow_parts, flow_state, flow_gain, flow_agg_weight, flow_self_weight, flow_out_weight, 0
     )

time: 179 us -> 174 us (0.972)
  the two profiles are of different devices: /device:TPU:32 before, /device:TPU:2 now
where the time goes in v3:
time: 174 us; the launch traced here: 173 us
  blocking collectives  92.3 us (53%)
  starting transfers between devices  48.7 us (28%)
  waiting for transfers between devices  22.8 us (13%)
  Pallas kernels  5.92 us (3%)
  other arithmetic  2.11 us (1%)
    all_gather x1, blocking collectives, gather_rows(): got = lax.all_gather(sent, 'row', axis=0, tiled=True)  49.3 us
    ppermute x7, starting transfers between devices, sum_over_rows(): got_b = lax.ppermute(b, 'row', swap_b)  24.1 us
    all_to_all x1, blocking collectives, on_device(): lax.all_to_all(own, 'col', 0, 0, tiled=True, axis_index_groups=same_core)  23.4 us
    all_to_all x1, blocking collectives, on_device(): lax.all_to_all(link_copies, 'col', 0, 0, tiled=True, axis_index_groups=sa...  19.6 us
    ppermute x7, starting transfers between devices, sum_over_rows(): got_a = lax.ppermute(a, 'row', swap_a)  15 us
    ppermute x7, waiting for transfers between devices, sum_over_rows(): got_b = lax.ppermute(b, 'row', swap_b)  10 us
    ppermute x7, waiting for transfers between devices, sum_over_rows(): got_a = lax.ppermute(a, 'row', swap_a)  7.04 us
    ppermute x1, starting transfers between devices, sum_over_rows(): got_b = lax.ppermute(half_b, 'row', swap_b)  3.61 us
  transfers between devices with their start and end apart: 18, of which 16 were waited for; matrix products, arithmetic and copies ran while one was open for 0% of the time, Pallas kernels for 0%

profile of v3, /device:TPU:2, one launch (start us, length us, event | category | flops | bytes accessed | tf_op | source)
XLA Modules:
  0.0 173.4 jit_solution(1447663671104164911)
XLA Ops:
  1.6 49.3 %all-gather.1 = f16[4096,256]{1,0:T(8,128)(2,1)S(1)} all-gather(f16[256,256]{1,0:T(8,128)(2,1)S(1)} %multiply_convert_fusion.1), channel_id=1, replica_groups=mesh['row'=16,'col'=32] {'row'}, dimensions={0}, use_global_device_ids=true | all-gather | bytes 2228224 | tf_op jit(solution)/shard_map/all_gather | solution.py:220
  52.1 1.6 link_products.1
  53.7 1.9 %collective-permute-start = (bf16[16,128,256]{2,1,0:T(8,128)(2,1)S(1)}, bf16[16,128,256]{2,1,0:T(8,128)(2,1)S(1)}, u32[]{:S(2)}, u32[]{:S(2)}) collective-permute-start(bf16[16,128,256]{2,1,0:T(8,128)(2,1)S(1)} %get-tuple-element.24), channel_id=1, source_target_pairs={{0,1},{1,0},{2,3},{3,2},{4,5},{5,4},{6,7},{7,6},{8,9},{9,8},{10,11... | collective-permute-start | bytes 3145736 | tf_op jit(solution)/shard_map/ppermute | solution.py:201
  55.6 2.6 %collective-permute-done.b_ref = bf16[16,128,256]{2,1,0:T(8,128)(2,1)S(1)} collective-permute-done((bf16[16,128,256]{2,1,0:T(8,128)(2,1)S(1)}, bf16[16,128,256]{2,1,0:T(8,128)(2,1)S(1)}, u32[]{:S(2)}, u32[]{:S(2)}) %collective-permute-start) | collective-permute-done | bytes 1048608 | tf_op jit(solution)/shard_map/ppermute | solution.py:201
  58.5 23.4 %all_to_all.10.parts_ref = bf16[16,128,256]{2,1,0:T(8,128)(2,1)S(1)} all-to-all(bf16[16,128,256]{2,1,0:T(8,128)(2,1)S(1)} %add_two.1), channel_id=1, replica_groups={{0,2,4,6,8,10,12,14,16,18,20,22,24,26,28,30},{1,3,5,7,9,11,13,15,17,19,..., dimensions={0} | all-to-all | bytes 2097152 | tf_op jit(solution)/shard_map/all_to_all | solution.py:202
  81.9 1.2 link_update.1
  83.0 19.6 %all_to_all.11.own_ref = bf16[16,128,256]{2,1,0:T(8,128)(2,1)S(1)} all-to-all(bf16[16,128,256]{2,1,0:T(8,128)(2,1)S(1)} %get-tuple-element.26), channel_id=1, replica_groups={{0,2,4,6,8,10,12,14,16,18,20,22,24,26,28,30},{1,3,5,7,9,11,13,15,17,19,..., dimensions={0} | all-to-all | bytes 2097152 | tf_op jit(solution)/shard_map/all_to_all | solution.py:206
  102.7 1.9 %collective-permute-start.1 = (bf16[16,128,256]{2,1,0:T(8,128)(2,1)S(1)}, bf16[16,128,256]{2,1,0:T(8,128)(2,1)S(1)}, u32[]{:S(2)}, u32[]{:S(2)}) collective-permute-start(bf16[16,128,256]{2,1,0:T(8,128)(2,1)S(1)} %all_to_all.11.own_ref), channel_id=1, source_target_pairs={{0,1},{1,0},{2,3},{3,2},{4,5},{5,4},{6,7},{7,6},{8,9},{9,8},{10,11... | collective-permute-start | bytes 3145736 | tf_op jit(solution)/shard_map/ppermute | solution.py:207
  104.6 2.6 %collective-permute-done.1.other_ref = bf16[16,128,256]{2,1,0:T(8,128)(2,1)S(1)} collective-permute-done((bf16[16,128,256]{2,1,0:T(8,128)(2,1)S(1)}, bf16[16,128,256]{2,1,0:T(8,128)(2,1)S(1)}, u32[]{:S(2)}, u32[]{:S(2)}) %collective-permute-start.1) | collective-permute-done | bytes 1048608 | tf_op jit(solution)/shard_map/ppermute | solution.py:207
  107.2 1.9 %flow_products.1 = (bf16[2,128,256]{2,1,0:T(8,128)(2,1)S(1)}, bf16[2,128,256]{2,1,0:T(8,128)(2,1)S(1)}, bf16[2,128,256]{2,1,0:T(8,128)(2,1)S(1)}, bf16[2,128,256...) custom-call(s32[2]{0:T(128)S(1)} %pad_add_fusion.me_ref, ...), custom_call_target="tpu_custom_call" | custom-call | tf_op jit(solution)/shard_map/flow_products/pallas_call | solution.py:87
  109.1 2.2 %collective-permute-start.10 = (bf16[1,128,256]{2,1,0:T(8,128)(2,1)S(1)}, bf16[1,128,256]{2,1,0:T(8,128)(2,1)S(1)}, u32[]{:S(2)}, u32[]{:S(2)}) collective-permute-start(bf16[1,128,256]{2,1,0:T(8,128)(2,1)S(1)} %get-tuple-element.43), channel_id=1, source_target_pairs={{0,32},{32,0},{64,96},{96,64},{128,160},{160,128},{192,224},{224,1... | collective-permute-start | bytes 196616 | tf_op jit(solution)/shard_map/ppermute | solution.py:111
  111.3 3.6 %collective-permute-start.2 = (bf16[1,128,256]{2,1,0:T(8,128)(2,1)S(1)}, bf16[1,128,256]{2,1,0:T(8,128)(2,1)S(1)}, u32[]{:S(2)}, u32[]{:S(2)}) collective-permute-start(bf16[1,128,256]{2,1,0:T(8,128)(2,1)S(1)} %get-tuple-element.35), channel_id=1, source_target_pairs={{0,480},{32,64},{64,32},{96,128},{128,96},{160,192},{192,160},{224... | collective-permute-start | bytes 196616 | tf_op jit(solution)/shard_map/ppermute | solution.py:112
  115.3 3.2 %collective-permute-start.11 = (bf16[2,128,256]{2,1,0:T(8,128)(2,1)S(1)}, bf16[2,128,256]{2,1,0:T(8,128)(2,1)S(1)}, u32[]{:S(2)}, u32[]{:S(2)}) collective-permute-start(bf16[2,128,256]{2,1,0:T(8,128)(2,1)S(1)} %pad_maximum_fusion.2), channel_id=1, source_target_pairs={{0,480},{32,64},{64,32},{96,128},{128,96},{160,192},{192,160},{224... | collective-permute-start | bytes 393224 | tf_op jit(solution)/shard_map/ppermute | solution.py:117
  118.7 2.4 %collective-permute-start.3 = (bf16[2,128,256]{2,1,0:T(8,128)(2,1)S(1)}, bf16[2,128,256]{2,1,0:T(8,128)(2,1)S(1)}, u32[]{:S(2)}, u32[]{:S(2)}) collective-permute-start(bf16[2,128,256]{2,1,0:T(8,128)(2,1)S(1)} %pad_maximum_fusion.1), channel_id=1, source_target_pairs={{0,32},{32,0},{64,96},{96,64},{128,160},{160,128},{192,224},{224,1... | collective-permute-start | bytes 393224 | tf_op jit(solution)/shard_map/ppermute | solution.py:116
  121.2 2.2 %collective-permute-done.11 = bf16[2,128,256]{2,1,0:T(8,128)(2,1)S(1)} collective-permute-done((bf16[2,128,256]{2,1,0:T(8,128)(2,1)S(1)}, bf16[2,128,256]{2,1,0:T(8,128)(2,1)S(1)}, u32[]{:S(2)}, u32[]{:S(2)}) %collective-permute-start.11) | collective-permute-done | bytes 131104 | tf_op jit(solution)/shard_map/ppermute | solution.py:117
  123.4 1.9 %collective-permute-start.12 = (bf16[2,128,256]{2,1,0:T(8,128)(2,1)S(1)}, bf16[2,128,256]{2,1,0:T(8,128)(2,1)S(1)}, u32[]{:S(2)}, u32[]{:S(2)}) collective-permute-start(bf16[2,128,256]{2,1,0:T(8,128)(2,1)S(1)} %add_convert_fusion.5), channel_id=1, source_target_pairs={{0,32},{32,0},{64,96},{96,64},{128,160},{160,128},{192,224},{224,1... | collective-permute-start | bytes 393224 | tf_op jit(solution)/shard_map/ppermute | solution.py:116
  125.6 3.7 %collective-permute-start.4 = (bf16[2,128,256]{2,1,0:T(8,128)(2,1)S(1)}, bf16[2,128,256]{2,1,0:T(8,128)(2,1)S(1)}, u32[]{:S(2)}, u32[]{:S(2)}) collective-permute-start(bf16[2,128,256]{2,1,0:T(8,128)(2,1)S(1)} %add_convert_fusion.11), channel_id=1, source_target_pairs={{0,480},{32,64},{64,32},{96,128},{128,96},{160,192},{192,160},{224... | collective-permute-start | bytes 393224 | tf_op jit(solution)/shard_map/ppermute | solution.py:117
  130.3 3.2 %collective-permute-start.13 = (bf16[2,128,256]{2,1,0:T(8,128)(2,1)S(1)}, bf16[2,128,256]{2,1,0:T(8,128)(2,1)S(1)}, u32[]{:S(2)}, u32[]{:S(2)}) collective-permute-start(bf16[2,128,256]{2,1,0:T(8,128)(2,1)S(1)} %add_convert_fusion.4), channel_id=1, source_target_pairs={{0,480},{32,64},{64,32},{96,128},{128,96},{160,192},{192,160},{224... | collective-permute-start | bytes 393224 | tf_op jit(solution)/shard_map/ppermute | solution.py:117
  134.5 2.4 %collective-permute-start.5 = (bf16[2,128,256]{2,1,0:T(8,128)(2,1)S(1)}, bf16[2,128,256]{2,1,0:T(8,128)(2,1)S(1)}, u32[]{:S(2)}, u32[]{:S(2)}) collective-permute-start(bf16[2,128,256]{2,1,0:T(8,128)(2,1)S(1)} %add_convert_fusion.10), channel_id=1, source_target_pairs={{0,32},{32,0},{64,96},{96,64},{128,160},{160,128},{192,224},{224,1... | collective-permute-start | bytes 393224 | tf_op jit(solution)/shard_map/ppermute | solution.py:116
  137.0 1.4 collective-permute-done.13
  138.4 2.2 %collective-permute-start.14 = (bf16[2,128,256]{2,1,0:T(8,128)(2,1)S(1)}, bf16[2,128,256]{2,1,0:T(8,128)(2,1)S(1)}, u32[]{:S(2)}, u32[]{:S(2)}) collective-permute-start(bf16[2,128,256]{2,1,0:T(8,128)(2,1)S(1)} %add_convert_fusion.3), channel_id=1, source_target_pairs={{0,32},{32,0},{64,96},{96,64},{128,160},{160,128},{192,224},{224,1... | collective-permute-start | bytes 393224 | tf_op jit(solution)/shard_map/ppermute | solution.py:116
  140.6 1.7 collective-permute-done.5
  142.3 3.7 %collective-permute-start.6 = (bf16[2,128,256]{2,1,0:T(8,128)(2,1)S(1)}, bf16[2,128,256]{2,1,0:T(8,128)(2,1)S(1)}, u32[]{:S(2)}, u32[]{:S(2)}) collective-permute-start(bf16[2,128,256]{2,1,0:T(8,128)(2,1)S(1)} %add_convert_fusion.9), channel_id=1, source_target_pairs={{0,480},{32,64},{64,32},{96,128},{128,96},{160,192},{192,160},{224... | collective-permute-start | bytes 393224 | tf_op jit(solution)/shard_map/ppermute | solution.py:117
  146.0 3.4 %collective-permute-start.15 = (bf16[2,128,256]{2,1,0:T(8,128)(2,1)S(1)}, bf16[2,128,256]{2,1,0:T(8,128)(2,1)S(1)}, u32[]{:S(2)}, u32[]{:S(2)}) collective-permute-start(bf16[2,128,256]{2,1,0:T(8,128)(2,1)S(1)} %add_convert_fusion.2), channel_id=1, source_target_pairs={{0,480},{32,64},{64,32},{96,128},{128,96},{160,192},{192,160},{224... | collective-permute-start | bytes 393224 | tf_op jit(solution)/shard_map/ppermute | solution.py:117
  150.4 1.9 %collective-permute-start.7 = (bf16[2,128,256]{2,1,0:T(8,128)(2,1)S(1)}, bf16[2,128,256]{2,1,0:T(8,128)(2,1)S(1)}, u32[]{:S(2)}, u32[]{:S(2)}) collective-permute-start(bf16[2,128,256]{2,1,0:T(8,128)(2,1)S(1)} %add_convert_fusion.8), channel_id=1, source_target_pairs={{0,32},{32,0},{64,96},{96,64},{128,160},{160,128},{192,224},{224,1... | collective-permute-start | bytes 393224 | tf_op jit(solution)/shard_map/ppermute | solution.py:116
  152.3 1.8 %collective-permute-done.15 = bf16[2,128,256]{2,1,0:T(8,128)(2,1)S(1)} collective-permute-done((bf16[2,128,256]{2,1,0:T(8,128)(2,1)S(1)}, bf16[2,128,256]{2,1,0:T(8,128)(2,1)S(1)}, u32[]{:S(2)}, u32[]{:S(2)}) %collective-permute-start.15) | collective-permute-done | bytes 131104 | tf_op jit(solution)/shard_map/ppermute | solution.py:117
  154.1 2.2 %collective-permute-start.16 = (bf16[2,128,256]{2,1,0:T(8,128)(2,1)S(1)}, bf16[2,128,256]{2,1,0:T(8,128)(2,1)S(1)}, u32[]{:S(2)}, u32[]{:S(2)}) collective-permute-start(bf16[2,128,256]{2,1,0:T(8,128)(2,1)S(1)} %add_convert_fusion.1), channel_id=1, source_target_pairs={{0,32},{32,0},{64,96},{96,64},{128,160},{160,128},{192,224},{224,1... | collective-permute-start | bytes 393224 | tf_op jit(solution)/shard_map/ppermute | solution.py:116
  157.3 3.7 %collective-permute-start.8 = (bf16[2,128,256]{2,1,0:T(8,128)(2,1)S(1)}, bf16[2,128,256]{2,1,0:T(8,128)(2,1)S(1)}, u32[]{:S(2)}, u32[]{:S(2)}) collective-permute-start(bf16[2,128,256]{2,1,0:T(8,128)(2,1)S(1)} %add_convert_fusion.7), channel_id=1, source_target_pairs={{0,480},{32,64},{64,32},{96,128},{128,96},{160,192},{192,160},{224... | collective-permute-start | bytes 393224 | tf_op jit(solution)/shard_map/ppermute | solution.py:117
  161.0 3.4 %collective-permute-start.17 = (bf16[2,128,256]{2,1,0:T(8,128)(2,1)S(1)}, bf16[2,128,256]{2,1,0:T(8,128)(2,1)S(1)}, u32[]{:S(2)}, u32[]{:S(2)}) collective-permute-start(bf16[2,128,256]{2,1,0:T(8,128)(2,1)S(1)} %add_convert_fusion), channel_id=1, source_target_pairs={{0,480},{32,64},{64,32},{96,128},{128,96},{160,192},{192,160},{224... | collective-permute-start | bytes 393224 | tf_op jit(solution)/shard_map/ppermute | solution.py:117
  165.4 1.9 %collective-permute-start.9 = (bf16[2,128,256]{2,1,0:T(8,128)(2,1)S(1)}, bf16[2,128,256]{2,1,0:T(8,128)(2,1)S(1)}, u32[]{:S(2)}, u32[]{:S(2)}) collective-permute-start(bf16[2,128,256]{2,1,0:T(8,128)(2,1)S(1)} %add_convert_fusion.6), channel_id=1, source_target_pairs={{0,32},{32,0},{64,96},{96,64},{128,160},{160,128},{192,224},{224,1... | collective-permute-start | bytes 393224 | tf_op jit(solution)/shard_map/ppermute | solution.py:116
  167.3 1.8 %collective-permute-done.17 = bf16[2,128,256]{2,1,0:T(8,128)(2,1)S(1)} collective-permute-done((bf16[2,128,256]{2,1,0:T(8,128)(2,1)S(1)}, bf16[2,128,256]{2,1,0:T(8,128)(2,1)S(1)}, u32[]{:S(2)}, u32[]{:S(2)}) %collective-permute-start.17) | collective-permute-done | bytes 131104 | tf_op jit(solution)/shard_map/ppermute | solution.py:117
  169.1 3.2 %collective-permute-done.9 = bf16[2,128,256]{2,1,0:T(8,128)(2,1)S(1)} collective-permute-done((bf16[2,128,256]{2,1,0:T(8,128)(2,1)S(1)}, bf16[2,128,256]{2,1,0:T(8,128)(2,1)S(1)}, u32[]{:S(2)}, u32[]{:S(2)}) %collective-permute-start.9) | collective-permute-done | bytes 131104 | tf_op jit(solution)/shard_map/ppermute | solution.py:116
  (62 shorter events, 9.6 us)
Async XLA Ops:
  50.9 1.1 copy-start
  50.9 1.1 copy-start.9
  50.9 1.1 copy-start.10
  50.9 1.1 copy-start.11
  53.7 4.6 %collective-permute-start = (bf16[16,128,256]{2,1,0:T(8,128)(2,1)S(1)}, bf16[16,128,256]{2,1,0:T(8,128)(2,1)S(1)}, u32[]{:S(2)}, u32[]{:S(2)}) collective-permute-start(bf16[16,128,256]{2,1,0:T(8,128)(2,1)S(1)} %get-tuple-element.24), channel_id=1, source_target_pairs={{0,1},{1,0},{2,3},{3,2},{4,5},{5,4},{6,7},{7,6},{8,9},{9,8},{10,11... | collective-permute-start | bytes 3145736 | tf_op jit(solution)/shard_map/ppermute | solution.py:201
  58.2 23.6 %copy-start.2 = (bf16[256,256]{1,0:T(8,128)(2,1)S(1)}, bf16[256,256]{1,0:T(8,128)(2,1)}, u32[]{:S(2)}) copy-start(bf16[256,256]{1,0:T(8,128)(2,1)} %agg_ref.2) | copy-start | bytes 393220
  58.2 23.6 %copy-start.3 = (bf16[256,256]{1,0:T(8,128)(2,1)S(1)}, bf16[256,256]{1,0:T(8,128)(2,1)}, u32[]{:S(2)}) copy-start(bf16[256,256]{1,0:T(8,128)(2,1)} %self_ref.2) | copy-start | bytes 393220
  58.2 23.6 %copy-start.4 = (bf16[256,256]{1,0:T(8,128)(2,1)S(1)}, bf16[256,256]{1,0:T(8,128)(2,1)}, u32[]{:S(2)}) copy-start(bf16[256,256]{1,0:T(8,128)(2,1)} %out_w_ref.2) | copy-start | bytes 393220
  58.2 23.6 %copy-start.8 = (bf16[128,256]{1,0:T(8,128)(2,1)S(1)}, bf16[128,256]{1,0:T(8,128)(2,1)}, u32[]{:S(2)}) copy-start(bf16[128,256]{1,0:T(8,128)(2,1)} %state_ref.2) | copy-start | bytes 196612
  58.2 23.6 %copy-start.12 = (f32[256]{0:T(256)S(1)}, f32[256]{0:T(256)}, u32[]{:S(2)}) copy-start(f32[256]{0:T(256)} %param.20) | copy-start | bytes 3076
  102.7 4.5 %collective-permute-start.1 = (bf16[16,128,256]{2,1,0:T(8,128)(2,1)S(1)}, bf16[16,128,256]{2,1,0:T(8,128)(2,1)S(1)}, u32[]{:S(2)}, u32[]{:S(2)}) collective-permute-start(bf16[16,128,256]{2,1,0:T(8,128)(2,1)S(1)} %all_to_all.11.own_ref), channel_id=1, source_target_pairs={{0,1},{1,0},{2,3},{3,2},{4,5},{5,4},{6,7},{7,6},{8,9},{9,8},{10,11... | collective-permute-start | bytes 3145736 | tf_op jit(solution)/shard_map/ppermute | solution.py:207
  109.1 6.2 %collective-permute-start.10 = (bf16[1,128,256]{2,1,0:T(8,128)(2,1)S(1)}, bf16[1,128,256]{2,1,0:T(8,128)(2,1)S(1)}, u32[]{:S(2)}, u32[]{:S(2)}) collective-permute-start(bf16[1,128,256]{2,1,0:T(8,128)(2,1)S(1)} %get-tuple-element.43), channel_id=1, source_target_pairs={{0,32},{32,0},{64,96},{96,64},{128,160},{160,128},{192,224},{224,1... | collective-permute-start | bytes 196616 | tf_op jit(solution)/shard_map/ppermute | solution.py:111
  111.3 7.4 %collective-permute-start.2 = (bf16[1,128,256]{2,1,0:T(8,128)(2,1)S(1)}, bf16[1,128,256]{2,1,0:T(8,128)(2,1)S(1)}, u32[]{:S(2)}, u32[]{:S(2)}) collective-permute-start(bf16[1,128,256]{2,1,0:T(8,128)(2,1)S(1)} %get-tuple-element.35), channel_id=1, source_target_pairs={{0,480},{32,64},{64,32},{96,128},{128,96},{160,192},{192,160},{224... | collective-permute-start | bytes 196616 | tf_op jit(solution)/shard_map/ppermute | solution.py:112
  115.3 8.1 %collective-permute-start.11 = (bf16[2,128,256]{2,1,0:T(8,128)(2,1)S(1)}, bf16[2,128,256]{2,1,0:T(8,128)(2,1)S(1)}, u32[]{:S(2)}, u32[]{:S(2)}) collective-permute-start(bf16[2,128,256]{2,1,0:T(8,128)(2,1)S(1)} %pad_maximum_fusion.2), channel_id=1, source_target_pairs={{0,480},{32,64},{64,32},{96,128},{128,96},{160,192},{192,160},{224... | collective-permute-start | bytes 393224 | tf_op jit(solution)/shard_map/ppermute | solution.py:117
  118.7 6.9 %collective-permute-start.3 = (bf16[2,128,256]{2,1,0:T(8,128)(2,1)S(1)}, bf16[2,128,256]{2,1,0:T(8,128)(2,1)S(1)}, u32[]{:S(2)}, u32[]{:S(2)}) collective-permute-start(bf16[2,128,256]{2,1,0:T(8,128)(2,1)S(1)} %pad_maximum_fusion.1), channel_id=1, source_target_pairs={{0,32},{32,0},{64,96},{96,64},{128,160},{160,128},{192,224},{224,1... | collective-permute-start | bytes 393224 | tf_op jit(solution)/shard_map/ppermute | solution.py:116
  123.4 6.9 %collective-permute-start.12 = (bf16[2,128,256]{2,1,0:T(8,128)(2,1)S(1)}, bf16[2,128,256]{2,1,0:T(8,128)(2,1)S(1)}, u32[]{:S(2)}, u32[]{:S(2)}) collective-permute-start(bf16[2,128,256]{2,1,0:T(8,128)(2,1)S(1)} %add_convert_fusion.5), channel_id=1, source_target_pairs={{0,32},{32,0},{64,96},{96,64},{128,160},{160,128},{192,224},{224,1... | collective-permute-start | bytes 393224 | tf_op jit(solution)/shard_map/ppermute | solution.py:116
  125.6 8.8 %collective-permute-start.4 = (bf16[2,128,256]{2,1,0:T(8,128)(2,1)S(1)}, bf16[2,128,256]{2,1,0:T(8,128)(2,1)S(1)}, u32[]{:S(2)}, u32[]{:S(2)}) collective-permute-start(bf16[2,128,256]{2,1,0:T(8,128)(2,1)S(1)} %add_convert_fusion.11), channel_id=1, source_target_pairs={{0,480},{32,64},{64,32},{96,128},{128,96},{160,192},{192,160},{224... | collective-permute-start | bytes 393224 | tf_op jit(solution)/shard_map/ppermute | solution.py:117
  130.3 8.1 %collective-permute-start.13 = (bf16[2,128,256]{2,1,0:T(8,128)(2,1)S(1)}, bf16[2,128,256]{2,1,0:T(8,128)(2,1)S(1)}, u32[]{:S(2)}, u32[]{:S(2)}) collective-permute-start(bf16[2,128,256]{2,1,0:T(8,128)(2,1)S(1)} %add_convert_fusion.4), channel_id=1, source_target_pairs={{0,480},{32,64},{64,32},{96,128},{128,96},{160,192},{192,160},{224... | collective-permute-start | bytes 393224 | tf_op jit(solution)/shard_map/ppermute | solution.py:117
  134.5 37.9 %copy-start.1 = (bf16[256,256]{1,0:T(8,128)(2,1)S(1)}, bf16[256,256]{1,0:T(8,128)(2,1)}, u32[]{:S(2)}) copy-start(bf16[256,256]{1,0:T(8,128)(2,1)} %state_ref.3) | copy-start | bytes 393220
  134.5 37.9 %copy-start.5 = (bf16[256,256]{1,0:T(8,128)(2,1)S(1)}, bf16[256,256]{1,0:T(8,128)(2,1)}, u32[]{:S(2)}) copy-start(bf16[256,256]{1,0:T(8,128)(2,1)} %agg_ref.3) | copy-start | bytes 393220
  134.5 37.9 %copy-start.6 = (bf16[256,256]{1,0:T(8,128)(2,1)S(1)}, bf16[256,256]{1,0:T(8,128)(2,1)}, u32[]{:S(2)}) copy-start(bf16[256,256]{1,0:T(8,128)(2,1)} %self_ref.3) | copy-start | bytes 393220
  134.5 37.9 %copy-start.7 = (bf16[256,256]{1,0:T(8,128)(2,1)S(1)}, bf16[256,256]{1,0:T(8,128)(2,1)}, u32[]{:S(2)}) copy-start(bf16[256,256]{1,0:T(8,128)(2,1)} %out_w_ref.3) | copy-start | bytes 393220
  134.5 37.9 %copy-start.13 = (f32[256]{0:T(256)S(1)}, f32[256]{0:T(256)}, u32[]{:S(2)}) copy-start(f32[256]{0:T(256)} %param.24) | copy-start | bytes 3076
  134.5 7.7 %collective-permute-start.5 = (bf16[2,128,256]{2,1,0:T(8,128)(2,1)S(1)}, bf16[2,128,256]{2,1,0:T(8,128)(2,1)S(1)}, u32[]{:S(2)}, u32[]{:S(2)}) collective-permute-start(bf16[2,128,256]{2,1,0:T(8,128)(2,1)S(1)} %add_convert_fusion.10), channel_id=1, source_target_pairs={{0,32},{32,0},{64,96},{96,64},{128,160},{160,128},{192,224},{224,1... | collective-permute-start | bytes 393224 | tf_op jit(solution)/shard_map/ppermute | solution.py:116
  138.4 7.6 %collective-permute-start.14 = (bf16[2,128,256]{2,1,0:T(8,128)(2,1)S(1)}, bf16[2,128,256]{2,1,0:T(8,128)(2,1)S(1)}, u32[]{:S(2)}, u32[]{:S(2)}) collective-permute-start(bf16[2,128,256]{2,1,0:T(8,128)(2,1)S(1)} %add_convert_fusion.3), channel_id=1, source_target_pairs={{0,32},{32,0},{64,96},{96,64},{128,160},{160,128},{192,224},{224,1... | collective-permute-start | bytes 393224 | tf_op jit(solution)/shard_map/ppermute | solution.py:116
  142.3 8.1 %collective-permute-start.6 = (bf16[2,128,256]{2,1,0:T(8,128)(2,1)S(1)}, bf16[2,128,256]{2,1,0:T(8,128)(2,1)S(1)}, u32[]{:S(2)}, u32[]{:S(2)}) collective-permute-start(bf16[2,128,256]{2,1,0:T(8,128)(2,1)S(1)} %add_convert_fusion.9), channel_id=1, source_target_pairs={{0,480},{32,64},{64,32},{96,128},{128,96},{160,192},{192,160},{224... | collective-permute-start | bytes 393224 | tf_op jit(solution)/shard_map/ppermute | solution.py:117
  146.0 8.1 %collective-permute-start.15 = (bf16[2,128,256]{2,1,0:T(8,128)(2,1)S(1)}, bf16[2,128,256]{2,1,0:T(8,128)(2,1)S(1)}, u32[]{:S(2)}, u32[]{:S(2)}) collective-permute-start(bf16[2,128,256]{2,1,0:T(8,128)(2,1)S(1)} %add_convert_fusion.2), channel_id=1, source_target_pairs={{0,480},{32,64},{64,32},{96,128},{128,96},{160,192},{192,160},{224... | collective-permute-start | bytes 393224 | tf_op jit(solution)/shard_map/ppermute | solution.py:117
  150.4 6.9 %collective-permute-start.7 = (bf16[2,128,256]{2,1,0:T(8,128)(2,1)S(1)}, bf16[2,128,256]{2,1,0:T(8,128)(2,1)S(1)}, u32[]{:S(2)}, u32[]{:S(2)}) collective-permute-start(bf16[2,128,256]{2,1,0:T(8,128)(2,1)S(1)} %add_convert_fusion.8), channel_id=1, source_target_pairs={{0,32},{32,0},{64,96},{96,64},{128,160},{160,128},{192,224},{224,1... | collective-permute-start | bytes 393224 | tf_op jit(solution)/shard_map/ppermute | solution.py:116
  154.1 6.9 %collective-permute-start.16 = (bf16[2,128,256]{2,1,0:T(8,128)(2,1)S(1)}, bf16[2,128,256]{2,1,0:T(8,128)(2,1)S(1)}, u32[]{:S(2)}, u32[]{:S(2)}) collective-permute-start(bf16[2,128,256]{2,1,0:T(8,128)(2,1)S(1)} %add_convert_fusion.1), channel_id=1, source_target_pairs={{0,32},{32,0},{64,96},{96,64},{128,160},{160,128},{192,224},{224,1... | collective-permute-start | bytes 393224 | tf_op jit(solution)/shard_map/ppermute | solution.py:116
  157.3 8.1 %collective-permute-start.8 = (bf16[2,128,256]{2,1,0:T(8,128)(2,1)S(1)}, bf16[2,128,256]{2,1,0:T(8,128)(2,1)S(1)}, u32[]{:S(2)}, u32[]{:S(2)}) collective-permute-start(bf16[2,128,256]{2,1,0:T(8,128)(2,1)S(1)} %add_convert_fusion.7), channel_id=1, source_target_pairs={{0,480},{32,64},{64,32},{96,128},{128,96},{160,192},{192,160},{224... | collective-permute-start | bytes 393224 | tf_op jit(solution)/shard_map/ppermute | solution.py:117
  161.0 8.1 %collective-permute-start.17 = (bf16[2,128,256]{2,1,0:T(8,128)(2,1)S(1)}, bf16[2,128,256]{2,1,0:T(8,128)(2,1)S(1)}, u32[]{:S(2)}, u32[]{:S(2)}) collective-permute-start(bf16[2,128,256]{2,1,0:T(8,128)(2,1)S(1)} %add_convert_fusion), channel_id=1, source_target_pairs={{0,480},{32,64},{64,32},{96,128},{128,96},{160,192},{192,160},{224... | collective-permute-start | bytes 393224 | tf_op jit(solution)/shard_map/ppermute | solution.py:117
  165.4 6.9 %collective-permute-start.9 = (bf16[2,128,256]{2,1,0:T(8,128)(2,1)S(1)}, bf16[2,128,256]{2,1,0:T(8,128)(2,1)S(1)}, u32[]{:S(2)}, u32[]{:S(2)}) collective-permute-start(bf16[2,128,256]{2,1,0:T(8,128)(2,1)S(1)} %add_convert_fusion.6), channel_id=1, source_target_pairs={{0,32},{32,0},{64,96},{96,64},{128,160},{160,128},{192,224},{224,1... | collective-permute-start | bytes 393224 | tf_op jit(solution)/shard_map/ppermute | solution.py:116

commit v4 on v3

--- a/solution.py
+++ b/solution.py
@@ -54,19 +54,16 @@
 ):
     *out_refs, acc_ref, pieces_ref = rest
     blocks = acc_ref.shape[0] - 1
-    rows = blocks // 2
+    quarter = blocks // 4
     half = own_ref.shape[0]
     pieces_ref[:half] = own_ref[...]
     pieces_ref[half:] = other_ref[...]
     acc_ref[...] = jnp.zeros_like(acc_ref)
     for slot in range(coefs_ref.shape[0]):
         block = flow_ref[0, 0, slot]
-        ahead = (block // 2 - me_ref[0] + rows) % rows
-        upward = ahead < rows // 2
-        steps = jnp.where(upward, ahead, (rows - ahead) % (rows // 2))
-        odd = me_ref[0] % 2
-        second = jnp.where(steps == 0, jnp.where(ahead == 0, 0, 1), jnp.where(upward, odd, 1 - odd))
-        place = second * rows + steps * 2 + block % 2
+        row = block // 2
+        ahead = jnp.where(me_ref[0] % 2 == 0, row - me_ref[0], me_ref[0] - row)
+        place = ((ahead + 2 * blocks) % 4) * quarter + (row // 4) * 2 + block % 2
         place = jnp.where(live_ref[0, 0, slot] == 1, place, blocks)
         piece = link_ref[0, 0, slot]
         piece = ((piece + me_ref[1]) % 2) * half + piece // 2
@@ -81,14 +78,12 @@
 
 
 def flow_products(me, flow, link, live, coefs, own, other, blocks):
-    row = jax.ShapeDtypeStruct((2, BS, H), BF16)
-    half_row = jax.ShapeDtypeStruct((1, BS, H), BF16)
-    shapes = [row] * (blocks // 4) + [half_row] * 2 + [row] * (blocks // 4 - 1)
-    outs = pl.pallas_call(
+    counts = [blocks // 4, blocks // 4, blocks // 8, blocks // 8, blocks // 4]
+    return pl.pallas_call(
         flow_products_kernel,
-        out_shape=shapes,
+        out_shape=[jax.ShapeDtypeStruct((count, BS, H), BF16) for count in counts],
         in_specs=[SMEM, SMEM, SMEM, SMEM, VMEM, VMEM, VMEM],
-        out_specs=[VMEM] * len(shapes),
+        out_specs=[VMEM] * len(counts),
         scratch_shapes=[
             pltpu.VMEM((blocks + 1, BS, H), F32),
             pltpu.VMEM((2 * own.shape[0], BS, H), BF16),
@@ -96,28 +91,69 @@
         compiler_params=PARAMS,
         name="flow_products",
     )(me, flow, link, live, coefs, own, other)
-    side = blocks // 4
-    return outs[0], outs[1:side], outs[side], outs[side + 1], outs[side + 2 :]
+
+
+def near_sum_kernel(me_ref, own_ref, a_ref, b_ref, mine_ref, next_a_ref, half_a_ref, half_b_ref, next_b_ref):
+    group = me_ref[0] // 4
+    groups = own_ref.shape[0] // 2
+    forth = jnp.where(group % 2 == 0, 1, groups - 1)
+
+    def total(steps, part):
+        at = ((group + steps) % groups) * 2 + part
+        return (
+            own_ref[at].astype(F32) + a_ref[at].astype(F32) + b_ref[at].astype(F32)
+        ).astype(BF16)
+
+    for part in range(2):
+        mine_ref[part] = total(0, part)
+        next_a_ref[part] = total(forth, part)
+        next_b_ref[part] = total(groups - forth, part)
+    half_a_ref[0] = total(2, 0)
+    half_b_ref[0] = total(2, 1)
+
+
+def near_sum(me, own, a, b):
+    counts = [2, 2, 1, 1, 2]
+    return pl.pallas_call(
+        near_sum_kernel,
+        out_shape=[jax.ShapeDtypeStruct((count, BS, H), BF16) for count in counts],
+        in_specs=[SMEM, VMEM, VMEM, VMEM],
+        out_specs=[VMEM] * len(counts),
+        compiler_params=PARAMS,
+        name="near_sum",
+    )(me, own, a, b)
 
 
 def add(a, b):
     return (a.astype(F32) + b.astype(F32)).astype(BF16)
 
 
-def sum_over_rows(mine, for_a, half_a, half_b, for_b, rows):
-    swap_a = [(i, i ^ 1) for i in range(rows)]
-    swap_b = [(i, ((i - 1) ^ 1) + 1 if i % rows else rows - 1) for i in range(rows)]
-    swap_b = [(i, j % rows) for i, j in swap_b]
+def pair_ring(next_a, half_a, half_b, next_b, swap_a, swap_b):
+    cut = half_a.shape[0]
     got_a = lax.ppermute(half_a, "row", swap_a)
     got_b = lax.ppermute(half_b, "row", swap_b)
-    a = jnp.concatenate([for_a[-1][:1], add(for_a[-1][1:], got_b)], axis=0)
-    b = jnp.concatenate([add(for_b[-1][:1], got_a), for_b[-1][1:]], axis=0)
-    for step in range(len(for_a) - 2, -2, -1):
-        got_a = lax.ppermute(a, "row", swap_a)
-        got_b = lax.ppermute(b, "row", swap_b)
-        if step >= 0:
-            b = add(for_b[step], got_a)
-            a = add(for_a[step], got_b)
+    next_b = jnp.concatenate([add(next_b[:cut], got_a), next_b[cut:]], axis=0)
+    next_a = jnp.concatenate([next_a[:cut], add(next_a[cut:], got_b)], axis=0)
+    got_b = lax.ppermute(next_b, "row", swap_b)
+    got_a = lax.ppermute(next_a, "row", swap_a)
+    return got_a, got_b
+
+
+def sum_over_rows(me, own, near_a, half_a, half_b, near_b, rows):
+    def swaps(step):
+        return (
+            [(i, i ^ step) for i in range(rows)],
+            [(i, (((i - step) % rows) ^ step) + step) for i in range(rows)],
+        )
+
+    def wrap(pairs):
+        return [(i, j % rows) for i, j in pairs]
+
+    swap_a, swap_b = map(wrap, swaps(1))
+    got_a, got_b = pair_ring(near_a, half_a, half_b, near_b, swap_a, swap_b)
+    mine, far_a, half_a, half_b, far_b = near_sum(me, own, got_a, got_b)
+    swap_a, swap_b = map(wrap, swaps(4))
+    got_a, got_b = pair_ring(far_a, half_a, half_b, far_b, swap_a, swap_b)
     return jnp.stack([x.reshape(2 * BS, H) for x in (mine, got_a, got_b)])
 
 
@@ -205,10 +241,10 @@
     )
     own = lax.all_to_all(link_copies, "col", 0, 0, tiled=True, axis_index_groups=same_core)
     other = lax.ppermute(own, "col", sibling)
-    mine, for_a, half_a, half_b, for_b = flow_products(
+    parts = flow_products(
         me, tile_flow, tile_link, tile_live, coefs, own, other, flow_blocks
     )
-    flow_parts = sum_over_rows(mine, for_a, half_a, half_b, for_b, rows)
+    flow_parts = sum_over_rows(me, *parts, rows)
     (flow_next,) = update(
         flow_parts, flow_state, flow_gain, flow_agg_weight, flow_self_weight, flow_out_weight, 0
     )

time: 174 us -> 175 us (level)
  the two profiles are of different devices: /device:TPU:2 before, /device:TPU:96 now
where the time goes in v4:
time: 175 us
  blocking collectives  88.7 us (51%)
  waiting for transfers between devices  38.5 us (22%)
  starting transfers between devices  37.5 us (21%)
  Pallas kernels  6.65 us (4%)
  other arithmetic  1.95 us (1%)
    all_gather x1, blocking collectives, gather_rows(): got = lax.all_gather(sent, 'row', axis=0, tiled=True)  44.9 us
    all_to_all x1, blocking collectives, on_device(): lax.all_to_all(own, 'col', 0, 0, tiled=True, axis_index_groups=same_core)  24.3 us
    all_to_all x1, blocking collectives, on_device(): lax.all_to_all(link_copies, 'col', 0, 0, tiled=True, axis_index_groups=sa...  19.6 us
    ppermute x2, waiting for transfers between devices, pair_ring(): got_a = lax.ppermute(next_a, 'row', swap_a)  11.4 us
    ppermute x2, starting transfers between devices, pair_ring(): got_b = lax.ppermute(next_b, 'row', swap_b)  10.7 us
    ppermute x2, waiting for transfers between devices, pair_ring(): got_b = lax.ppermute(next_b, 'row', swap_b)  9.62 us
    ppermute x2, starting transfers between devices, pair_ring(): got_a = lax.ppermute(half_a, 'row', swap_a)  9.45 us
    ppermute x2, waiting for transfers between devices, pair_ring(): got_b = lax.ppermute(half_b, 'row', swap_b)  9.1 us
  transfers between devices with their start and end apart: 10, of which 9 were waited for; matrix products, arithmetic and copies ran while one was open for 0% of the time, Pallas kernels for 0%

profile of v4, /device:TPU:96, one launch (start us, length us, event | category | flops | bytes accessed | tf_op | source)
XLA Modules:
  0.0 174.8 jit_solution(10447921780512770153)
XLA Ops:
  0.6 0.9 multiply_convert_fusion.1
  1.6 44.9 %all-gather.1 = f16[4096,256]{1,0:T(8,128)(2,1)S(1)} all-gather(f16[256,256]{1,0:T(8,128)(2,1)S(1)} %multiply_convert_fusion.1), channel_id=1, replica_groups=mesh['row'=16,'col'=32] {'row'}, dimensions={0}, use_global_device_ids=true | all-gather | bytes 2228224 | tf_op jit(solution)/shard_map/all_gather | solution.py:256
  46.5 0.6 multiply_convert_fusion
  47.1 0.1 pad_add_fusion.me_ref
  47.1 0.5 copy-done
  47.6 1.6 link_products.1
  49.2 1.9 %collective-permute-start = (bf16[16,128,256]{2,1,0:T(8,128)(2,1)S(1)}, bf16[16,128,256]{2,1,0:T(8,128)(2,1)S(1)}, u32[]{:S(2)}, u32[]{:S(2)}) collective-permute-start(bf16[16,128,256]{2,1,0:T(8,128)(2,1)S(1)} %get-tuple-element.17), channel_id=1, source_target_pairs={{0,1},{1,0},{2,3},{3,2},{4,5},{5,4},{6,7},{7,6},{8,9},{9,8},{10,11... | collective-permute-start | bytes 3145736 | tf_op jit(solution)/shard_map/ppermute | solution.py:237
  51.1 2.6 %collective-permute-done.b_ref = bf16[16,128,256]{2,1,0:T(8,128)(2,1)S(1)} collective-permute-done((bf16[16,128,256]{2,1,0:T(8,128)(2,1)S(1)}, bf16[16,128,256]{2,1,0:T(8,128)(2,1)S(1)}, u32[]{:S(2)}, u32[]{:S(2)}) %collective-permute-start) | collective-permute-done | bytes 1048608 | tf_op jit(solution)/shard_map/ppermute | solution.py:237
  53.8 0.2 add_two.1
  54.0 24.3 %all_to_all.10.parts_ref = bf16[16,128,256]{2,1,0:T(8,128)(2,1)S(1)} all-to-all(bf16[16,128,256]{2,1,0:T(8,128)(2,1)S(1)} %add_two.1), channel_id=1, replica_groups={{0,2,4,6,8,10,12,14,16,18,20,22,24,26,28,30},{1,3,5,7,9,11,13,15,17,19,..., dimensions={0} | all-to-all | bytes 2097152 | tf_op jit(solution)/shard_map/all_to_all | solution.py:238
  78.3 1.2 link_update.1
  79.5 19.6 %all_to_all.11.own_ref = bf16[16,128,256]{2,1,0:T(8,128)(2,1)S(1)} all-to-all(bf16[16,128,256]{2,1,0:T(8,128)(2,1)S(1)} %get-tuple-element.19), channel_id=1, replica_groups={{0,2,4,6,8,10,12,14,16,18,20,22,24,26,28,30},{1,3,5,7,9,11,13,15,17,19,..., dimensions={0} | all-to-all | bytes 2097152 | tf_op jit(solution)/shard_map/all_to_all | solution.py:242
  99.1 1.9 %collective-permute-start.1 = (bf16[16,128,256]{2,1,0:T(8,128)(2,1)S(1)}, bf16[16,128,256]{2,1,0:T(8,128)(2,1)S(1)}, u32[]{:S(2)}, u32[]{:S(2)}) collective-permute-start(bf16[16,128,256]{2,1,0:T(8,128)(2,1)S(1)} %all_to_all.11.own_ref), channel_id=1, source_target_pairs={{0,1},{1,0},{2,3},{3,2},{4,5},{5,4},{6,7},{7,6},{8,9},{9,8},{10,11... | collective-permute-start | bytes 3145736 | tf_op jit(solution)/shard_map/ppermute | solution.py:243
  101.0 2.6 %collective-permute-done.1.other_ref = bf16[16,128,256]{2,1,0:T(8,128)(2,1)S(1)} collective-permute-done((bf16[16,128,256]{2,1,0:T(8,128)(2,1)S(1)}, bf16[16,128,256]{2,1,0:T(8,128)(2,1)S(1)}, u32[]{:S(2)}, u32[]{:S(2)}) %collective-permute-start.1) | collective-permute-done | bytes 1048608 | tf_op jit(solution)/shard_map/ppermute | solution.py:243
  103.6 1.8 %flow_products.1 = (bf16[8,128,256]{2,1,0:T(8,128)(2,1)S(1)}, bf16[8,128,256]{2,1,0:T(8,128)(2,1)S(1)}, bf16[4,128,256]{2,1,0:T(8,128)(2,1)S(1)}, bf16[4,128,256...) custom-call(s32[2]{0:T(128)S(1)} %pad_add_fusion.me_ref, s32[1,1,24]{2,1,0:T(1,128)S(1)} %copy-done.9, ...), custom_call_target="tpu_custom_call" | custom-call | tf_op jit(solution)/shard_map/flow_products/pallas_call | solution.py:82
  105.5 3.5 %collective-permute-start.4 = (bf16[4,128,256]{2,1,0:T(8,128)(2,1)S(1)}, bf16[4,128,256]{2,1,0:T(8,128)(2,1)S(1)}, u32[]{:S(2)}, u32[]{:S(2)}) collective-permute-start(bf16[4,128,256]{2,1,0:T(8,128)(2,1)S(1)} %get-tuple-element.24), channel_id=1, source_target_pairs={{0,32},{32,0},{64,96},{96,64},{128,160},{160,128},{192,224},{224,1... | collective-permute-start | bytes 786440 | tf_op jit(solution)/shard_map/ppermute | solution.py:133
  109.0 3.6 %collective-permute-start.2 = (bf16[4,128,256]{2,1,0:T(8,128)(2,1)S(1)}, bf16[4,128,256]{2,1,0:T(8,128)(2,1)S(1)}, u32[]{:S(2)}, u32[]{:S(2)}) collective-permute-start(bf16[4,128,256]{2,1,0:T(8,128)(2,1)S(1)} %get-tuple-element.22), channel_id=1, source_target_pairs={{0,480},{32,64},{64,32},{96,128},{128,96},{160,192},{192,160},{224... | collective-permute-start | bytes 786440 | tf_op jit(solution)/shard_map/ppermute | solution.py:134
  112.6 3.1 %collective-permute-done.4 = bf16[4,128,256]{2,1,0:T(8,128)(2,1)S(1)} collective-permute-done((bf16[4,128,256]{2,1,0:T(8,128)(2,1)S(1)}, bf16[4,128,256]{2,1,0:T(8,128)(2,1)S(1)}, u32[]{:S(2)}, u32[]{:S(2)}) %collective-permute-start.4) | collective-permute-done | bytes 262176 | tf_op jit(solution)/shard_map/ppermute | solution.py:133
  115.8 4.2 %collective-permute-start.5 = (bf16[8,128,256]{2,1,0:T(8,128)(2,1)S(1)}, bf16[8,128,256]{2,1,0:T(8,128)(2,1)S(1)}, u32[]{:S(2)}, u32[]{:S(2)}) collective-permute-start(bf16[8,128,256]{2,1,0:T(8,128)(2,1)S(1)} %pad_maximum_fusion.1), channel_id=1, source_target_pairs={{0,480},{32,64},{64,32},{96,128},{128,96},{160,192},{192,160},{224... | collective-permute-start | bytes 1572872 | tf_op jit(solution)/shard_map/ppermute | solution.py:137
  120.0 0.2 collective-permute-done.2
  120.4 2.7 %collective-permute-start.3 = (bf16[8,128,256]{2,1,0:T(8,128)(2,1)S(1)}, bf16[8,128,256]{2,1,0:T(8,128)(2,1)S(1)}, u32[]{:S(2)}, u32[]{:S(2)}) collective-permute-start(bf16[8,128,256]{2,1,0:T(8,128)(2,1)S(1)} %pad_maximum_fusion), channel_id=1, source_target_pairs={{0,32},{32,0},{64,96},{96,64},{128,160},{160,128},{192,224},{224,1... | collective-permute-start | bytes 1572872 | tf_op jit(solution)/shard_map/ppermute | solution.py:138
  123.1 9.0 %collective-permute-done.5.b_ref = bf16[8,128,256]{2,1,0:T(8,128)(2,1)S(1)} collective-permute-done((bf16[8,128,256]{2,1,0:T(8,128)(2,1)S(1)}, bf16[8,128,256]{2,1,0:T(8,128)(2,1)S(1)}, u32[]{:S(2)}, u32[]{:S(2)}) %collective-permute-start.5) | collective-permute-done | bytes 524320 | tf_op jit(solution)/shard_map/ppermute | solution.py:137
  132.1 3.1 %collective-permute-done.3.a_ref = bf16[8,128,256]{2,1,0:T(8,128)(2,1)S(1)} collective-permute-done((bf16[8,128,256]{2,1,0:T(8,128)(2,1)S(1)}, bf16[8,128,256]{2,1,0:T(8,128)(2,1)S(1)}, u32[]{:S(2)}, u32[]{:S(2)}) %collective-permute-start.3) | collective-permute-done | bytes 524320 | tf_op jit(solution)/shard_map/ppermute | solution.py:138
  135.2 0.7 near_sum.1
  136.0 6.0 %collective-permute-start.8 = (bf16[1,128,256]{2,1,0:T(8,128)(2,1)S(1)}, bf16[1,128,256]{2,1,0:T(8,128)(2,1)S(1)}, u32[]{:S(2)}, u32[]{:S(2)}) collective-permute-start(bf16[1,128,256]{2,1,0:T(8,128)(2,1)S(1)} %get-tuple-element.29), channel_id=1, source_target_pairs={{0,128},{32,160},{64,192},{96,224},{128,0},{160,32},{192,64},{224,... | collective-permute-start | bytes 196616 | tf_op jit(solution)/shard_map/ppermute | solution.py:133
  142.0 5.3 %collective-permute-start.6 = (bf16[1,128,256]{2,1,0:T(8,128)(2,1)S(1)}, bf16[1,128,256]{2,1,0:T(8,128)(2,1)S(1)}, u32[]{:S(2)}, u32[]{:S(2)}) collective-permute-start(bf16[1,128,256]{2,1,0:T(8,128)(2,1)S(1)} %get-tuple-element.27), channel_id=1, source_target_pairs={{0,384},{32,416},{64,448},{96,480},{128,256},{160,288},{192,320},{... | collective-permute-start | bytes 196616 | tf_op jit(solution)/shard_map/ppermute | solution.py:134
  147.4 6.5 %collective-permute-start.9 = (bf16[2,128,256]{2,1,0:T(8,128)(2,1)S(1)}, bf16[2,128,256]{2,1,0:T(8,128)(2,1)S(1)}, u32[]{:S(2)}, u32[]{:S(2)}) collective-permute-start(bf16[2,128,256]{2,1,0:T(8,128)(2,1)S(1)} %pad_maximum_fusion.4), channel_id=1, source_target_pairs={{0,384},{32,416},{64,448},{96,480},{128,256},{160,288},{192,320},{... | collective-permute-start | bytes 393224 | tf_op jit(solution)/shard_map/ppermute | solution.py:137
  153.9 8.9 %collective-permute-done.6 = bf16[1,128,256]{2,1,0:T(8,128)(2,1)S(1)} collective-permute-done((bf16[1,128,256]{2,1,0:T(8,128)(2,1)S(1)}, bf16[1,128,256]{2,1,0:T(8,128)(2,1)S(1)}, u32[]{:S(2)}, u32[]{:S(2)}) %collective-permute-start.6) | collective-permute-done | bytes 65568 | tf_op jit(solution)/shard_map/ppermute | solution.py:134
  162.9 1.9 %collective-permute-start.7 = (bf16[2,128,256]{2,1,0:T(8,128)(2,1)S(1)}, bf16[2,128,256]{2,1,0:T(8,128)(2,1)S(1)}, u32[]{:S(2)}, u32[]{:S(2)}) collective-permute-start(bf16[2,128,256]{2,1,0:T(8,128)(2,1)S(1)} %pad_maximum_fusion.3), channel_id=1, source_target_pairs={{0,128},{32,160},{64,192},{96,224},{128,0},{160,32},{192,64},{224,... | collective-permute-start | bytes 393224 | tf_op jit(solution)/shard_map/ppermute | solution.py:138
  164.8 0.6 collective-permute-done.9
  165.4 8.2 %collective-permute-done.7 = bf16[2,128,256]{2,1,0:T(8,128)(2,1)S(1)} collective-permute-done((bf16[2,128,256]{2,1,0:T(8,128)(2,1)S(1)}, bf16[2,128,256]{2,1,0:T(8,128)(2,1)S(1)}, u32[]{:S(2)}, u32[]{:S(2)}) %collective-permute-start.7) | collective-permute-done | bytes 131104 | tf_op jit(solution)/shard_map/ppermute | solution.py:138
  173.8 1.1 flow_update.1
  (41 shorter events, 0.5 us)
Async XLA Ops:
  46.5 1.1 copy-start
  46.5 1.1 copy-start.9
  46.5 1.1 copy-start.10
  46.5 1.1 copy-start.11
  49.2 4.6 %collective-permute-start = (bf16[16,128,256]{2,1,0:T(8,128)(2,1)S(1)}, bf16[16,128,256]{2,1,0:T(8,128)(2,1)S(1)}, u32[]{:S(2)}, u32[]{:S(2)}) collective-permute-start(bf16[16,128,256]{2,1,0:T(8,128)(2,1)S(1)} %get-tuple-element.17), channel_id=1, source_target_pairs={{0,1},{1,0},{2,3},{3,2},{4,5},{5,4},{6,7},{7,6},{8,9},{9,8},{10,11... | collective-permute-start | bytes 3145736 | tf_op jit(solution)/shard_map/ppermute | solution.py:237
  53.8 24.6 %copy-start.2 = (bf16[256,256]{1,0:T(8,128)(2,1)S(1)}, bf16[256,256]{1,0:T(8,128)(2,1)}, u32[]{:S(2)}) copy-start(bf16[256,256]{1,0:T(8,128)(2,1)} %agg_ref.2) | copy-start | bytes 393220
  53.8 24.6 %copy-start.3 = (bf16[256,256]{1,0:T(8,128)(2,1)S(1)}, bf16[256,256]{1,0:T(8,128)(2,1)}, u32[]{:S(2)}) copy-start(bf16[256,256]{1,0:T(8,128)(2,1)} %self_ref.2) | copy-start | bytes 393220
  53.8 24.6 %copy-start.4 = (bf16[256,256]{1,0:T(8,128)(2,1)S(1)}, bf16[256,256]{1,0:T(8,128)(2,1)}, u32[]{:S(2)}) copy-start(bf16[256,256]{1,0:T(8,128)(2,1)} %out_w_ref.2) | copy-start | bytes 393220
  53.8 24.6 %copy-start.8 = (bf16[128,256]{1,0:T(8,128)(2,1)S(1)}, bf16[128,256]{1,0:T(8,128)(2,1)}, u32[]{:S(2)}) copy-start(bf16[128,256]{1,0:T(8,128)(2,1)} %state_ref.2) | copy-start | bytes 196612
  53.8 24.6 %copy-start.12 = (f32[256]{0:T(256)S(1)}, f32[256]{0:T(256)}, u32[]{:S(2)}) copy-start(f32[256]{0:T(256)} %param.20) | copy-start | bytes 3076
  99.1 4.5 %collective-permute-start.1 = (bf16[16,128,256]{2,1,0:T(8,128)(2,1)S(1)}, bf16[16,128,256]{2,1,0:T(8,128)(2,1)S(1)}, u32[]{:S(2)}, u32[]{:S(2)}) collective-permute-start(bf16[16,128,256]{2,1,0:T(8,128)(2,1)S(1)} %all_to_all.11.own_ref), channel_id=1, source_target_pairs={{0,1},{1,0},{2,3},{3,2},{4,5},{5,4},{6,7},{7,6},{8,9},{9,8},{10,11... | collective-permute-start | bytes 3145736 | tf_op jit(solution)/shard_map/ppermute | solution.py:243
  105.5 10.2 %collective-permute-start.4 = (bf16[4,128,256]{2,1,0:T(8,128)(2,1)S(1)}, bf16[4,128,256]{2,1,0:T(8,128)(2,1)S(1)}, u32[]{:S(2)}, u32[]{:S(2)}) collective-permute-start(bf16[4,128,256]{2,1,0:T(8,128)(2,1)S(1)} %get-tuple-element.24), channel_id=1, source_target_pairs={{0,32},{32,0},{64,96},{96,64},{128,160},{160,128},{192,224},{224,1... | collective-permute-start | bytes 786440 | tf_op jit(solution)/shard_map/ppermute | solution.py:133
  109.0 11.2 %collective-permute-start.2 = (bf16[4,128,256]{2,1,0:T(8,128)(2,1)S(1)}, bf16[4,128,256]{2,1,0:T(8,128)(2,1)S(1)}, u32[]{:S(2)}, u32[]{:S(2)}) collective-permute-start(bf16[4,128,256]{2,1,0:T(8,128)(2,1)S(1)} %get-tuple-element.22), channel_id=1, source_target_pairs={{0,480},{32,64},{64,32},{96,128},{128,96},{160,192},{192,160},{224... | collective-permute-start | bytes 786440 | tf_op jit(solution)/shard_map/ppermute | solution.py:134
  115.8 16.2 %collective-permute-start.5 = (bf16[8,128,256]{2,1,0:T(8,128)(2,1)S(1)}, bf16[8,128,256]{2,1,0:T(8,128)(2,1)S(1)}, u32[]{:S(2)}, u32[]{:S(2)}) collective-permute-start(bf16[8,128,256]{2,1,0:T(8,128)(2,1)S(1)} %pad_maximum_fusion.1), channel_id=1, source_target_pairs={{0,480},{32,64},{64,32},{96,128},{128,96},{160,192},{192,160},{224... | collective-permute-start | bytes 1572872 | tf_op jit(solution)/shard_map/ppermute | solution.py:137
  120.2 53.5 %copy-start.1 = (bf16[256,256]{1,0:T(8,128)(2,1)S(1)}, bf16[256,256]{1,0:T(8,128)(2,1)}, u32[]{:S(2)}) copy-start(bf16[256,256]{1,0:T(8,128)(2,1)} %state_ref.3) | copy-start | bytes 393220
  120.3 53.5 %copy-start.5 = (bf16[256,256]{1,0:T(8,128)(2,1)S(1)}, bf16[256,256]{1,0:T(8,128)(2,1)}, u32[]{:S(2)}) copy-start(bf16[256,256]{1,0:T(8,128)(2,1)} %agg_ref.3) | copy-start | bytes 393220
  120.3 53.5 %copy-start.6 = (bf16[256,256]{1,0:T(8,128)(2,1)S(1)}, bf16[256,256]{1,0:T(8,128)(2,1)}, u32[]{:S(2)}) copy-start(bf16[256,256]{1,0:T(8,128)(2,1)} %self_ref.3) | copy-start | bytes 393220
  120.3 53.5 %copy-start.7 = (bf16[256,256]{1,0:T(8,128)(2,1)S(1)}, bf16[256,256]{1,0:T(8,128)(2,1)}, u32[]{:S(2)}) copy-start(bf16[256,256]{1,0:T(8,128)(2,1)} %out_w_ref.3) | copy-start | bytes 393220
  120.3 53.5 %copy-start.13 = (f32[256]{0:T(256)S(1)}, f32[256]{0:T(256)}, u32[]{:S(2)}) copy-start(f32[256]{0:T(256)} %param.24) | copy-start | bytes 3076
  120.4 14.8 %collective-permute-start.3 = (bf16[8,128,256]{2,1,0:T(8,128)(2,1)S(1)}, bf16[8,128,256]{2,1,0:T(8,128)(2,1)S(1)}, u32[]{:S(2)}, u32[]{:S(2)}) collective-permute-start(bf16[8,128,256]{2,1,0:T(8,128)(2,1)S(1)} %pad_maximum_fusion), channel_id=1, source_target_pairs={{0,32},{32,0},{64,96},{96,64},{128,160},{160,128},{192,224},{224,1... | collective-permute-start | bytes 1572872 | tf_op jit(solution)/shard_map/ppermute | solution.py:138
  136.0 11.4 %collective-permute-start.8 = (bf16[1,128,256]{2,1,0:T(8,128)(2,1)S(1)}, bf16[1,128,256]{2,1,0:T(8,128)(2,1)S(1)}, u32[]{:S(2)}, u32[]{:S(2)}) collective-permute-start(bf16[1,128,256]{2,1,0:T(8,128)(2,1)S(1)} %get-tuple-element.29), channel_id=1, source_target_pairs={{0,128},{32,160},{64,192},{96,224},{128,0},{160,32},{192,64},{224,... | collective-permute-start | bytes 196616 | tf_op jit(solution)/shard_map/ppermute | solution.py:133
  142.0 20.9 %collective-permute-start.6 = (bf16[1,128,256]{2,1,0:T(8,128)(2,1)S(1)}, bf16[1,128,256]{2,1,0:T(8,128)(2,1)S(1)}, u32[]{:S(2)}, u32[]{:S(2)}) collective-permute-start(bf16[1,128,256]{2,1,0:T(8,128)(2,1)S(1)} %get-tuple-element.27), channel_id=1, source_target_pairs={{0,384},{32,416},{64,448},{96,480},{128,256},{160,288},{192,320},{... | collective-permute-start | bytes 196616 | tf_op jit(solution)/shard_map/ppermute | solution.py:134
  147.4 18.0 %collective-permute-start.9 = (bf16[2,128,256]{2,1,0:T(8,128)(2,1)S(1)}, bf16[2,128,256]{2,1,0:T(8,128)(2,1)S(1)}, u32[]{:S(2)}, u32[]{:S(2)}) collective-permute-start(bf16[2,128,256]{2,1,0:T(8,128)(2,1)S(1)} %pad_maximum_fusion.4), channel_id=1, source_target_pairs={{0,384},{32,416},{64,448},{96,480},{128,256},{160,288},{192,320},{... | collective-permute-start | bytes 393224 | tf_op jit(solution)/shard_map/ppermute | solution.py:137
  162.9 10.8 %collective-permute-start.7 = (bf16[2,128,256]{2,1,0:T(8,128)(2,1)S(1)}, bf16[2,128,256]{2,1,0:T(8,128)(2,1)S(1)}, u32[]{:S(2)}, u32[]{:S(2)}) collective-permute-start(bf16[2,128,256]{2,1,0:T(8,128)(2,1)S(1)} %pad_maximum_fusion.3), channel_id=1, source_target_pairs={{0,128},{32,160},{64,192},{96,224},{128,0},{160,32},{192,64},{224,... | collective-permute-start | bytes 393224 | tf_op jit(solution)/shard_map/ppermute | solution.py:138

commit v5 on v4

--- a/solution.py
+++ b/solution.py
@@ -132,11 +132,14 @@
     cut = half_a.shape[0]
     got_a = lax.ppermute(half_a, "row", swap_a)
     got_b = lax.ppermute(half_b, "row", swap_b)
-    next_b = jnp.concatenate([add(next_b[:cut], got_a), next_b[cut:]], axis=0)
-    next_a = jnp.concatenate([next_a[:cut], add(next_a[cut:], got_b)], axis=0)
-    got_b = lax.ppermute(next_b, "row", swap_b)
-    got_a = lax.ppermute(next_a, "row", swap_a)
-    return got_a, got_b
+    plain_a = lax.ppermute(next_a[:cut], "row", swap_a)
+    plain_b = lax.ppermute(next_b[cut:], "row", swap_b)
+    summed_b = lax.ppermute(add(next_b[:cut], got_a), "row", swap_b)
+    summed_a = lax.ppermute(add(next_a[cut:], got_b), "row", swap_a)
+    return (
+        jnp.concatenate([plain_a, summed_a], axis=0),
+        jnp.concatenate([summed_b, plain_b], axis=0),
+    )
 
 
 def sum_over_rows(me, own, near_a, half_a, half_b, near_b, rows):

time: 175 us -> 179 us (1.023)
  the two profiles are of different devices: /device:TPU:96 before, /device:TPU:1 now
where the time goes in v5:
time: 179 us; the launch traced here: 178 us
  blocking collectives  86.5 us (48%)
  starting transfers between devices  53.5 us (30%)
  waiting for transfers between devices  28.1 us (16%)
  Pallas kernels  6.65 us (4%)
  other arithmetic  1.95 us (1%)
    all_gather x1, blocking collectives, gather_rows(): got = lax.all_gather(sent, 'row', axis=0, tiled=True)  44.6 us
    all_to_all x1, blocking collectives, on_device(): lax.all_to_all(own, 'col', 0, 0, tiled=True, axis_index_groups=same_core)  22.9 us
    all_to_all x1, blocking collectives, on_device(): lax.all_to_all(link_copies, 'col', 0, 0, tiled=True, axis_index_groups=sa...  19 us
    ppermute x2, waiting for transfers between devices, pair_ring(): got_a = lax.ppermute(half_a, 'row', swap_a)  10.5 us
    ppermute x1, starting transfers between devices, on_device(): own = add_two(own, lax.ppermute(other, 'col', sibling))  8.14 us
    ppermute x2, starting transfers between devices, pair_ring(): plain_b = lax.ppermute(next_b[cut:], 'row', swap_b)  8.12 us
    ppermute x2, starting transfers between devices, pair_ring(): got_b = lax.ppermute(half_b, 'row', swap_b)  7.33 us
    ppermute x2, starting transfers between devices, pair_ring(): summed_a = lax.ppermute(add(next_a[cut:], got_b), 'row', swap_a)  7.33 us
  transfers between devices with their start and end apart: 14, of which 8 were waited for; matrix products, arithmetic and copies ran while one was open for 0% of the time, Pallas kernels for 0%

profile of v5, /device:TPU:1, one launch (start us, length us, event | category | flops | bytes accessed | tf_op | source)
XLA Modules:
  0.0 178.3 jit_solution(12217725687319807891)
XLA Ops:
  0.6 0.9 multiply_convert_fusion.1
  1.6 44.6 %all-gather.1 = f16[4096,256]{1,0:T(8,128)(2,1)S(1)} all-gather(f16[256,256]{1,0:T(8,128)(2,1)S(1)} %multiply_convert_fusion.1), channel_id=1, replica_groups=mesh['row'=16,'col'=32] {'row'}, dimensions={0}, use_global_device_ids=true | all-gather | bytes 2228224 | tf_op jit(solution)/shard_map/all_gather | solution.py:259
  46.2 0.6 multiply_convert_fusion
  46.9 0.5 copy-done
  47.3 1.6 link_products.1
  48.9 8.1 %collective-permute-start = (bf16[16,128,256]{2,1,0:T(8,128)(2,1)S(1)}, bf16[16,128,256]{2,1,0:T(8,128)(2,1)S(1)}, u32[]{:S(2)}, u32[]{:S(2)}) collective-permute-start(bf16[16,128,256]{2,1,0:T(8,128)(2,1)S(1)} %get-tuple-element.17), channel_id=1, source_target_pairs={{0,1},{1,0},{2,3},{3,2},{4,5},{5,4},{6,7},{7,6},{8,9},{9,8},{10,11... | collective-permute-start | bytes 3145736 | tf_op jit(solution)/shard_map/ppermute | solution.py:240
  57.1 2.3 %collective-permute-done.b_ref = bf16[16,128,256]{2,1,0:T(8,128)(2,1)S(1)} collective-permute-done((bf16[16,128,256]{2,1,0:T(8,128)(2,1)S(1)}, bf16[16,128,256]{2,1,0:T(8,128)(2,1)S(1)}, u32[]{:S(2)}, u32[]{:S(2)}) %collective-permute-start) | collective-permute-done | bytes 1048608 | tf_op jit(solution)/shard_map/ppermute | solution.py:240
  59.6 22.9 %all_to_all.10.parts_ref = bf16[16,128,256]{2,1,0:T(8,128)(2,1)S(1)} all-to-all(bf16[16,128,256]{2,1,0:T(8,128)(2,1)S(1)} %add_two.1), channel_id=1, replica_groups={{0,2,4,6,8,10,12,14,16,18,20,22,24,26,28,30},{1,3,5,7,9,11,13,15,17,19,..., dimensions={0} | all-to-all | bytes 2097152 | tf_op jit(solution)/shard_map/all_to_all | solution.py:241
  82.5 1.2 link_update.1
  83.7 19.0 %all_to_all.11.own_ref = bf16[16,128,256]{2,1,0:T(8,128)(2,1)S(1)} all-to-all(bf16[16,128,256]{2,1,0:T(8,128)(2,1)S(1)} %get-tuple-element.19), channel_id=1, replica_groups={{0,2,4,6,8,10,12,14,16,18,20,22,24,26,28,30},{1,3,5,7,9,11,13,15,17,19,..., dimensions={0} | all-to-all | bytes 2097152 | tf_op jit(solution)/shard_map/all_to_all | solution.py:245
  102.7 4.2 %collective-permute-start.1 = (bf16[16,128,256]{2,1,0:T(8,128)(2,1)S(1)}, bf16[16,128,256]{2,1,0:T(8,128)(2,1)S(1)}, u32[]{:S(2)}, u32[]{:S(2)}) collective-permute-start(bf16[16,128,256]{2,1,0:T(8,128)(2,1)S(1)} %all_to_all.11.own_ref), channel_id=1, source_target_pairs={{0,1},{1,0},{2,3},{3,2},{4,5},{5,4},{6,7},{7,6},{8,9},{9,8},{10,11... | collective-permute-start | bytes 3145736 | tf_op jit(solution)/shard_map/ppermute | solution.py:246
  107.0 2.3 %collective-permute-done.1.other_ref = bf16[16,128,256]{2,1,0:T(8,128)(2,1)S(1)} collective-permute-done((bf16[16,128,256]{2,1,0:T(8,128)(2,1)S(1)}, bf16[16,128,256]{2,1,0:T(8,128)(2,1)S(1)}, u32[]{:S(2)}, u32[]{:S(2)}) %collective-permute-start.1) | collective-permute-done | bytes 1048608 | tf_op jit(solution)/shard_map/ppermute | solution.py:246
  109.2 1.8 %flow_products.1 = (bf16[8,128,256]{2,1,0:T(8,128)(2,1)S(1)}, bf16[8,128,256]{2,1,0:T(8,128)(2,1)S(1)}, bf16[4,128,256]{2,1,0:T(8,128)(2,1)S(1)}, bf16[4,128,256...) custom-call(s32[2]{0:T(128)S(1)} %pad_add_fusion.me_ref, s32[1,1,24]{2,1,0:T(1,128)S(1)} %copy-done.9, ...), custom_call_target="tpu_custom_call" | custom-call | tf_op jit(solution)/shard_map/flow_products/pallas_call | solution.py:82
  111.1 1.9 %collective-permute-start.3 = (bf16[4,128,256]{2,1,0:T(8,128)(2,1)S(1)}, bf16[4,128,256]{2,1,0:T(8,128)(2,1)S(1)}, u32[]{:S(2)}, u32[]{:S(2)}) collective-permute-start(bf16[4,128,256]{2,1,0:T(8,128)(2,1)S(1)} %get-tuple-element.22), channel_id=1, source_target_pairs={{0,480},{32,64},{64,32},{96,128},{128,96},{160,192},{192,160},{224... | collective-permute-start | bytes 786440 | tf_op jit(solution)/shard_map/ppermute | solution.py:134
  113.0 2.2 %collective-permute-start.5 = (bf16[4,128,256]{2,1,0:T(8,128)(2,1)S(1)}, bf16[4,128,256]{2,1,0:T(8,128)(2,1)S(1)}, u32[]{:S(2)}, u32[]{:S(2)}) collective-permute-start(bf16[4,128,256]{2,1,0:T(8,128)(2,1)S(1)} %get-tuple-element.24), channel_id=1, source_target_pairs={{0,32},{32,0},{64,96},{96,64},{128,160},{160,128},{192,224},{224,1... | collective-permute-start | bytes 786440 | tf_op jit(solution)/shard_map/ppermute | solution.py:133
  115.2 4.3 %collective-permute-start.7 = (bf16[4,128,256]{2,1,0:T(8,128)(2,1)S(1)}, bf16[4,128,256]{2,1,0:T(8,128)(2,1)S(1)}, u32[]{:S(2)}, u32[]{:S(2)}) collective-permute-start(bf16[4,128,256]{2,1,0:T(8,128)(2,1)S(1)} %slice.27), channel_id=1, source_target_pairs={{0,480},{32,64},{64,32},{96,128},{128,96},{160,192},{192,160},{224... | collective-permute-start | bytes 786440 | tf_op jit(solution)/shard_map/ppermute | solution.py:136
  119.6 1.9 %collective-permute-start.2 = (bf16[4,128,256]{2,1,0:T(8,128)(2,1)S(1)}, bf16[4,128,256]{2,1,0:T(8,128)(2,1)S(1)}, u32[]{:S(2)}, u32[]{:S(2)}) collective-permute-start(bf16[4,128,256]{2,1,0:T(8,128)(2,1)S(1)} %slice.24), channel_id=1, source_target_pairs={{0,32},{32,0},{64,96},{96,64},{128,160},{160,128},{192,224},{224,1... | collective-permute-start | bytes 786440 | tf_op jit(solution)/shard_map/ppermute | solution.py:135
  121.8 3.2 %collective-permute-start.4 = (bf16[4,128,256]{2,1,0:T(8,128)(2,1)S(1)}, bf16[4,128,256]{2,1,0:T(8,128)(2,1)S(1)}, u32[]{:S(2)}, u32[]{:S(2)}) collective-permute-start(bf16[4,128,256]{2,1,0:T(8,128)(2,1)S(1)} %add_convert_fusion.1), channel_id=1, source_target_pairs={{0,32},{32,0},{64,96},{96,64},{128,160},{160,128},{192,224},{224,1... | collective-permute-start | bytes 786440 | tf_op jit(solution)/shard_map/ppermute | solution.py:138
  125.0 2.2 %collective-permute-start.6 = (bf16[4,128,256]{2,1,0:T(8,128)(2,1)S(1)}, bf16[4,128,256]{2,1,0:T(8,128)(2,1)S(1)}, u32[]{:S(2)}, u32[]{:S(2)}) collective-permute-start(bf16[4,128,256]{2,1,0:T(8,128)(2,1)S(1)} %add_convert_fusion), channel_id=1, source_target_pairs={{0,480},{32,64},{64,32},{96,128},{128,96},{160,192},{192,160},{224... | collective-permute-start | bytes 786440 | tf_op jit(solution)/shard_map/ppermute | solution.py:137
  127.2 0.9 collective-permute-done.2
  128.1 5.6 %collective-permute-done.4 = bf16[4,128,256]{2,1,0:T(8,128)(2,1)S(1)} collective-permute-done((bf16[4,128,256]{2,1,0:T(8,128)(2,1)S(1)}, bf16[4,128,256]{2,1,0:T(8,128)(2,1)S(1)}, u32[]{:S(2)}, u32[]{:S(2)}) %collective-permute-start.4) | collective-permute-done | bytes 262176 | tf_op jit(solution)/shard_map/ppermute | solution.py:138
  133.8 0.4 collective-permute-done.6
  134.3 0.7 near_sum.1
  135.0 5.4 %collective-permute-start.9 = (bf16[1,128,256]{2,1,0:T(8,128)(2,1)S(1)}, bf16[1,128,256]{2,1,0:T(8,128)(2,1)S(1)}, u32[]{:S(2)}, u32[]{:S(2)}) collective-permute-start(bf16[1,128,256]{2,1,0:T(8,128)(2,1)S(1)} %get-tuple-element.27), channel_id=1, source_target_pairs={{0,384},{32,416},{64,448},{96,480},{128,256},{160,288},{192,320},{... | collective-permute-start | bytes 196616 | tf_op jit(solution)/shard_map/ppermute | solution.py:134
  140.5 3.8 %collective-permute-start.13 = (bf16[1,128,256]{2,1,0:T(8,128)(2,1)S(1)}, bf16[1,128,256]{2,1,0:T(8,128)(2,1)S(1)}, u32[]{:S(2)}, u32[]{:S(2)}) collective-permute-start(bf16[1,128,256]{2,1,0:T(8,128)(2,1)S(1)} %slice.31), channel_id=1, source_target_pairs={{0,384},{32,416},{64,448},{96,480},{128,256},{160,288},{192,320},{... | collective-permute-start | bytes 196616 | tf_op jit(solution)/shard_map/ppermute | solution.py:136
  144.2 4.2 %collective-permute-start.8 = (bf16[1,128,256]{2,1,0:T(8,128)(2,1)S(1)}, bf16[1,128,256]{2,1,0:T(8,128)(2,1)S(1)}, u32[]{:S(2)}, u32[]{:S(2)}) collective-permute-start(bf16[1,128,256]{2,1,0:T(8,128)(2,1)S(1)} %slice.28), channel_id=1, source_target_pairs={{0,128},{32,160},{64,192},{96,224},{128,0},{160,32},{192,64},{224,... | collective-permute-start | bytes 196616 | tf_op jit(solution)/shard_map/ppermute | solution.py:135
  148.4 5.0 %collective-permute-start.11 = (bf16[1,128,256]{2,1,0:T(8,128)(2,1)S(1)}, bf16[1,128,256]{2,1,0:T(8,128)(2,1)S(1)}, u32[]{:S(2)}, u32[]{:S(2)}) collective-permute-start(bf16[1,128,256]{2,1,0:T(8,128)(2,1)S(1)} %get-tuple-element.29), channel_id=1, source_target_pairs={{0,128},{32,160},{64,192},{96,224},{128,0},{160,32},{192,64},{224,... | collective-permute-start | bytes 196616 | tf_op jit(solution)/shard_map/ppermute | solution.py:133
  153.5 4.2 %collective-permute-start.10 = (bf16[1,128,256]{2,1,0:T(8,128)(2,1)S(1)}, bf16[1,128,256]{2,1,0:T(8,128)(2,1)S(1)}, u32[]{:S(2)}, u32[]{:S(2)}) collective-permute-start(bf16[1,128,256]{2,1,0:T(8,128)(2,1)S(1)} %add_convert_fusion.3), channel_id=1, source_target_pairs={{0,128},{32,160},{64,192},{96,224},{128,0},{160,32},{192,64},{224,... | collective-permute-start | bytes 196616 | tf_op jit(solution)/shard_map/ppermute | solution.py:138
  157.6 10.5 %collective-permute-done.11 = bf16[1,128,256]{2,1,0:T(8,128)(2,1)S(1)} collective-permute-done((bf16[1,128,256]{2,1,0:T(8,128)(2,1)S(1)}, bf16[1,128,256]{2,1,0:T(8,128)(2,1)S(1)}, u32[]{:S(2)}, u32[]{:S(2)}) %collective-permute-start.11) | collective-permute-done | bytes 65568 | tf_op jit(solution)/shard_map/ppermute | solution.py:133
  168.2 3.0 %collective-permute-start.12 = (bf16[1,128,256]{2,1,0:T(8,128)(2,1)S(1)}, bf16[1,128,256]{2,1,0:T(8,128)(2,1)S(1)}, u32[]{:S(2)}, u32[]{:S(2)}) collective-permute-start(bf16[1,128,256]{2,1,0:T(8,128)(2,1)S(1)} %add_convert_fusion.2), channel_id=1, source_target_pairs={{0,384},{32,416},{64,448},{96,480},{128,256},{160,288},{192,320},{... | collective-permute-start | bytes 196616 | tf_op jit(solution)/shard_map/ppermute | solution.py:137
  171.2 5.9 %collective-permute-done.12 = bf16[1,128,256]{2,1,0:T(8,128)(2,1)S(1)} collective-permute-done((bf16[1,128,256]{2,1,0:T(8,128)(2,1)S(1)}, bf16[1,128,256]{2,1,0:T(8,128)(2,1)S(1)}, u32[]{:S(2)}, u32[]{:S(2)}) %collective-permute-start.12) | collective-permute-done | bytes 65568 | tf_op jit(solution)/shard_map/ppermute | solution.py:137
  177.2 1.1 flow_update.1
  (49 shorter events, 1.0 us)
Async XLA Ops:
  46.2 1.1 copy-start
  46.2 1.1 copy-start.9
  46.2 1.1 copy-start.10
  46.2 1.1 copy-start.11
  48.9 10.4 %collective-permute-start = (bf16[16,128,256]{2,1,0:T(8,128)(2,1)S(1)}, bf16[16,128,256]{2,1,0:T(8,128)(2,1)S(1)}, u32[]{:S(2)}, u32[]{:S(2)}) collective-permute-start(bf16[16,128,256]{2,1,0:T(8,128)(2,1)S(1)} %get-tuple-element.17), channel_id=1, source_target_pairs={{0,1},{1,0},{2,3},{3,2},{4,5},{5,4},{6,7},{7,6},{8,9},{9,8},{10,11... | collective-permute-start | bytes 3145736 | tf_op jit(solution)/shard_map/ppermute | solution.py:240
  59.3 23.1 %copy-start.2 = (bf16[256,256]{1,0:T(8,128)(2,1)S(1)}, bf16[256,256]{1,0:T(8,128)(2,1)}, u32[]{:S(2)}) copy-start(bf16[256,256]{1,0:T(8,128)(2,1)} %agg_ref.2) | copy-start | bytes 393220
  59.3 23.2 %copy-start.3 = (bf16[256,256]{1,0:T(8,128)(2,1)S(1)}, bf16[256,256]{1,0:T(8,128)(2,1)}, u32[]{:S(2)}) copy-start(bf16[256,256]{1,0:T(8,128)(2,1)} %self_ref.2) | copy-start | bytes 393220
  59.4 23.2 %copy-start.4 = (bf16[256,256]{1,0:T(8,128)(2,1)S(1)}, bf16[256,256]{1,0:T(8,128)(2,1)}, u32[]{:S(2)}) copy-start(bf16[256,256]{1,0:T(8,128)(2,1)} %out_w_ref.2) | copy-start | bytes 393220
  59.4 23.2 %copy-start.8 = (bf16[128,256]{1,0:T(8,128)(2,1)S(1)}, bf16[128,256]{1,0:T(8,128)(2,1)}, u32[]{:S(2)}) copy-start(bf16[128,256]{1,0:T(8,128)(2,1)} %state_ref.2) | copy-start | bytes 196612
  59.4 23.2 %copy-start.12 = (f32[256]{0:T(256)S(1)}, f32[256]{0:T(256)}, u32[]{:S(2)}) copy-start(f32[256]{0:T(256)} %param.20) | copy-start | bytes 3076
  102.7 6.5 %collective-permute-start.1 = (bf16[16,128,256]{2,1,0:T(8,128)(2,1)S(1)}, bf16[16,128,256]{2,1,0:T(8,128)(2,1)S(1)}, u32[]{:S(2)}, u32[]{:S(2)}) collective-permute-start(bf16[16,128,256]{2,1,0:T(8,128)(2,1)S(1)} %all_to_all.11.own_ref), channel_id=1, source_target_pairs={{0,1},{1,0},{2,3},{3,2},{4,5},{5,4},{6,7},{7,6},{8,9},{9,8},{10,11... | collective-permute-start | bytes 3145736 | tf_op jit(solution)/shard_map/ppermute | solution.py:246
  111.1 10.6 %collective-permute-start.3 = (bf16[4,128,256]{2,1,0:T(8,128)(2,1)S(1)}, bf16[4,128,256]{2,1,0:T(8,128)(2,1)S(1)}, u32[]{:S(2)}, u32[]{:S(2)}) collective-permute-start(bf16[4,128,256]{2,1,0:T(8,128)(2,1)S(1)} %get-tuple-element.22), channel_id=1, source_target_pairs={{0,480},{32,64},{64,32},{96,128},{128,96},{160,192},{192,160},{224... | collective-permute-start | bytes 786440 | tf_op jit(solution)/shard_map/ppermute | solution.py:134
  113.0 11.9 %collective-permute-start.5 = (bf16[4,128,256]{2,1,0:T(8,128)(2,1)S(1)}, bf16[4,128,256]{2,1,0:T(8,128)(2,1)S(1)}, u32[]{:S(2)}, u32[]{:S(2)}) collective-permute-start(bf16[4,128,256]{2,1,0:T(8,128)(2,1)S(1)} %get-tuple-element.24), channel_id=1, source_target_pairs={{0,32},{32,0},{64,96},{96,64},{128,160},{160,128},{192,224},{224,1... | collective-permute-start | bytes 786440 | tf_op jit(solution)/shard_map/ppermute | solution.py:133
  115.2 18.6 %collective-permute-start.7 = (bf16[4,128,256]{2,1,0:T(8,128)(2,1)S(1)}, bf16[4,128,256]{2,1,0:T(8,128)(2,1)S(1)}, u32[]{:S(2)}, u32[]{:S(2)}) collective-permute-start(bf16[4,128,256]{2,1,0:T(8,128)(2,1)S(1)} %slice.27), channel_id=1, source_target_pairs={{0,480},{32,64},{64,32},{96,128},{128,96},{160,192},{192,160},{224... | collective-permute-start | bytes 786440 | tf_op jit(solution)/shard_map/ppermute | solution.py:136
  119.6 8.5 %collective-permute-start.2 = (bf16[4,128,256]{2,1,0:T(8,128)(2,1)S(1)}, bf16[4,128,256]{2,1,0:T(8,128)(2,1)S(1)}, u32[]{:S(2)}, u32[]{:S(2)}) collective-permute-start(bf16[4,128,256]{2,1,0:T(8,128)(2,1)S(1)} %slice.24), channel_id=1, source_target_pairs={{0,32},{32,0},{64,96},{96,64},{128,160},{160,128},{192,224},{224,1... | collective-permute-start | bytes 786440 | tf_op jit(solution)/shard_map/ppermute | solution.py:135
  121.8 11.9 %collective-permute-start.4 = (bf16[4,128,256]{2,1,0:T(8,128)(2,1)S(1)}, bf16[4,128,256]{2,1,0:T(8,128)(2,1)S(1)}, u32[]{:S(2)}, u32[]{:S(2)}) collective-permute-start(bf16[4,128,256]{2,1,0:T(8,128)(2,1)S(1)} %add_convert_fusion.1), channel_id=1, source_target_pairs={{0,32},{32,0},{64,96},{96,64},{128,160},{160,128},{192,224},{224,1... | collective-permute-start | bytes 786440 | tf_op jit(solution)/shard_map/ppermute | solution.py:138
  125.0 9.2 %collective-permute-start.6 = (bf16[4,128,256]{2,1,0:T(8,128)(2,1)S(1)}, bf16[4,128,256]{2,1,0:T(8,128)(2,1)S(1)}, u32[]{:S(2)}, u32[]{:S(2)}) collective-permute-start(bf16[4,128,256]{2,1,0:T(8,128)(2,1)S(1)} %add_convert_fusion), channel_id=1, source_target_pairs={{0,480},{32,64},{64,32},{96,128},{128,96},{160,192},{192,160},{224... | collective-permute-start | bytes 786440 | tf_op jit(solution)/shard_map/ppermute | solution.py:137
  133.8 43.4 %copy-start.1 = (bf16[256,256]{1,0:T(8,128)(2,1)S(1)}, bf16[256,256]{1,0:T(8,128)(2,1)}, u32[]{:S(2)}) copy-start(bf16[256,256]{1,0:T(8,128)(2,1)} %state_ref.3) | copy-start | bytes 393220
  133.8 43.4 %copy-start.5 = (bf16[256,256]{1,0:T(8,128)(2,1)S(1)}, bf16[256,256]{1,0:T(8,128)(2,1)}, u32[]{:S(2)}) copy-start(bf16[256,256]{1,0:T(8,128)(2,1)} %agg_ref.3) | copy-start | bytes 393220
  133.8 43.4 %copy-start.6 = (bf16[256,256]{1,0:T(8,128)(2,1)S(1)}, bf16[256,256]{1,0:T(8,128)(2,1)}, u32[]{:S(2)}) copy-start(bf16[256,256]{1,0:T(8,128)(2,1)} %self_ref.3) | copy-start | bytes 393220
  133.8 43.4 %copy-start.7 = (bf16[256,256]{1,0:T(8,128)(2,1)S(1)}, bf16[256,256]{1,0:T(8,128)(2,1)}, u32[]{:S(2)}) copy-start(bf16[256,256]{1,0:T(8,128)(2,1)} %out_w_ref.3) | copy-start | bytes 393220
  133.8 43.4 %copy-start.13 = (f32[256]{0:T(256)S(1)}, f32[256]{0:T(256)}, u32[]{:S(2)}) copy-start(f32[256]{0:T(256)} %param.24) | copy-start | bytes 3076
  135.0 18.4 %collective-permute-start.9 = (bf16[1,128,256]{2,1,0:T(8,128)(2,1)S(1)}, bf16[1,128,256]{2,1,0:T(8,128)(2,1)S(1)}, u32[]{:S(2)}, u32[]{:S(2)}) collective-permute-start(bf16[1,128,256]{2,1,0:T(8,128)(2,1)S(1)} %get-tuple-element.27), channel_id=1, source_target_pairs={{0,384},{32,416},{64,448},{96,480},{128,256},{160,288},{192,320},{... | collective-permute-start | bytes 196616 | tf_op jit(solution)/shard_map/ppermute | solution.py:134
  140.5 30.8 %collective-permute-start.13 = (bf16[1,128,256]{2,1,0:T(8,128)(2,1)S(1)}, bf16[1,128,256]{2,1,0:T(8,128)(2,1)S(1)}, u32[]{:S(2)}, u32[]{:S(2)}) collective-permute-start(bf16[1,128,256]{2,1,0:T(8,128)(2,1)S(1)} %slice.31), channel_id=1, source_target_pairs={{0,384},{32,416},{64,448},{96,480},{128,256},{160,288},{192,320},{... | collective-permute-start | bytes 196616 | tf_op jit(solution)/shard_map/ppermute | solution.py:136
  144.2 26.9 %collective-permute-start.8 = (bf16[1,128,256]{2,1,0:T(8,128)(2,1)S(1)}, bf16[1,128,256]{2,1,0:T(8,128)(2,1)S(1)}, u32[]{:S(2)}, u32[]{:S(2)}) collective-permute-start(bf16[1,128,256]{2,1,0:T(8,128)(2,1)S(1)} %slice.28), channel_id=1, source_target_pairs={{0,128},{32,160},{64,192},{96,224},{128,0},{160,32},{192,64},{224,... | collective-permute-start | bytes 196616 | tf_op jit(solution)/shard_map/ppermute | solution.py:135
  148.4 19.8 %collective-permute-start.11 = (bf16[1,128,256]{2,1,0:T(8,128)(2,1)S(1)}, bf16[1,128,256]{2,1,0:T(8,128)(2,1)S(1)}, u32[]{:S(2)}, u32[]{:S(2)}) collective-permute-start(bf16[1,128,256]{2,1,0:T(8,128)(2,1)S(1)} %get-tuple-element.29), channel_id=1, source_target_pairs={{0,128},{32,160},{64,192},{96,224},{128,0},{160,32},{192,64},{224,... | collective-permute-start | bytes 196616 | tf_op jit(solution)/shard_map/ppermute | solution.py:133
  153.5 17.7 %collective-permute-start.10 = (bf16[1,128,256]{2,1,0:T(8,128)(2,1)S(1)}, bf16[1,128,256]{2,1,0:T(8,128)(2,1)S(1)}, u32[]{:S(2)}, u32[]{:S(2)}) collective-permute-start(bf16[1,128,256]{2,1,0:T(8,128)(2,1)S(1)} %add_convert_fusion.3), channel_id=1, source_target_pairs={{0,128},{32,160},{64,192},{96,224},{128,0},{160,32},{192,64},{224,... | collective-permute-start | bytes 196616 | tf_op jit(solution)/shard_map/ppermute | solution.py:138
  168.2 8.9 %collective-permute-start.12 = (bf16[1,128,256]{2,1,0:T(8,128)(2,1)S(1)}, bf16[1,128,256]{2,1,0:T(8,128)(2,1)S(1)}, u32[]{:S(2)}, u32[]{:S(2)}) collective-permute-start(bf16[1,128,256]{2,1,0:T(8,128)(2,1)S(1)} %add_convert_fusion.2), channel_id=1, source_target_pairs={{0,384},{32,416},{64,448},{96,480},{128,256},{160,288},{192,320},{... | collective-permute-start | bytes 196616 | tf_op jit(solution)/shard_map/ppermute | solution.py:137

commit v6 on v3

--- a/solution.py
+++ b/solution.py
@@ -49,24 +49,25 @@
     )(me, flow, link, live, coefs, pieces)
 
 
+ROW_ORDER = (0, 5, -5, 2, 7, -3, -2, -7, 3, 1, 6, -4, -1, -6, 4, 8)
+
+
 def flow_products_kernel(
     me_ref, flow_ref, link_ref, live_ref, coefs_ref, own_ref, other_ref, *rest
 ):
-    *out_refs, acc_ref, pieces_ref = rest
+    *out_refs, acc_ref, pieces_ref, order_ref = rest
     blocks = acc_ref.shape[0] - 1
     rows = blocks // 2
     half = own_ref.shape[0]
+    for place, ahead in enumerate(ROW_ORDER):
+        order_ref[ahead % rows] = 2 * place
     pieces_ref[:half] = own_ref[...]
     pieces_ref[half:] = other_ref[...]
     acc_ref[...] = jnp.zeros_like(acc_ref)
     for slot in range(coefs_ref.shape[0]):
         block = flow_ref[0, 0, slot]
-        ahead = (block // 2 - me_ref[0] + rows) % rows
-        upward = ahead < rows // 2
-        steps = jnp.where(upward, ahead, (rows - ahead) % (rows // 2))
-        odd = me_ref[0] % 2
-        second = jnp.where(steps == 0, jnp.where(ahead == 0, 0, 1), jnp.where(upward, odd, 1 - odd))
-        place = second * rows + steps * 2 + block % 2
+        ahead = jnp.where(me_ref[0] % 2 == 0, block // 2 - me_ref[0], me_ref[0] - block // 2)
+        place = order_ref[(ahead + rows) % rows] + block % 2
         place = jnp.where(live_ref[0, 0, slot] == 1, place, blocks)
         piece = link_ref[0, 0, slot]
         piece = ((piece + me_ref[1]) % 2) * half + piece // 2
@@ -81,43 +82,51 @@
 
 
 def flow_products(me, flow, link, live, coefs, own, other, blocks):
-    row = jax.ShapeDtypeStruct((2, BS, H), BF16)
-    half_row = jax.ShapeDtypeStruct((1, BS, H), BF16)
-    shapes = [row] * (blocks // 4) + [half_row] * 2 + [row] * (blocks // 4 - 1)
-    outs = pl.pallas_call(
+    assert blocks == 2 * len(ROW_ORDER)
+    counts = [6] * 5 + [1, 1]
+    return pl.pallas_call(
         flow_products_kernel,
-        out_shape=shapes,
+        out_shape=[jax.ShapeDtypeStruct((count, BS, H), BF16) for count in counts],
         in_specs=[SMEM, SMEM, SMEM, SMEM, VMEM, VMEM, VMEM],
-        out_specs=[VMEM] * len(shapes),
+        out_specs=[VMEM] * len(counts),
         scratch_shapes=[
             pltpu.VMEM((blocks + 1, BS, H), F32),
             pltpu.VMEM((2 * own.shape[0], BS, H), BF16),
+            pltpu.SMEM((len(ROW_ORDER),), jnp.int32),
         ],
         compiler_params=PARAMS,
         name="flow_products",
     )(me, flow, link, live, coefs, own, other)
-    side = blocks // 4
-    return outs[0], outs[1:side], outs[side], outs[side + 1], outs[side + 2 :]
-
-
-def add(a, b):
-    return (a.astype(F32) + b.astype(F32)).astype(BF16)
-
-
-def sum_over_rows(mine, for_a, half_a, half_b, for_b, rows):
-    swap_a = [(i, i ^ 1) for i in range(rows)]
-    swap_b = [(i, ((i - 1) ^ 1) + 1 if i % rows else rows - 1) for i in range(rows)]
-    swap_b = [(i, j % rows) for i, j in swap_b]
-    got_a = lax.ppermute(half_a, "row", swap_a)
-    got_b = lax.ppermute(half_b, "row", swap_b)
-    a = jnp.concatenate([for_a[-1][:1], add(for_a[-1][1:], got_b)], axis=0)
-    b = jnp.concatenate([add(for_b[-1][:1], got_a), for_b[-1][1:]], axis=0)
-    for step in range(len(for_a) - 2, -2, -1):
-        got_a = lax.ppermute(a, "row", swap_a)
-        got_b = lax.ppermute(b, "row", swap_b)
-        if step >= 0:
-            b = add(for_b[step], got_a)
-            a = add(for_a[step], got_b)
+
+
+def add(*terms):
+    total = terms[0].astype(F32)
+    for term in terms[1:]:
+        total = total + term.astype(F32)
+    return total.astype(BF16)
+
+
+def sum_over_rows(own, two_a, two_b, one_a, one_b, opposite_a, opposite_b, rows):
+    def swap_a(x, step):
+        pairs = [(i, (i + step if i % 2 == 0 else i - step) % rows) for i in range(rows)]
+        return lax.ppermute(x, "row", pairs)
+
+    def swap_b(x, step):
+        pairs = [(i, (i - step if i % 2 == 0 else i + step) % rows) for i in range(rows)]
+        return lax.ppermute(x, "row", pairs)
+
+    got_a, got_b = swap_a(two_a, 1), swap_b(two_b, 1)
+    from_a, from_b = swap_a(opposite_a, 3), swap_b(opposite_b, 3)
+    one_b, one_a = add(one_b, got_a), add(one_a, got_b)
+    got_a, got_b = swap_a(one_a, 1), swap_b(one_b, 1)
+    mine = add(own[:2], got_a[:2], got_b[:2])
+    far_a = jnp.concatenate(
+        [add(own[2:3], got_a[4:5], got_b[2:3]), add(own[3:4], got_a[5:6], got_b[3:4], from_b)], axis=0
+    )
+    far_b = jnp.concatenate(
+        [add(own[4:5], got_a[2:3], got_b[4:5], from_a), add(own[5:6], got_a[3:4], got_b[5:6])], axis=0
+    )
+    got_a, got_b = swap_a(far_a, 5), swap_b(far_b, 5)
     return jnp.stack([x.reshape(2 * BS, H) for x in (mine, got_a, got_b)])
 
 
@@ -205,10 +214,10 @@
     )
     own = lax.all_to_all(link_copies, "col", 0, 0, tiled=True, axis_index_groups=same_core)
     other = lax.ppermute(own, "col", sibling)
-    mine, for_a, half_a, half_b, for_b = flow_products(
+    parts = flow_products(
         me, tile_flow, tile_link, tile_live, coefs, own, other, flow_blocks
     )
-    flow_parts = sum_over_rows(mine, for_a, half_a, half_b, for_b, rows)
+    flow_parts = sum_over_rows(*parts, rows)
     (flow_next,) = update(
         flow_parts, flow_state, flow_gain, flow_agg_weight, flow_self_weight, flow_out_weight, 0
     )

time: 174 us -> 168 us (0.966)
  the two profiles are of different devices: /device:TPU:2 before, /device:TPU:32 now
where the time goes in v6:
time: 168 us; the launch traced here: 167 us
  blocking collectives  91.6 us (55%)
  starting transfers between devices  39.4 us (23%)
  waiting for transfers between devices  27.1 us (16%)
  Pallas kernels  5.85 us (3%)
  other arithmetic  2.04 us (1%)
    all_gather x1, blocking collectives, gather_rows(): got = lax.all_gather(sent, 'row', axis=0, tiled=True)  47.7 us
    all_to_all x1, blocking collectives, on_device(): lax.all_to_all(own, 'col', 0, 0, tiled=True, axis_index_groups=same_core)  24.3 us
    ppermute x4, starting transfers between devices, swap_a(): return lax.ppermute(x, 'row', pairs)  22.2 us
    all_to_all x1, blocking collectives, on_device(): lax.all_to_all(link_copies, 'col', 0, 0, tiled=True, axis_index_groups=sa...  19.6 us
    ppermute x4, starting transfers between devices, swap_b(): return lax.ppermute(x, 'row', pairs)  13.4 us
    ppermute x4, waiting for transfers between devices, swap_a(): return lax.ppermute(x, 'row', pairs)  11.6 us
    ppermute x4, waiting for transfers between devices, swap_b(): return lax.ppermute(x, 'row', pairs)  10.2 us
  transfers between devices with their start and end apart: 10, of which 8 were waited for; matrix products, arithmetic and copies ran while one was open for 0% of the time, Pallas kernels for 0%

profile of v6, /device:TPU:32, one launch (start us, length us, event | category | flops | bytes accessed | tf_op | source)
XLA Modules:
  0.0 167.4 jit_solution(7417166275509289142)
XLA Ops:
  0.6 0.9 multiply_convert_fusion.1
  1.6 47.7 %all-gather.1 = f16[4096,256]{1,0:T(8,128)(2,1)S(1)} all-gather(f16[256,256]{1,0:T(8,128)(2,1)S(1)} %multiply_convert_fusion.1), channel_id=1, replica_groups=mesh['row'=16,'col'=32] {'row'}, dimensions={0}, use_global_device_ids=true | all-gather | bytes 2228224 | tf_op jit(solution)/shard_map/all_gather | solution.py:229
  49.3 0.6 multiply_convert_fusion
  50.0 0.5 copy-done
  50.4 1.6 link_products.1
  52.0 1.9 %collective-permute-start = (bf16[16,128,256]{2,1,0:T(8,128)(2,1)S(1)}, bf16[16,128,256]{2,1,0:T(8,128)(2,1)S(1)}, u32[]{:S(2)}, u32[]{:S(2)}) collective-permute-start(bf16[16,128,256]{2,1,0:T(8,128)(2,1)S(1)} %get-tuple-element.14), channel_id=1, source_target_pairs={{0,1},{1,0},{2,3},{3,2},{4,5},{5,4},{6,7},{7,6},{8,9},{9,8},{10,11... | collective-permute-start | bytes 3145736 | tf_op jit(solution)/shard_map/ppermute | solution.py:210
  54.0 2.6 %collective-permute-done.b_ref = bf16[16,128,256]{2,1,0:T(8,128)(2,1)S(1)} collective-permute-done((bf16[16,128,256]{2,1,0:T(8,128)(2,1)S(1)}, bf16[16,128,256]{2,1,0:T(8,128)(2,1)S(1)}, u32[]{:S(2)}, u32[]{:S(2)}) %collective-permute-start) | collective-permute-done | bytes 1048608 | tf_op jit(solution)/shard_map/ppermute | solution.py:210
  56.6 0.2 add_two.1
  56.9 24.3 %all_to_all.10.parts_ref = bf16[16,128,256]{2,1,0:T(8,128)(2,1)S(1)} all-to-all(bf16[16,128,256]{2,1,0:T(8,128)(2,1)S(1)} %add_two.1), channel_id=1, replica_groups={{0,2,4,6,8,10,12,14,16,18,20,22,24,26,28,30},{1,3,5,7,9,11,13,15,17,19,..., dimensions={0} | all-to-all | bytes 2097152 | tf_op jit(solution)/shard_map/all_to_all | solution.py:211
  81.2 1.2 link_update.1
  82.3 19.6 %all_to_all.11.own_ref = bf16[16,128,256]{2,1,0:T(8,128)(2,1)S(1)} all-to-all(bf16[16,128,256]{2,1,0:T(8,128)(2,1)S(1)} %get-tuple-element.16), channel_id=1, replica_groups={{0,2,4,6,8,10,12,14,16,18,20,22,24,26,28,30},{1,3,5,7,9,11,13,15,17,19,..., dimensions={0} | all-to-all | bytes 2097152 | tf_op jit(solution)/shard_map/all_to_all | solution.py:215
  101.9 1.9 %collective-permute-start.1 = (bf16[16,128,256]{2,1,0:T(8,128)(2,1)S(1)}, bf16[16,128,256]{2,1,0:T(8,128)(2,1)S(1)}, u32[]{:S(2)}, u32[]{:S(2)}) collective-permute-start(bf16[16,128,256]{2,1,0:T(8,128)(2,1)S(1)} %all_to_all.11.own_ref), channel_id=1, source_target_pairs={{0,1},{1,0},{2,3},{3,2},{4,5},{5,4},{6,7},{7,6},{8,9},{9,8},{10,11... | collective-permute-start | bytes 3145736 | tf_op jit(solution)/shard_map/ppermute | solution.py:216
  103.8 2.6 %collective-permute-done.1.other_ref = bf16[16,128,256]{2,1,0:T(8,128)(2,1)S(1)} collective-permute-done((bf16[16,128,256]{2,1,0:T(8,128)(2,1)S(1)}, bf16[16,128,256]{2,1,0:T(8,128)(2,1)S(1)}, u32[]{:S(2)}, u32[]{:S(2)}) %collective-permute-start.1) | collective-permute-done | bytes 1048608 | tf_op jit(solution)/shard_map/ppermute | solution.py:216
  106.5 1.8 %flow_products.1 = (bf16[6,128,256]{2,1,0:T(8,128)(2,1)S(1)}, bf16[6,128,256]{2,1,0:T(8,128)(2,1)S(1)}, bf16[6,128,256]{2,1,0:T(8,128)(2,1)S(1)}, bf16[6,128,256...) custom-call(s32[2]{0:T(128)S(1)} %pad_add_fusion.me_ref, ...), custom_call_target="tpu_custom_call" | custom-call | tf_op jit(solution)/shard_map/flow_products/pallas_call | solution.py:87
  108.3 2.4 %collective-permute-start.2 = (bf16[6,128,256]{2,1,0:T(8,128)(2,1)S(1)}, bf16[6,128,256]{2,1,0:T(8,128)(2,1)S(1)}, u32[]{:S(2)}, u32[]{:S(2)}) collective-permute-start(bf16[6,128,256]{2,1,0:T(8,128)(2,1)S(1)} %get-tuple-element.19), channel_id=1, source_target_pairs={{0,480},{32,64},{64,32},{96,128},{128,96},{160,192},{192,160},{224... | collective-permute-start | bytes 1179656 | tf_op jit(solution)/shard_map/ppermute | solution.py:116
  110.7 3.4 %collective-permute-start.4 = (bf16[6,128,256]{2,1,0:T(8,128)(2,1)S(1)}, bf16[6,128,256]{2,1,0:T(8,128)(2,1)S(1)}, u32[]{:S(2)}, u32[]{:S(2)}) collective-permute-start(bf16[6,128,256]{2,1,0:T(8,128)(2,1)S(1)} %get-tuple-element.21), channel_id=1, source_target_pairs={{0,32},{32,0},{64,96},{96,64},{128,160},{160,128},{192,224},{224,1... | collective-permute-start | bytes 1179656 | tf_op jit(solution)/shard_map/ppermute | solution.py:112
  114.1 7.2 %collective-permute-done.2 = bf16[6,128,256]{2,1,0:T(8,128)(2,1)S(1)} collective-permute-done((bf16[6,128,256]{2,1,0:T(8,128)(2,1)S(1)}, bf16[6,128,256]{2,1,0:T(8,128)(2,1)S(1)}, u32[]{:S(2)}, u32[]{:S(2)}) %collective-permute-start.2) | collective-permute-done | bytes 393248 | tf_op jit(solution)/shard_map/ppermute | solution.py:116
  121.3 0.1 add_convert_fusion.1
  121.4 4.8 %collective-permute-start.3 = (bf16[6,128,256]{2,1,0:T(8,128)(2,1)S(1)}, bf16[6,128,256]{2,1,0:T(8,128)(2,1)S(1)}, u32[]{:S(2)}, u32[]{:S(2)}) collective-permute-start(bf16[6,128,256]{2,1,0:T(8,128)(2,1)S(1)} %add_convert_fusion.1), channel_id=1, source_target_pairs={{0,32},{32,0},{64,96},{96,64},{128,160},{160,128},{192,224},{224,1... | collective-permute-start | bytes 1179656 | tf_op jit(solution)/shard_map/ppermute | solution.py:112
  126.3 0.1 add_convert_fusion
  126.4 2.1 %collective-permute-start.5 = (bf16[6,128,256]{2,1,0:T(8,128)(2,1)S(1)}, bf16[6,128,256]{2,1,0:T(8,128)(2,1)S(1)}, u32[]{:S(2)}, u32[]{:S(2)}) collective-permute-start(bf16[6,128,256]{2,1,0:T(8,128)(2,1)S(1)} %add_convert_fusion), channel_id=1, source_target_pairs={{0,480},{32,64},{64,32},{96,128},{128,96},{160,192},{192,160},{224... | collective-permute-start | bytes 1179656 | tf_op jit(solution)/shard_map/ppermute | solution.py:116
  128.5 3.9 %collective-permute-start.6 = (bf16[1,128,256]{2,1,0:T(8,128)(2,1)S(1)}, bf16[1,128,256]{2,1,0:T(8,128)(2,1)S(1)}, u32[]{:S(2)}, u32[]{:S(2)}) collective-permute-start(bf16[1,128,256]{2,1,0:T(8,128)(2,1)S(1)} %get-tuple-element.22), channel_id=1, source_target_pairs={{0,416},{32,128},{64,480},{96,192},{128,32},{160,256},{192,96},{22... | collective-permute-start | bytes 196616 | tf_op jit(solution)/shard_map/ppermute | solution.py:116
  132.4 6.2 %collective-permute-start.8 = (bf16[1,128,256]{2,1,0:T(8,128)(2,1)S(1)}, bf16[1,128,256]{2,1,0:T(8,128)(2,1)S(1)}, u32[]{:S(2)}, u32[]{:S(2)}) collective-permute-start(bf16[1,128,256]{2,1,0:T(8,128)(2,1)S(1)} %get-tuple-element.23), channel_id=1, source_target_pairs={{0,96},{32,448},{64,160},{96,0},{128,224},{160,64},{192,288},{224,... | collective-permute-start | bytes 196616 | tf_op jit(solution)/shard_map/ppermute | solution.py:112
  138.6 2.3 %collective-permute-done.6 = bf16[1,128,256]{2,1,0:T(8,128)(2,1)S(1)} collective-permute-done((bf16[1,128,256]{2,1,0:T(8,128)(2,1)S(1)}, bf16[1,128,256]{2,1,0:T(8,128)(2,1)S(1)}, u32[]{:S(2)}, u32[]{:S(2)}) %collective-permute-start.6) | collective-permute-done | bytes 65568 | tf_op jit(solution)/shard_map/ppermute | solution.py:116
  140.9 0.9 collective-permute-done.8
  141.8 0.3 collective-permute-done.5
  142.0 0.1 add_convert_fusion.6
  142.2 5.1 %collective-permute-start.9 = (bf16[2,128,256]{2,1,0:T(8,128)(2,1)S(1)}, bf16[2,128,256]{2,1,0:T(8,128)(2,1)S(1)}, u32[]{:S(2)}, u32[]{:S(2)}) collective-permute-start(bf16[2,128,256]{2,1,0:T(8,128)(2,1)S(1)} %pad_maximum_fusion.2), channel_id=1, source_target_pairs={{0,352},{32,192},{64,416},{96,256},{128,480},{160,320},{192,32},{2... | collective-permute-start | bytes 393224 | tf_op jit(solution)/shard_map/ppermute | solution.py:116
  147.3 7.8 %collective-permute-start.7 = (bf16[2,128,256]{2,1,0:T(8,128)(2,1)S(1)}, bf16[2,128,256]{2,1,0:T(8,128)(2,1)S(1)}, u32[]{:S(2)}, u32[]{:S(2)}) collective-permute-start(bf16[2,128,256]{2,1,0:T(8,128)(2,1)S(1)} %pad_maximum_fusion.1), channel_id=1, source_target_pairs={{0,160},{32,384},{64,224},{96,448},{128,288},{160,0},{192,352},{22... | collective-permute-start | bytes 393224 | tf_op jit(solution)/shard_map/ppermute | solution.py:112
  155.2 0.4 collective-permute-done.9
  155.6 10.7 %collective-permute-done.7 = bf16[2,128,256]{2,1,0:T(8,128)(2,1)S(1)} collective-permute-done((bf16[2,128,256]{2,1,0:T(8,128)(2,1)S(1)}, bf16[2,128,256]{2,1,0:T(8,128)(2,1)S(1)}, u32[]{:S(2)}, u32[]{:S(2)}) %collective-permute-start.7) | collective-permute-done | bytes 131104 | tf_op jit(solution)/shard_map/ppermute | solution.py:112
  166.4 1.1 flow_update.1
  (34 shorter events, 0.3 us)
Async XLA Ops:
  49.3 1.1 copy-start
  49.3 1.1 copy-start.9
  49.3 1.1 copy-start.10
  49.3 1.1 copy-start.11
  52.0 4.6 %collective-permute-start = (bf16[16,128,256]{2,1,0:T(8,128)(2,1)S(1)}, bf16[16,128,256]{2,1,0:T(8,128)(2,1)S(1)}, u32[]{:S(2)}, u32[]{:S(2)}) collective-permute-start(bf16[16,128,256]{2,1,0:T(8,128)(2,1)S(1)} %get-tuple-element.14), channel_id=1, source_target_pairs={{0,1},{1,0},{2,3},{3,2},{4,5},{5,4},{6,7},{7,6},{8,9},{9,8},{10,11... | collective-permute-start | bytes 3145736 | tf_op jit(solution)/shard_map/ppermute | solution.py:210
  56.6 24.6 %copy-start.2 = (bf16[256,256]{1,0:T(8,128)(2,1)S(1)}, bf16[256,256]{1,0:T(8,128)(2,1)}, u32[]{:S(2)}) copy-start(bf16[256,256]{1,0:T(8,128)(2,1)} %agg_ref.2) | copy-start | bytes 393220
  56.6 24.6 %copy-start.3 = (bf16[256,256]{1,0:T(8,128)(2,1)S(1)}, bf16[256,256]{1,0:T(8,128)(2,1)}, u32[]{:S(2)}) copy-start(bf16[256,256]{1,0:T(8,128)(2,1)} %self_ref.2) | copy-start | bytes 393220
  56.6 24.6 %copy-start.4 = (bf16[256,256]{1,0:T(8,128)(2,1)S(1)}, bf16[256,256]{1,0:T(8,128)(2,1)}, u32[]{:S(2)}) copy-start(bf16[256,256]{1,0:T(8,128)(2,1)} %out_w_ref.2) | copy-start | bytes 393220
  56.6 24.6 %copy-start.8 = (bf16[128,256]{1,0:T(8,128)(2,1)S(1)}, bf16[128,256]{1,0:T(8,128)(2,1)}, u32[]{:S(2)}) copy-start(bf16[128,256]{1,0:T(8,128)(2,1)} %state_ref.2) | copy-start | bytes 196612
  56.6 24.6 %copy-start.12 = (f32[256]{0:T(256)S(1)}, f32[256]{0:T(256)}, u32[]{:S(2)}) copy-start(f32[256]{0:T(256)} %param.20) | copy-start | bytes 3076
  101.9 4.5 %collective-permute-start.1 = (bf16[16,128,256]{2,1,0:T(8,128)(2,1)S(1)}, bf16[16,128,256]{2,1,0:T(8,128)(2,1)S(1)}, u32[]{:S(2)}, u32[]{:S(2)}) collective-permute-start(bf16[16,128,256]{2,1,0:T(8,128)(2,1)S(1)} %all_to_all.11.own_ref), channel_id=1, source_target_pairs={{0,1},{1,0},{2,3},{3,2},{4,5},{5,4},{6,7},{7,6},{8,9},{9,8},{10,11... | collective-permute-start | bytes 3145736 | tf_op jit(solution)/shard_map/ppermute | solution.py:216
  108.3 13.1 %collective-permute-start.2 = (bf16[6,128,256]{2,1,0:T(8,128)(2,1)S(1)}, bf16[6,128,256]{2,1,0:T(8,128)(2,1)S(1)}, u32[]{:S(2)}, u32[]{:S(2)}) collective-permute-start(bf16[6,128,256]{2,1,0:T(8,128)(2,1)S(1)} %get-tuple-element.19), channel_id=1, source_target_pairs={{0,480},{32,64},{64,32},{96,128},{128,96},{160,192},{192,160},{224... | collective-permute-start | bytes 1179656 | tf_op jit(solution)/shard_map/ppermute | solution.py:116
  110.7 15.6 %collective-permute-start.4 = (bf16[6,128,256]{2,1,0:T(8,128)(2,1)S(1)}, bf16[6,128,256]{2,1,0:T(8,128)(2,1)S(1)}, u32[]{:S(2)}, u32[]{:S(2)}) collective-permute-start(bf16[6,128,256]{2,1,0:T(8,128)(2,1)S(1)} %get-tuple-element.21), channel_id=1, source_target_pairs={{0,32},{32,0},{64,96},{96,64},{128,160},{160,128},{192,224},{224,1... | collective-permute-start | bytes 1179656 | tf_op jit(solution)/shard_map/ppermute | solution.py:112
  121.4 20.4 %collective-permute-start.3 = (bf16[6,128,256]{2,1,0:T(8,128)(2,1)S(1)}, bf16[6,128,256]{2,1,0:T(8,128)(2,1)S(1)}, u32[]{:S(2)}, u32[]{:S(2)}) collective-permute-start(bf16[6,128,256]{2,1,0:T(8,128)(2,1)S(1)} %add_convert_fusion.1), channel_id=1, source_target_pairs={{0,32},{32,0},{64,96},{96,64},{128,160},{160,128},{192,224},{224,1... | collective-permute-start | bytes 1179656 | tf_op jit(solution)/shard_map/ppermute | solution.py:112
  126.3 40.0 %copy-start.1 = (bf16[256,256]{1,0:T(8,128)(2,1)S(1)}, bf16[256,256]{1,0:T(8,128)(2,1)}, u32[]{:S(2)}) copy-start(bf16[256,256]{1,0:T(8,128)(2,1)} %state_ref.3) | copy-start | bytes 393220
  126.3 40.0 %copy-start.5 = (bf16[256,256]{1,0:T(8,128)(2,1)S(1)}, bf16[256,256]{1,0:T(8,128)(2,1)}, u32[]{:S(2)}) copy-start(bf16[256,256]{1,0:T(8,128)(2,1)} %agg_ref.3) | copy-start | bytes 393220
  126.3 40.0 %copy-start.6 = (bf16[256,256]{1,0:T(8,128)(2,1)S(1)}, bf16[256,256]{1,0:T(8,128)(2,1)}, u32[]{:S(2)}) copy-start(bf16[256,256]{1,0:T(8,128)(2,1)} %self_ref.3) | copy-start | bytes 393220
  126.3 40.0 %copy-start.7 = (bf16[256,256]{1,0:T(8,128)(2,1)S(1)}, bf16[256,256]{1,0:T(8,128)(2,1)}, u32[]{:S(2)}) copy-start(bf16[256,256]{1,0:T(8,128)(2,1)} %out_w_ref.3) | copy-start | bytes 393220
  126.3 40.0 %copy-start.13 = (f32[256]{0:T(256)S(1)}, f32[256]{0:T(256)}, u32[]{:S(2)}) copy-start(f32[256]{0:T(256)} %param.24) | copy-start | bytes 3076
  126.4 15.6 %collective-permute-start.5 = (bf16[6,128,256]{2,1,0:T(8,128)(2,1)S(1)}, bf16[6,128,256]{2,1,0:T(8,128)(2,1)S(1)}, u32[]{:S(2)}, u32[]{:S(2)}) collective-permute-start(bf16[6,128,256]{2,1,0:T(8,128)(2,1)S(1)} %add_convert_fusion), channel_id=1, source_target_pairs={{0,480},{32,64},{64,32},{96,128},{128,96},{160,192},{192,160},{224... | collective-permute-start | bytes 1179656 | tf_op jit(solution)/shard_map/ppermute | solution.py:116
  128.5 12.4 %collective-permute-start.6 = (bf16[1,128,256]{2,1,0:T(8,128)(2,1)S(1)}, bf16[1,128,256]{2,1,0:T(8,128)(2,1)S(1)}, u32[]{:S(2)}, u32[]{:S(2)}) collective-permute-start(bf16[1,128,256]{2,1,0:T(8,128)(2,1)S(1)} %get-tuple-element.22), channel_id=1, source_target_pairs={{0,416},{32,128},{64,480},{96,192},{128,32},{160,256},{192,96},{22... | collective-permute-start | bytes 196616 | tf_op jit(solution)/shard_map/ppermute | solution.py:116
  132.4 9.4 %collective-permute-start.8 = (bf16[1,128,256]{2,1,0:T(8,128)(2,1)S(1)}, bf16[1,128,256]{2,1,0:T(8,128)(2,1)S(1)}, u32[]{:S(2)}, u32[]{:S(2)}) collective-permute-start(bf16[1,128,256]{2,1,0:T(8,128)(2,1)S(1)} %get-tuple-element.23), channel_id=1, source_target_pairs={{0,96},{32,448},{64,160},{96,0},{128,224},{160,64},{192,288},{224,... | collective-permute-start | bytes 196616 | tf_op jit(solution)/shard_map/ppermute | solution.py:112
  142.2 13.4 %collective-permute-start.9 = (bf16[2,128,256]{2,1,0:T(8,128)(2,1)S(1)}, bf16[2,128,256]{2,1,0:T(8,128)(2,1)S(1)}, u32[]{:S(2)}, u32[]{:S(2)}) collective-permute-start(bf16[2,128,256]{2,1,0:T(8,128)(2,1)S(1)} %pad_maximum_fusion.2), channel_id=1, source_target_pairs={{0,352},{32,192},{64,416},{96,256},{128,480},{160,320},{192,32},{2... | collective-permute-start | bytes 393224 | tf_op jit(solution)/shard_map/ppermute | solution.py:116
  147.3 19.0 %collective-permute-start.7 = (bf16[2,128,256]{2,1,0:T(8,128)(2,1)S(1)}, bf16[2,128,256]{2,1,0:T(8,128)(2,1)S(1)}, u32[]{:S(2)}, u32[]{:S(2)}) collective-permute-start(bf16[2,128,256]{2,1,0:T(8,128)(2,1)S(1)} %pad_maximum_fusion.1), channel_id=1, source_target_pairs={{0,160},{32,384},{64,224},{96,448},{128,288},{160,0},{192,352},{22... | collective-permute-start | bytes 393224 | tf_op jit(solution)/shard_map/ppermute | solution.py:112

commit v7 on v6

--- a/solution.py
+++ b/solution.py
@@ -83,7 +83,7 @@
 
 def flow_products(me, flow, link, live, coefs, own, other, blocks):
     assert blocks == 2 * len(ROW_ORDER)
-    counts = [6] * 5 + [1, 1]
+    counts = [6] * 5 + [2]
     return pl.pallas_call(
         flow_products_kernel,
         out_shape=[jax.ShapeDtypeStruct((count, BS, H), BF16) for count in counts],
@@ -106,7 +106,7 @@
     return total.astype(BF16)
 
 
-def sum_over_rows(own, two_a, two_b, one_a, one_b, opposite_a, opposite_b, rows):
+def sum_over_rows(own, two_a, two_b, one_a, one_b, opposite, rows):
     def swap_a(x, step):
         pairs = [(i, (i + step if i % 2 == 0 else i - step) % rows) for i in range(rows)]
         return lax.ppermute(x, "row", pairs)
@@ -116,16 +116,13 @@
         return lax.ppermute(x, "row", pairs)
 
     got_a, got_b = swap_a(two_a, 1), swap_b(two_b, 1)
-    from_a, from_b = swap_a(opposite_a, 3), swap_b(opposite_b, 3)
+    opposite = swap_a(opposite, 3)
+    got_a, got_b, opposite = lax.optimization_barrier((got_a, got_b, opposite))
     one_b, one_a = add(one_b, got_a), add(one_a, got_b)
     got_a, got_b = swap_a(one_a, 1), swap_b(one_b, 1)
     mine = add(own[:2], got_a[:2], got_b[:2])
-    far_a = jnp.concatenate(
-        [add(own[2:3], got_a[4:5], got_b[2:3]), add(own[3:4], got_a[5:6], got_b[3:4], from_b)], axis=0
-    )
-    far_b = jnp.concatenate(
-        [add(own[4:5], got_a[2:3], got_b[4:5], from_a), add(own[5:6], got_a[3:4], got_b[5:6])], axis=0
-    )
+    far_a = add(own[2:4], got_a[4:6], got_b[2:4])
+    far_b = add(own[4:6], got_a[2:4], got_b[4:6], opposite)
     got_a, got_b = swap_a(far_a, 5), swap_b(far_b, 5)
     return jnp.stack([x.reshape(2 * BS, H) for x in (mine, got_a, got_b)])
 

time: 168 us -> 170 us (1.012)
  waiting for transfers between devices: 27.1 us -> 33.9 us
  starting transfers between devices: 39.4 us -> 34.9 us
    ppermute x4, waiting for transfers between devices: 11.6 us -> 19.7 us  [swap_a(): return lax.ppermute(x, 'row', pairs)]
    ppermute x4, starting transfers between devices: 22.2 us -> 19.9 us  [swap_a(): return lax.ppermute(x, 'row', pairs)]
    ppermute x4 -> x3, starting transfers between devices: 13.4 us -> 11.1 us  [swap_b(): return lax.ppermute(x, 'row', pairs)]
    ppermute x4 -> x3, waiting for transfers between devices: 10.2 us -> 8.98 us  [swap_b(): return lax.ppermute(x, 'row', pairs)]
  transfers between devices with their start and end apart: 10 -> 9, of which waited for: 8 -> 8; matrix products, arithmetic and copies ran while one was open for 0% -> 0% of each run, Pallas kernels for 0% -> 0%
where the time goes in v7:
time: 170 us
  blocking collectives  91.6 us (54%)
  starting transfers between devices  34.9 us (21%)
  waiting for transfers between devices  33.9 us (20%)
  Pallas kernels  5.85 us (3%)
  other arithmetic  2 us (1%)
    all_gather x1, blocking collectives, gather_rows(): got = lax.all_gather(sent, 'row', axis=0, tiled=True)  47.7 us
    all_to_all x1, blocking collectives, on_device(): lax.all_to_all(own, 'col', 0, 0, tiled=True, axis_index_groups=same_core)  24.3 us
    ppermute x4, starting transfers between devices, swap_a(): return lax.ppermute(x, 'row', pairs)  19.9 us
    ppermute x4, waiting for transfers between devices, swap_a(): return lax.ppermute(x, 'row', pairs)  19.7 us
    all_to_all x1, blocking collectives, on_device(): lax.all_to_all(link_copies, 'col', 0, 0, tiled=True, axis_index_groups=sa...  19.6 us
    ppermute x3, starting transfers between devices, swap_b(): return lax.ppermute(x, 'row', pairs)  11.1 us
    ppermute x3, waiting for transfers between devices, swap_b(): return lax.ppermute(x, 'row', pairs)  8.98 us
  transfers between devices with their start and end apart: 9, of which 8 were waited for; matrix products, arithmetic and copies ran while one was open for 0% of the time, Pallas kernels for 0%

profile of v7, /device:TPU:32, one launch (start us, length us, event | category | flops | bytes accessed | tf_op | source)
XLA Modules:
  0.0 169.6 jit_solution(13365495719479874130)
XLA Ops:
  0.6 0.9 multiply_convert_fusion.1
  1.6 47.7 %all-gather.1 = f16[4096,256]{1,0:T(8,128)(2,1)S(1)} all-gather(f16[256,256]{1,0:T(8,128)(2,1)S(1)} %multiply_convert_fusion.1), channel_id=1, replica_groups=mesh['row'=16,'col'=32] {'row'}, dimensions={0}, use_global_device_ids=true | all-gather | bytes 2228224 | tf_op jit(solution)/shard_map/all_gather | solution.py:226
  49.3 0.6 multiply_convert_fusion
  49.9 0.1 pad_add_fusion.me_ref
  50.0 0.5 copy-done
  50.4 1.6 link_products.1
  52.0 1.9 %collective-permute-start = (bf16[16,128,256]{2,1,0:T(8,128)(2,1)S(1)}, bf16[16,128,256]{2,1,0:T(8,128)(2,1)S(1)}, u32[]{:S(2)}, u32[]{:S(2)}) collective-permute-start(bf16[16,128,256]{2,1,0:T(8,128)(2,1)S(1)} %get-tuple-element.16), channel_id=1, source_target_pairs={{0,1},{1,0},{2,3},{3,2},{4,5},{5,4},{6,7},{7,6},{8,9},{9,8},{10,11... | collective-permute-start | bytes 3145736 | tf_op jit(solution)/shard_map/ppermute | solution.py:207
  54.0 2.6 %collective-permute-done.b_ref = bf16[16,128,256]{2,1,0:T(8,128)(2,1)S(1)} collective-permute-done((bf16[16,128,256]{2,1,0:T(8,128)(2,1)S(1)}, bf16[16,128,256]{2,1,0:T(8,128)(2,1)S(1)}, u32[]{:S(2)}, u32[]{:S(2)}) %collective-permute-start) | collective-permute-done | bytes 1048608 | tf_op jit(solution)/shard_map/ppermute | solution.py:207
  56.6 0.2 add_two.1
  56.9 24.3 %all_to_all.10.parts_ref = bf16[16,128,256]{2,1,0:T(8,128)(2,1)S(1)} all-to-all(bf16[16,128,256]{2,1,0:T(8,128)(2,1)S(1)} %add_two.1), channel_id=1, replica_groups={{0,2,4,6,8,10,12,14,16,18,20,22,24,26,28,30},{1,3,5,7,9,11,13,15,17,19,..., dimensions={0} | all-to-all | bytes 2097152 | tf_op jit(solution)/shard_map/all_to_all | solution.py:208
  81.2 1.2 link_update.1
  82.3 19.6 %all_to_all.11.own_ref = bf16[16,128,256]{2,1,0:T(8,128)(2,1)S(1)} all-to-all(bf16[16,128,256]{2,1,0:T(8,128)(2,1)S(1)} %get-tuple-element.18), channel_id=1, replica_groups={{0,2,4,6,8,10,12,14,16,18,20,22,24,26,28,30},{1,3,5,7,9,11,13,15,17,19,..., dimensions={0} | all-to-all | bytes 2097152 | tf_op jit(solution)/shard_map/all_to_all | solution.py:212
  101.9 1.9 %collective-permute-start.1 = (bf16[16,128,256]{2,1,0:T(8,128)(2,1)S(1)}, bf16[16,128,256]{2,1,0:T(8,128)(2,1)S(1)}, u32[]{:S(2)}, u32[]{:S(2)}) collective-permute-start(bf16[16,128,256]{2,1,0:T(8,128)(2,1)S(1)} %all_to_all.11.own_ref), channel_id=1, source_target_pairs={{0,1},{1,0},{2,3},{3,2},{4,5},{5,4},{6,7},{7,6},{8,9},{9,8},{10,11... | collective-permute-start | bytes 3145736 | tf_op jit(solution)/shard_map/ppermute | solution.py:213
  103.8 2.6 %collective-permute-done.1.other_ref = bf16[16,128,256]{2,1,0:T(8,128)(2,1)S(1)} collective-permute-done((bf16[16,128,256]{2,1,0:T(8,128)(2,1)S(1)}, bf16[16,128,256]{2,1,0:T(8,128)(2,1)S(1)}, u32[]{:S(2)}, u32[]{:S(2)}) %collective-permute-start.1) | collective-permute-done | bytes 1048608 | tf_op jit(solution)/shard_map/ppermute | solution.py:213
  106.5 1.8 %flow_products.1 = (bf16[6,128,256]{2,1,0:T(8,128)(2,1)S(1)}, bf16[6,128,256]{2,1,0:T(8,128)(2,1)S(1)}, bf16[6,128,256]{2,1,0:T(8,128)(2,1)S(1)}, bf16[6,128,256...) custom-call(s32[2]{0:T(128)S(1)} %pad_add_fusion.me_ref, ...), custom_call_target="tpu_custom_call" | custom-call | tf_op jit(solution)/shard_map/flow_products/pallas_call | solution.py:87
  108.3 3.6 %collective-permute-start.2 = (bf16[6,128,256]{2,1,0:T(8,128)(2,1)S(1)}, bf16[6,128,256]{2,1,0:T(8,128)(2,1)S(1)}, u32[]{:S(2)}, u32[]{:S(2)}) collective-permute-start(bf16[6,128,256]{2,1,0:T(8,128)(2,1)S(1)} %get-tuple-element.21), channel_id=1, source_target_pairs={{0,32},{32,0},{64,96},{96,64},{128,160},{160,128},{192,224},{224,1... | collective-permute-start | bytes 1179656 | tf_op jit(solution)/shard_map/ppermute | solution.py:112
  111.9 1.9 %collective-permute-start.3 = (bf16[6,128,256]{2,1,0:T(8,128)(2,1)S(1)}, bf16[6,128,256]{2,1,0:T(8,128)(2,1)S(1)}, u32[]{:S(2)}, u32[]{:S(2)}) collective-permute-start(bf16[6,128,256]{2,1,0:T(8,128)(2,1)S(1)} %get-tuple-element.22), channel_id=1, source_target_pairs={{0,480},{32,64},{64,32},{96,128},{128,96},{160,192},{192,160},{224... | collective-permute-start | bytes 1179656 | tf_op jit(solution)/shard_map/ppermute | solution.py:116
  113.8 6.0 %collective-permute-start.4 = (bf16[2,128,256]{2,1,0:T(8,128)(2,1)S(1)}, bf16[2,128,256]{2,1,0:T(8,128)(2,1)S(1)}, u32[]{:S(2)}, u32[]{:S(2)}) collective-permute-start(bf16[2,128,256]{2,1,0:T(8,128)(2,1)S(1)} %get-tuple-element.23), channel_id=1, source_target_pairs={{0,96},{32,448},{64,160},{96,0},{128,224},{160,64},{192,288},{224,... | collective-permute-start | bytes 393224 | tf_op jit(solution)/shard_map/ppermute | solution.py:112
  119.8 6.3 %collective-permute-done.4 = bf16[2,128,256]{2,1,0:T(8,128)(2,1)S(1)} collective-permute-done((bf16[2,128,256]{2,1,0:T(8,128)(2,1)S(1)}, bf16[2,128,256]{2,1,0:T(8,128)(2,1)S(1)}, u32[]{:S(2)}, u32[]{:S(2)}) %collective-permute-start.4) | collective-permute-done | bytes 131104 | tf_op jit(solution)/shard_map/ppermute | solution.py:112
  126.2 1.3 collective-permute-done.3
  127.5 0.1 add_convert_fusion
  127.6 3.6 %collective-permute-start.6 = (bf16[6,128,256]{2,1,0:T(8,128)(2,1)S(1)}, bf16[6,128,256]{2,1,0:T(8,128)(2,1)S(1)}, u32[]{:S(2)}, u32[]{:S(2)}) collective-permute-start(bf16[6,128,256]{2,1,0:T(8,128)(2,1)S(1)} %add_convert_fusion), channel_id=1, source_target_pairs={{0,480},{32,64},{64,32},{96,128},{128,96},{160,192},{192,160},{224... | collective-permute-start | bytes 1179656 | tf_op jit(solution)/shard_map/ppermute | solution.py:116
  131.3 0.1 add_convert_fusion.1
  131.4 3.9 %collective-permute-start.5 = (bf16[6,128,256]{2,1,0:T(8,128)(2,1)S(1)}, bf16[6,128,256]{2,1,0:T(8,128)(2,1)S(1)}, u32[]{:S(2)}, u32[]{:S(2)}) collective-permute-start(bf16[6,128,256]{2,1,0:T(8,128)(2,1)S(1)} %add_convert_fusion.1), channel_id=1, source_target_pairs={{0,32},{32,0},{64,96},{96,64},{128,160},{160,128},{192,224},{224,1... | collective-permute-start | bytes 1179656 | tf_op jit(solution)/shard_map/ppermute | solution.py:112
  135.3 4.8 %collective-permute-done.6 = bf16[6,128,256]{2,1,0:T(8,128)(2,1)S(1)} collective-permute-done((bf16[6,128,256]{2,1,0:T(8,128)(2,1)S(1)}, bf16[6,128,256]{2,1,0:T(8,128)(2,1)S(1)}, u32[]{:S(2)}, u32[]{:S(2)}) %collective-permute-start.6) | collective-permute-done | bytes 393248 | tf_op jit(solution)/shard_map/ppermute | solution.py:116
  140.0 3.5 %collective-permute-done.5 = bf16[6,128,256]{2,1,0:T(8,128)(2,1)S(1)} collective-permute-done((bf16[6,128,256]{2,1,0:T(8,128)(2,1)S(1)}, bf16[6,128,256]{2,1,0:T(8,128)(2,1)S(1)}, u32[]{:S(2)}, u32[]{:S(2)}) %collective-permute-start.5) | collective-permute-done | bytes 393248 | tf_op jit(solution)/shard_map/ppermute | solution.py:112
  143.5 0.2 add_convert_fusion.4
  143.7 5.6 %collective-permute-start.8 = (bf16[2,128,256]{2,1,0:T(8,128)(2,1)S(1)}, bf16[2,128,256]{2,1,0:T(8,128)(2,1)S(1)}, u32[]{:S(2)}, u32[]{:S(2)}) collective-permute-start(bf16[2,128,256]{2,1,0:T(8,128)(2,1)S(1)} %get-tuple-element.29), channel_id=1, source_target_pairs={{0,352},{32,192},{64,416},{96,256},{128,480},{160,320},{192,32},{2... | collective-permute-start | bytes 393224 | tf_op jit(solution)/shard_map/ppermute | solution.py:116
  149.3 6.3 %collective-permute-start.7 = (bf16[2,128,256]{2,1,0:T(8,128)(2,1)S(1)}, bf16[2,128,256]{2,1,0:T(8,128)(2,1)S(1)}, u32[]{:S(2)}, u32[]{:S(2)}) collective-permute-start(bf16[2,128,256]{2,1,0:T(8,128)(2,1)S(1)} %get-tuple-element.30), channel_id=1, source_target_pairs={{0,160},{32,384},{64,224},{96,448},{128,288},{160,0},{192,352},{22... | collective-permute-start | bytes 393224 | tf_op jit(solution)/shard_map/ppermute | solution.py:112
  155.7 2.9 %collective-permute-done.8 = bf16[2,128,256]{2,1,0:T(8,128)(2,1)S(1)} collective-permute-done((bf16[2,128,256]{2,1,0:T(8,128)(2,1)S(1)}, bf16[2,128,256]{2,1,0:T(8,128)(2,1)S(1)}, u32[]{:S(2)}, u32[]{:S(2)}) %collective-permute-start.8) | collective-permute-done | bytes 131104 | tf_op jit(solution)/shard_map/ppermute | solution.py:116
  158.6 9.9 %collective-permute-done.7 = bf16[2,128,256]{2,1,0:T(8,128)(2,1)S(1)} collective-permute-done((bf16[2,128,256]{2,1,0:T(8,128)(2,1)S(1)}, bf16[2,128,256]{2,1,0:T(8,128)(2,1)S(1)}, u32[]{:S(2)}, u32[]{:S(2)}) %collective-permute-start.7) | collective-permute-done | bytes 131104 | tf_op jit(solution)/shard_map/ppermute | solution.py:112
  168.6 1.1 flow_update.1
  (29 shorter events, 0.1 us)
Async XLA Ops:
  49.3 1.1 copy-start
  49.3 1.1 copy-start.9
  49.3 1.1 copy-start.10
  49.3 1.1 copy-start.11
  52.0 4.6 %collective-permute-start = (bf16[16,128,256]{2,1,0:T(8,128)(2,1)S(1)}, bf16[16,128,256]{2,1,0:T(8,128)(2,1)S(1)}, u32[]{:S(2)}, u32[]{:S(2)}) collective-permute-start(bf16[16,128,256]{2,1,0:T(8,128)(2,1)S(1)} %get-tuple-element.16), channel_id=1, source_target_pairs={{0,1},{1,0},{2,3},{3,2},{4,5},{5,4},{6,7},{7,6},{8,9},{9,8},{10,11... | collective-permute-start | bytes 3145736 | tf_op jit(solution)/shard_map/ppermute | solution.py:207
  56.6 24.6 %copy-start.2 = (bf16[256,256]{1,0:T(8,128)(2,1)S(1)}, bf16[256,256]{1,0:T(8,128)(2,1)}, u32[]{:S(2)}) copy-start(bf16[256,256]{1,0:T(8,128)(2,1)} %agg_ref.2) | copy-start | bytes 393220
  56.6 24.6 %copy-start.3 = (bf16[256,256]{1,0:T(8,128)(2,1)S(1)}, bf16[256,256]{1,0:T(8,128)(2,1)}, u32[]{:S(2)}) copy-start(bf16[256,256]{1,0:T(8,128)(2,1)} %self_ref.2) | copy-start | bytes 393220
  56.6 24.6 %copy-start.4 = (bf16[256,256]{1,0:T(8,128)(2,1)S(1)}, bf16[256,256]{1,0:T(8,128)(2,1)}, u32[]{:S(2)}) copy-start(bf16[256,256]{1,0:T(8,128)(2,1)} %out_w_ref.2) | copy-start | bytes 393220
  56.6 24.6 %copy-start.8 = (bf16[128,256]{1,0:T(8,128)(2,1)S(1)}, bf16[128,256]{1,0:T(8,128)(2,1)}, u32[]{:S(2)}) copy-start(bf16[128,256]{1,0:T(8,128)(2,1)} %state_ref.2) | copy-start | bytes 196612
  56.6 24.6 %copy-start.12 = (f32[256]{0:T(256)S(1)}, f32[256]{0:T(256)}, u32[]{:S(2)}) copy-start(f32[256]{0:T(256)} %param.20) | copy-start | bytes 3076
  101.9 4.5 %collective-permute-start.1 = (bf16[16,128,256]{2,1,0:T(8,128)(2,1)S(1)}, bf16[16,128,256]{2,1,0:T(8,128)(2,1)S(1)}, u32[]{:S(2)}, u32[]{:S(2)}) collective-permute-start(bf16[16,128,256]{2,1,0:T(8,128)(2,1)S(1)} %all_to_all.11.own_ref), channel_id=1, source_target_pairs={{0,1},{1,0},{2,3},{3,2},{4,5},{5,4},{6,7},{7,6},{8,9},{9,8},{10,11... | collective-permute-start | bytes 3145736 | tf_op jit(solution)/shard_map/ppermute | solution.py:213
  108.3 17.9 %collective-permute-start.2 = (bf16[6,128,256]{2,1,0:T(8,128)(2,1)S(1)}, bf16[6,128,256]{2,1,0:T(8,128)(2,1)S(1)}, u32[]{:S(2)}, u32[]{:S(2)}) collective-permute-start(bf16[6,128,256]{2,1,0:T(8,128)(2,1)S(1)} %get-tuple-element.21), channel_id=1, source_target_pairs={{0,32},{32,0},{64,96},{96,64},{128,160},{160,128},{192,224},{224,1... | collective-permute-start | bytes 1179656 | tf_op jit(solution)/shard_map/ppermute | solution.py:112
  111.9 15.6 %collective-permute-start.3 = (bf16[6,128,256]{2,1,0:T(8,128)(2,1)S(1)}, bf16[6,128,256]{2,1,0:T(8,128)(2,1)S(1)}, u32[]{:S(2)}, u32[]{:S(2)}) collective-permute-start(bf16[6,128,256]{2,1,0:T(8,128)(2,1)S(1)} %get-tuple-element.22), channel_id=1, source_target_pairs={{0,480},{32,64},{64,32},{96,128},{128,96},{160,192},{192,160},{224... | collective-permute-start | bytes 1179656 | tf_op jit(solution)/shard_map/ppermute | solution.py:116
  113.8 12.3 %collective-permute-start.4 = (bf16[2,128,256]{2,1,0:T(8,128)(2,1)S(1)}, bf16[2,128,256]{2,1,0:T(8,128)(2,1)S(1)}, u32[]{:S(2)}, u32[]{:S(2)}) collective-permute-start(bf16[2,128,256]{2,1,0:T(8,128)(2,1)S(1)} %get-tuple-element.23), channel_id=1, source_target_pairs={{0,96},{32,448},{64,160},{96,0},{128,224},{160,64},{192,288},{224,... | collective-permute-start | bytes 393224 | tf_op jit(solution)/shard_map/ppermute | solution.py:112
  127.6 40.9 %copy-start.1 = (bf16[256,256]{1,0:T(8,128)(2,1)S(1)}, bf16[256,256]{1,0:T(8,128)(2,1)}, u32[]{:S(2)}) copy-start(bf16[256,256]{1,0:T(8,128)(2,1)} %state_ref.3) | copy-start | bytes 393220
  127.6 40.9 %copy-start.5 = (bf16[256,256]{1,0:T(8,128)(2,1)S(1)}, bf16[256,256]{1,0:T(8,128)(2,1)}, u32[]{:S(2)}) copy-start(bf16[256,256]{1,0:T(8,128)(2,1)} %agg_ref.3) | copy-start | bytes 393220
  127.6 40.9 %copy-start.6 = (bf16[256,256]{1,0:T(8,128)(2,1)S(1)}, bf16[256,256]{1,0:T(8,128)(2,1)}, u32[]{:S(2)}) copy-start(bf16[256,256]{1,0:T(8,128)(2,1)} %self_ref.3) | copy-start | bytes 393220
  127.6 40.9 %copy-start.7 = (bf16[256,256]{1,0:T(8,128)(2,1)S(1)}, bf16[256,256]{1,0:T(8,128)(2,1)}, u32[]{:S(2)}) copy-start(bf16[256,256]{1,0:T(8,128)(2,1)} %out_w_ref.3) | copy-start | bytes 393220
  127.6 40.9 %copy-start.13 = (f32[256]{0:T(256)S(1)}, f32[256]{0:T(256)}, u32[]{:S(2)}) copy-start(f32[256]{0:T(256)} %param.24) | copy-start | bytes 3076
  127.6 12.4 %collective-permute-start.6 = (bf16[6,128,256]{2,1,0:T(8,128)(2,1)S(1)}, bf16[6,128,256]{2,1,0:T(8,128)(2,1)S(1)}, u32[]{:S(2)}, u32[]{:S(2)}) collective-permute-start(bf16[6,128,256]{2,1,0:T(8,128)(2,1)S(1)} %add_convert_fusion), channel_id=1, source_target_pairs={{0,480},{32,64},{64,32},{96,128},{128,96},{160,192},{192,160},{224... | collective-permute-start | bytes 1179656 | tf_op jit(solution)/shard_map/ppermute | solution.py:116
  131.4 12.2 %collective-permute-start.5 = (bf16[6,128,256]{2,1,0:T(8,128)(2,1)S(1)}, bf16[6,128,256]{2,1,0:T(8,128)(2,1)S(1)}, u32[]{:S(2)}, u32[]{:S(2)}) collective-permute-start(bf16[6,128,256]{2,1,0:T(8,128)(2,1)S(1)} %add_convert_fusion.1), channel_id=1, source_target_pairs={{0,32},{32,0},{64,96},{96,64},{128,160},{160,128},{192,224},{224,1... | collective-permute-start | bytes 1179656 | tf_op jit(solution)/shard_map/ppermute | solution.py:112
  143.7 14.9 %collective-permute-start.8 = (bf16[2,128,256]{2,1,0:T(8,128)(2,1)S(1)}, bf16[2,128,256]{2,1,0:T(8,128)(2,1)S(1)}, u32[]{:S(2)}, u32[]{:S(2)}) collective-permute-start(bf16[2,128,256]{2,1,0:T(8,128)(2,1)S(1)} %get-tuple-element.29), channel_id=1, source_target_pairs={{0,352},{32,192},{64,416},{96,256},{128,480},{160,320},{192,32},{2... | collective-permute-start | bytes 393224 | tf_op jit(solution)/shard_map/ppermute | solution.py:116
  149.3 19.1 %collective-permute-start.7 = (bf16[2,128,256]{2,1,0:T(8,128)(2,1)S(1)}, bf16[2,128,256]{2,1,0:T(8,128)(2,1)S(1)}, u32[]{:S(2)}, u32[]{:S(2)}) collective-permute-start(bf16[2,128,256]{2,1,0:T(8,128)(2,1)S(1)} %get-tuple-element.30), channel_id=1, source_target_pairs={{0,160},{32,384},{64,224},{96,448},{128,288},{160,0},{192,352},{22... | collective-permute-start | bytes 393224 | tf_op jit(solution)/shard_map/ppermute | solution.py:112

commit v8 on v7

--- a/solution.py
+++ b/solution.py
@@ -83,7 +83,7 @@
 
 def flow_products(me, flow, link, live, coefs, own, other, blocks):
     assert blocks == 2 * len(ROW_ORDER)
-    counts = [6] * 5 + [2]
+    counts = [6] + [3] * 8 + [2]
     return pl.pallas_call(
         flow_products_kernel,
         out_shape=[jax.ShapeDtypeStruct((count, BS, H), BF16) for count in counts],
@@ -106,7 +106,10 @@
     return total.astype(BF16)
 
 
-def sum_over_rows(own, two_a, two_b, one_a, one_b, opposite, rows):
+def sum_over_rows(own, *parts):
+    *two_a, two_b0, two_b1, one_a0, one_a1, one_b0, one_b1, opposite = parts
+    rows = len(ROW_ORDER)
+
     def swap_a(x, step):
         pairs = [(i, (i + step if i % 2 == 0 else i - step) % rows) for i in range(rows)]
         return lax.ppermute(x, "row", pairs)
@@ -115,11 +118,15 @@
         pairs = [(i, (i - step if i % 2 == 0 else i + step) % rows) for i in range(rows)]
         return lax.ppermute(x, "row", pairs)
 
-    got_a, got_b = swap_a(two_a, 1), swap_b(two_b, 1)
+    halves_a, halves_b = [], []
+    for half_a, half_b, next_a, next_b in zip(
+        two_a, (two_b0, two_b1), (one_a0, one_a1), (one_b0, one_b1)
+    ):
+        got_a, got_b = swap_a(half_a, 1), swap_b(half_b, 1)
+        halves_b.append(swap_b(add(next_b, got_a), 1))
+        halves_a.append(swap_a(add(next_a, got_b), 1))
     opposite = swap_a(opposite, 3)
-    got_a, got_b, opposite = lax.optimization_barrier((got_a, got_b, opposite))
-    one_b, one_a = add(one_b, got_a), add(one_a, got_b)
-    got_a, got_b = swap_a(one_a, 1), swap_b(one_b, 1)
+    got_a, got_b = jnp.concatenate(halves_a, axis=0), jnp.concatenate(halves_b, axis=0)
     mine = add(own[:2], got_a[:2], got_b[:2])
     far_a = add(own[2:4], got_a[4:6], got_b[2:4])
     far_b = add(own[4:6], got_a[2:4], got_b[4:6], opposite)
@@ -214,7 +221,7 @@
     parts = flow_products(
         me, tile_flow, tile_link, tile_live, coefs, own, other, flow_blocks
     )
-    flow_parts = sum_over_rows(*parts, rows)
+    flow_parts = sum_over_rows(*parts)
     (flow_next,) = update(
         flow_parts, flow_state, flow_gain, flow_agg_weight, flow_self_weight, flow_out_weight, 0
     )

time: 170 us -> 169 us (level)
  waiting for transfers between devices: 33.9 us -> 26.7 us
  starting transfers between devices: 34.9 us -> 41.2 us
    ppermute x4 -> x6, waiting for transfers between devices: 19.7 us -> 15.6 us  [swap_a(): return lax.ppermute(x, 'row', pairs)]
    ppermute x4 -> x6, starting transfers between devices: 19.9 us -> 23.4 us  [swap_a(): return lax.ppermute(x, 'row', pairs)]
    ppermute x3 -> x5, waiting for transfers between devices: 8.98 us -> 5.79 us  [swap_b(): return lax.ppermute(x, 'row', pairs)]
    ppermute x3 -> x5, starting transfers between devices: 11.1 us -> 13.9 us  [swap_b(): return lax.ppermute(x, 'row', pairs)]
  transfers between devices with their start and end apart: 9 -> 13, of which waited for: 8 -> 5; matrix products, arithmetic and copies ran while one was open for 0% -> 0% of each run, Pallas kernels for 0% -> 0%
where the time goes in v8:
time: 169 us
  blocking collectives  91.6 us (54%)
  starting transfers between devices  41.2 us (24%)
  waiting for transfers between devices  26.7 us (16%)
  Pallas kernels  5.85 us (3%)
  other arithmetic  2.01 us (1%)
    all_gather x1, blocking collectives, gather_rows(): got = lax.all_gather(sent, 'row', axis=0, tiled=True)  47.7 us
    all_to_all x1, blocking collectives, on_device(): lax.all_to_all(own, 'col', 0, 0, tiled=True, axis_index_groups=same_core)  24.3 us
    ppermute x6, starting transfers between devices, swap_a(): return lax.ppermute(x, 'row', pairs)  23.4 us
    all_to_all x1, blocking collectives, on_device(): lax.all_to_all(link_copies, 'col', 0, 0, tiled=True, axis_index_groups=sa...  19.6 us
    ppermute x6, waiting for transfers between devices, swap_a(): return lax.ppermute(x, 'row', pairs)  15.6 us
    ppermute x5, starting transfers between devices, swap_b(): return lax.ppermute(x, 'row', pairs)  13.9 us
    ppermute x5, waiting for transfers between devices, swap_b(): return lax.ppermute(x, 'row', pairs)  5.79 us
  transfers between devices with their start and end apart: 13, of which 5 were waited for; matrix products, arithmetic and copies ran while one was open for 0% of the time, Pallas kernels for 0%

profile of v8, /device:TPU:32, one launch (start us, length us, event | category | flops | bytes accessed | tf_op | source)
XLA Modules:
  0.0 168.8 jit_solution(16443290699525202487)
XLA Ops:
  0.6 0.9 multiply_convert_fusion.1
  1.6 47.7 %all-gather.1 = f16[4096,256]{1,0:T(8,128)(2,1)S(1)} all-gather(f16[256,256]{1,0:T(8,128)(2,1)S(1)} %multiply_convert_fusion.1), channel_id=1, replica_groups=mesh['row'=16,'col'=32] {'row'}, dimensions={0}, use_global_device_ids=true | all-gather | bytes 2228224 | tf_op jit(solution)/shard_map/all_gather | solution.py:233
  49.3 0.6 multiply_convert_fusion
  49.9 0.1 pad_add_fusion.me_ref
  50.0 0.5 copy-done
  50.4 1.6 link_products.1
  52.0 1.9 %collective-permute-start = (bf16[16,128,256]{2,1,0:T(8,128)(2,1)S(1)}, bf16[16,128,256]{2,1,0:T(8,128)(2,1)S(1)}, u32[]{:S(2)}, u32[]{:S(2)}) collective-permute-start(bf16[16,128,256]{2,1,0:T(8,128)(2,1)S(1)} %get-tuple-element.17), channel_id=1, source_target_pairs={{0,1},{1,0},{2,3},{3,2},{4,5},{5,4},{6,7},{7,6},{8,9},{9,8},{10,11... | collective-permute-start | bytes 3145736 | tf_op jit(solution)/shard_map/ppermute | solution.py:214
  54.0 2.6 %collective-permute-done.b_ref = bf16[16,128,256]{2,1,0:T(8,128)(2,1)S(1)} collective-permute-done((bf16[16,128,256]{2,1,0:T(8,128)(2,1)S(1)}, bf16[16,128,256]{2,1,0:T(8,128)(2,1)S(1)}, u32[]{:S(2)}, u32[]{:S(2)}) %collective-permute-start) | collective-permute-done | bytes 1048608 | tf_op jit(solution)/shard_map/ppermute | solution.py:214
  56.6 0.0 copy-start.12
  56.6 0.2 add_two.1
  56.9 24.3 %all_to_all.10.parts_ref = bf16[16,128,256]{2,1,0:T(8,128)(2,1)S(1)} all-to-all(bf16[16,128,256]{2,1,0:T(8,128)(2,1)S(1)} %add_two.1), channel_id=1, replica_groups={{0,2,4,6,8,10,12,14,16,18,20,22,24,26,28,30},{1,3,5,7,9,11,13,15,17,19,..., dimensions={0} | all-to-all | bytes 2097152 | tf_op jit(solution)/shard_map/all_to_all | solution.py:215
  81.2 1.2 link_update.1
  82.3 19.6 %all_to_all.11.own_ref = bf16[16,128,256]{2,1,0:T(8,128)(2,1)S(1)} all-to-all(bf16[16,128,256]{2,1,0:T(8,128)(2,1)S(1)} %get-tuple-element.19), channel_id=1, replica_groups={{0,2,4,6,8,10,12,14,16,18,20,22,24,26,28,30},{1,3,5,7,9,11,13,15,17,19,..., dimensions={0} | all-to-all | bytes 2097152 | tf_op jit(solution)/shard_map/all_to_all | solution.py:219
  101.9 1.9 %collective-permute-start.1 = (bf16[16,128,256]{2,1,0:T(8,128)(2,1)S(1)}, bf16[16,128,256]{2,1,0:T(8,128)(2,1)S(1)}, u32[]{:S(2)}, u32[]{:S(2)}) collective-permute-start(bf16[16,128,256]{2,1,0:T(8,128)(2,1)S(1)} %all_to_all.11.own_ref), channel_id=1, source_target_pairs={{0,1},{1,0},{2,3},{3,2},{4,5},{5,4},{6,7},{7,6},{8,9},{9,8},{10,11... | collective-permute-start | bytes 3145736 | tf_op jit(solution)/shard_map/ppermute | solution.py:220
  103.8 2.6 %collective-permute-done.1.other_ref = bf16[16,128,256]{2,1,0:T(8,128)(2,1)S(1)} collective-permute-done((bf16[16,128,256]{2,1,0:T(8,128)(2,1)S(1)}, bf16[16,128,256]{2,1,0:T(8,128)(2,1)S(1)}, u32[]{:S(2)}, u32[]{:S(2)}) %collective-permute-start.1) | collective-permute-done | bytes 1048608 | tf_op jit(solution)/shard_map/ppermute | solution.py:220
  106.5 1.8 %flow_products.1 = (bf16[6,128,256]{2,1,0:T(8,128)(2,1)S(1)}, bf16[3,128,256]{2,1,0:T(8,128)(2,1)S(1)}, bf16[3,128,256]{2,1,0:T(8,128)(2,1)S(1)}, bf16[3,128,256...) custom-call(s32[2]{0:T(128)S(1)} %pad_add_fusion.me_ref, ...), custom_call_target="tpu_custom_call" | custom-call | tf_op jit(solution)/shard_map/flow_products/pallas_call | solution.py:87
  108.3 2.4 %collective-permute-start.2 = (bf16[3,128,256]{2,1,0:T(8,128)(2,1)S(1)}, bf16[3,128,256]{2,1,0:T(8,128)(2,1)S(1)}, u32[]{:S(2)}, u32[]{:S(2)}) collective-permute-start(bf16[3,128,256]{2,1,0:T(8,128)(2,1)S(1)} %get-tuple-element.22), channel_id=1, source_target_pairs={{0,480},{32,64},{64,32},{96,128},{128,96},{160,192},{192,160},{224... | collective-permute-start | bytes 589832 | tf_op jit(solution)/shard_map/ppermute | solution.py:119
  110.7 3.4 %collective-permute-start.4 = (bf16[3,128,256]{2,1,0:T(8,128)(2,1)S(1)}, bf16[3,128,256]{2,1,0:T(8,128)(2,1)S(1)}, u32[]{:S(2)}, u32[]{:S(2)}) collective-permute-start(bf16[3,128,256]{2,1,0:T(8,128)(2,1)S(1)} %get-tuple-element.24), channel_id=1, source_target_pairs={{0,32},{32,0},{64,96},{96,64},{128,160},{160,128},{192,224},{224,1... | collective-permute-start | bytes 589832 | tf_op jit(solution)/shard_map/ppermute | solution.py:115
  114.1 3.2 %collective-permute-start.6 = (bf16[3,128,256]{2,1,0:T(8,128)(2,1)S(1)}, bf16[3,128,256]{2,1,0:T(8,128)(2,1)S(1)}, u32[]{:S(2)}, u32[]{:S(2)}) collective-permute-start(bf16[3,128,256]{2,1,0:T(8,128)(2,1)S(1)} %get-tuple-element.26), channel_id=1, source_target_pairs={{0,480},{32,64},{64,32},{96,128},{128,96},{160,192},{192,160},{224... | collective-permute-start | bytes 589832 | tf_op jit(solution)/shard_map/ppermute | solution.py:119
  117.3 3.9 %collective-permute-start.8 = (bf16[3,128,256]{2,1,0:T(8,128)(2,1)S(1)}, bf16[3,128,256]{2,1,0:T(8,128)(2,1)S(1)}, u32[]{:S(2)}, u32[]{:S(2)}) collective-permute-start(bf16[3,128,256]{2,1,0:T(8,128)(2,1)S(1)} %get-tuple-element.28), channel_id=1, source_target_pairs={{0,32},{32,0},{64,96},{96,64},{128,160},{160,128},{192,224},{224,1... | collective-permute-start | bytes 589832 | tf_op jit(solution)/shard_map/ppermute | solution.py:115
  121.2 2.0 %collective-permute-start.3 = (bf16[3,128,256]{2,1,0:T(8,128)(2,1)S(1)}, bf16[3,128,256]{2,1,0:T(8,128)(2,1)S(1)}, u32[]{:S(2)}, u32[]{:S(2)}) collective-permute-start(bf16[3,128,256]{2,1,0:T(8,128)(2,1)S(1)} %add_convert_fusion.3), channel_id=1, source_target_pairs={{0,32},{32,0},{64,96},{96,64},{128,160},{160,128},{192,224},{224,1... | collective-permute-start | bytes 589832 | tf_op jit(solution)/shard_map/ppermute | solution.py:115
  123.2 2.7 %collective-permute-start.5 = (bf16[3,128,256]{2,1,0:T(8,128)(2,1)S(1)}, bf16[3,128,256]{2,1,0:T(8,128)(2,1)S(1)}, u32[]{:S(2)}, u32[]{:S(2)}) collective-permute-start(bf16[3,128,256]{2,1,0:T(8,128)(2,1)S(1)} %add_convert_fusion.2), channel_id=1, source_target_pairs={{0,480},{32,64},{64,32},{96,128},{128,96},{160,192},{192,160},{224... | collective-permute-start | bytes 589832 | tf_op jit(solution)/shard_map/ppermute | solution.py:119
  126.0 3.8 %collective-permute-start.7 = (bf16[3,128,256]{2,1,0:T(8,128)(2,1)S(1)}, bf16[3,128,256]{2,1,0:T(8,128)(2,1)S(1)}, u32[]{:S(2)}, u32[]{:S(2)}) collective-permute-start(bf16[3,128,256]{2,1,0:T(8,128)(2,1)S(1)} %add_convert_fusion.1), channel_id=1, source_target_pairs={{0,32},{32,0},{64,96},{96,64},{128,160},{160,128},{192,224},{224,1... | collective-permute-start | bytes 589832 | tf_op jit(solution)/shard_map/ppermute | solution.py:115
  129.9 3.4 %collective-permute-start.9 = (bf16[3,128,256]{2,1,0:T(8,128)(2,1)S(1)}, bf16[3,128,256]{2,1,0:T(8,128)(2,1)S(1)}, u32[]{:S(2)}, u32[]{:S(2)}) collective-permute-start(bf16[3,128,256]{2,1,0:T(8,128)(2,1)S(1)} %add_convert_fusion), channel_id=1, source_target_pairs={{0,480},{32,64},{64,32},{96,128},{128,96},{160,192},{192,160},{224... | collective-permute-start | bytes 589832 | tf_op jit(solution)/shard_map/ppermute | solution.py:119
  133.4 4.5 %collective-permute-start.11 = (bf16[2,128,256]{2,1,0:T(8,128)(2,1)S(1)}, bf16[2,128,256]{2,1,0:T(8,128)(2,1)S(1)}, u32[]{:S(2)}, u32[]{:S(2)}) collective-permute-start(bf16[2,128,256]{2,1,0:T(8,128)(2,1)S(1)} %get-tuple-element.29), channel_id=1, source_target_pairs={{0,96},{32,448},{64,160},{96,0},{128,224},{160,64},{192,288},{224,... | collective-permute-start | bytes 393224 | tf_op jit(solution)/shard_map/ppermute | solution.py:115
  137.9 6.6 %collective-permute-done.11 = bf16[2,128,256]{2,1,0:T(8,128)(2,1)S(1)} collective-permute-done((bf16[2,128,256]{2,1,0:T(8,128)(2,1)S(1)}, bf16[2,128,256]{2,1,0:T(8,128)(2,1)S(1)}, u32[]{:S(2)}, u32[]{:S(2)}) %collective-permute-start.11) | collective-permute-done | bytes 131104 | tf_op jit(solution)/shard_map/ppermute | solution.py:115
  144.5 0.2 add_convert_fusion.5
  144.7 5.8 %collective-permute-start.10 = (bf16[2,128,256]{2,1,0:T(8,128)(2,1)S(1)}, bf16[2,128,256]{2,1,0:T(8,128)(2,1)S(1)}, u32[]{:S(2)}, u32[]{:S(2)}) collective-permute-start(bf16[2,128,256]{2,1,0:T(8,128)(2,1)S(1)} %get-tuple-element.30), channel_id=1, source_target_pairs={{0,160},{32,384},{64,224},{96,448},{128,288},{160,0},{192,352},{22... | collective-permute-start | bytes 393224 | tf_op jit(solution)/shard_map/ppermute | solution.py:115
  150.5 2.3 %collective-permute-start.12 = (bf16[2,128,256]{2,1,0:T(8,128)(2,1)S(1)}, bf16[2,128,256]{2,1,0:T(8,128)(2,1)S(1)}, u32[]{:S(2)}, u32[]{:S(2)}) collective-permute-start(bf16[2,128,256]{2,1,0:T(8,128)(2,1)S(1)} %get-tuple-element.31), channel_id=1, source_target_pairs={{0,352},{32,192},{64,416},{96,256},{128,480},{160,320},{192,32},{2... | collective-permute-start | bytes 393224 | tf_op jit(solution)/shard_map/ppermute | solution.py:119
  152.8 9.1 %collective-permute-done.10 = bf16[2,128,256]{2,1,0:T(8,128)(2,1)S(1)} collective-permute-done((bf16[2,128,256]{2,1,0:T(8,128)(2,1)S(1)}, bf16[2,128,256]{2,1,0:T(8,128)(2,1)S(1)}, u32[]{:S(2)}, u32[]{:S(2)}) %collective-permute-start.10) | collective-permute-done | bytes 131104 | tf_op jit(solution)/shard_map/ppermute | solution.py:115
  161.8 5.8 %collective-permute-done.12 = bf16[2,128,256]{2,1,0:T(8,128)(2,1)S(1)} collective-permute-done((bf16[2,128,256]{2,1,0:T(8,128)(2,1)S(1)}, bf16[2,128,256]{2,1,0:T(8,128)(2,1)S(1)}, u32[]{:S(2)}, u32[]{:S(2)}) %collective-permute-start.12) | collective-permute-done | bytes 131104 | tf_op jit(solution)/shard_map/ppermute | solution.py:119
  167.7 1.1 flow_update.1
  (39 shorter events, 0.3 us)
Async XLA Ops:
  49.3 1.1 copy-start
  49.3 1.1 copy-start.9
  49.3 1.1 copy-start.10
  49.3 1.1 copy-start.11
  52.0 4.6 %collective-permute-start = (bf16[16,128,256]{2,1,0:T(8,128)(2,1)S(1)}, bf16[16,128,256]{2,1,0:T(8,128)(2,1)S(1)}, u32[]{:S(2)}, u32[]{:S(2)}) collective-permute-start(bf16[16,128,256]{2,1,0:T(8,128)(2,1)S(1)} %get-tuple-element.17), channel_id=1, source_target_pairs={{0,1},{1,0},{2,3},{3,2},{4,5},{5,4},{6,7},{7,6},{8,9},{9,8},{10,11... | collective-permute-start | bytes 3145736 | tf_op jit(solution)/shard_map/ppermute | solution.py:214
  56.6 24.6 %copy-start.2 = (bf16[256,256]{1,0:T(8,128)(2,1)S(1)}, bf16[256,256]{1,0:T(8,128)(2,1)}, u32[]{:S(2)}) copy-start(bf16[256,256]{1,0:T(8,128)(2,1)} %agg_ref.2) | copy-start | bytes 393220
  56.6 24.6 %copy-start.3 = (bf16[256,256]{1,0:T(8,128)(2,1)S(1)}, bf16[256,256]{1,0:T(8,128)(2,1)}, u32[]{:S(2)}) copy-start(bf16[256,256]{1,0:T(8,128)(2,1)} %self_ref.2) | copy-start | bytes 393220
  56.6 24.6 %copy-start.4 = (bf16[256,256]{1,0:T(8,128)(2,1)S(1)}, bf16[256,256]{1,0:T(8,128)(2,1)}, u32[]{:S(2)}) copy-start(bf16[256,256]{1,0:T(8,128)(2,1)} %out_w_ref.2) | copy-start | bytes 393220
  56.6 24.6 %copy-start.8 = (bf16[128,256]{1,0:T(8,128)(2,1)S(1)}, bf16[128,256]{1,0:T(8,128)(2,1)}, u32[]{:S(2)}) copy-start(bf16[128,256]{1,0:T(8,128)(2,1)} %state_ref.2) | copy-start | bytes 196612
  56.6 24.6 %copy-start.12 = (f32[256]{0:T(256)S(1)}, f32[256]{0:T(256)}, u32[]{:S(2)}) copy-start(f32[256]{0:T(256)} %param.20) | copy-start | bytes 3076
  101.9 4.5 %collective-permute-start.1 = (bf16[16,128,256]{2,1,0:T(8,128)(2,1)S(1)}, bf16[16,128,256]{2,1,0:T(8,128)(2,1)S(1)}, u32[]{:S(2)}, u32[]{:S(2)}) collective-permute-start(bf16[16,128,256]{2,1,0:T(8,128)(2,1)S(1)} %all_to_all.11.own_ref), channel_id=1, source_target_pairs={{0,1},{1,0},{2,3},{3,2},{4,5},{5,4},{6,7},{7,6},{8,9},{9,8},{10,11... | collective-permute-start | bytes 3145736 | tf_op jit(solution)/shard_map/ppermute | solution.py:220
  108.3 12.9 %collective-permute-start.2 = (bf16[3,128,256]{2,1,0:T(8,128)(2,1)S(1)}, bf16[3,128,256]{2,1,0:T(8,128)(2,1)S(1)}, u32[]{:S(2)}, u32[]{:S(2)}) collective-permute-start(bf16[3,128,256]{2,1,0:T(8,128)(2,1)S(1)} %get-tuple-element.22), channel_id=1, source_target_pairs={{0,480},{32,64},{64,32},{96,128},{128,96},{160,192},{192,160},{224... | collective-permute-start | bytes 589832 | tf_op jit(solution)/shard_map/ppermute | solution.py:119
  110.7 12.5 %collective-permute-start.4 = (bf16[3,128,256]{2,1,0:T(8,128)(2,1)S(1)}, bf16[3,128,256]{2,1,0:T(8,128)(2,1)S(1)}, u32[]{:S(2)}, u32[]{:S(2)}) collective-permute-start(bf16[3,128,256]{2,1,0:T(8,128)(2,1)S(1)} %get-tuple-element.24), channel_id=1, source_target_pairs={{0,32},{32,0},{64,96},{96,64},{128,160},{160,128},{192,224},{224,1... | collective-permute-start | bytes 589832 | tf_op jit(solution)/shard_map/ppermute | solution.py:115
  114.1 11.9 %collective-permute-start.6 = (bf16[3,128,256]{2,1,0:T(8,128)(2,1)S(1)}, bf16[3,128,256]{2,1,0:T(8,128)(2,1)S(1)}, u32[]{:S(2)}, u32[]{:S(2)}) collective-permute-start(bf16[3,128,256]{2,1,0:T(8,128)(2,1)S(1)} %get-tuple-element.26), channel_id=1, source_target_pairs={{0,480},{32,64},{64,32},{96,128},{128,96},{160,192},{192,160},{224... | collective-permute-start | bytes 589832 | tf_op jit(solution)/shard_map/ppermute | solution.py:119
  117.3 12.6 %collective-permute-start.8 = (bf16[3,128,256]{2,1,0:T(8,128)(2,1)S(1)}, bf16[3,128,256]{2,1,0:T(8,128)(2,1)S(1)}, u32[]{:S(2)}, u32[]{:S(2)}) collective-permute-start(bf16[3,128,256]{2,1,0:T(8,128)(2,1)S(1)} %get-tuple-element.28), channel_id=1, source_target_pairs={{0,32},{32,0},{64,96},{96,64},{128,160},{160,128},{192,224},{224,1... | collective-permute-start | bytes 589832 | tf_op jit(solution)/shard_map/ppermute | solution.py:115
  121.2 23.3 %collective-permute-start.3 = (bf16[3,128,256]{2,1,0:T(8,128)(2,1)S(1)}, bf16[3,128,256]{2,1,0:T(8,128)(2,1)S(1)}, u32[]{:S(2)}, u32[]{:S(2)}) collective-permute-start(bf16[3,128,256]{2,1,0:T(8,128)(2,1)S(1)} %add_convert_fusion.3), channel_id=1, source_target_pairs={{0,32},{32,0},{64,96},{96,64},{128,160},{160,128},{192,224},{224,1... | collective-permute-start | bytes 589832 | tf_op jit(solution)/shard_map/ppermute | solution.py:115
  123.2 21.2 %collective-permute-start.5 = (bf16[3,128,256]{2,1,0:T(8,128)(2,1)S(1)}, bf16[3,128,256]{2,1,0:T(8,128)(2,1)S(1)}, u32[]{:S(2)}, u32[]{:S(2)}) collective-permute-start(bf16[3,128,256]{2,1,0:T(8,128)(2,1)S(1)} %add_convert_fusion.2), channel_id=1, source_target_pairs={{0,480},{32,64},{64,32},{96,128},{128,96},{160,192},{192,160},{224... | collective-permute-start | bytes 589832 | tf_op jit(solution)/shard_map/ppermute | solution.py:119
  125.9 41.7 %copy-start.1 = (bf16[256,256]{1,0:T(8,128)(2,1)S(1)}, bf16[256,256]{1,0:T(8,128)(2,1)}, u32[]{:S(2)}) copy-start(bf16[256,256]{1,0:T(8,128)(2,1)} %state_ref.3) | copy-start | bytes 393220
  125.9 41.7 %copy-start.5 = (bf16[256,256]{1,0:T(8,128)(2,1)S(1)}, bf16[256,256]{1,0:T(8,128)(2,1)}, u32[]{:S(2)}) copy-start(bf16[256,256]{1,0:T(8,128)(2,1)} %agg_ref.3) | copy-start | bytes 393220
  126.0 41.7 %copy-start.6 = (bf16[256,256]{1,0:T(8,128)(2,1)S(1)}, bf16[256,256]{1,0:T(8,128)(2,1)}, u32[]{:S(2)}) copy-start(bf16[256,256]{1,0:T(8,128)(2,1)} %self_ref.3) | copy-start | bytes 393220
  126.0 41.7 %copy-start.7 = (bf16[256,256]{1,0:T(8,128)(2,1)S(1)}, bf16[256,256]{1,0:T(8,128)(2,1)}, u32[]{:S(2)}) copy-start(bf16[256,256]{1,0:T(8,128)(2,1)} %out_w_ref.3) | copy-start | bytes 393220
  126.0 41.7 %copy-start.13 = (f32[256]{0:T(256)S(1)}, f32[256]{0:T(256)}, u32[]{:S(2)}) copy-start(f32[256]{0:T(256)} %param.24) | copy-start | bytes 3076
  126.0 18.4 %collective-permute-start.7 = (bf16[3,128,256]{2,1,0:T(8,128)(2,1)S(1)}, bf16[3,128,256]{2,1,0:T(8,128)(2,1)S(1)}, u32[]{:S(2)}, u32[]{:S(2)}) collective-permute-start(bf16[3,128,256]{2,1,0:T(8,128)(2,1)S(1)} %add_convert_fusion.1), channel_id=1, source_target_pairs={{0,32},{32,0},{64,96},{96,64},{128,160},{160,128},{192,224},{224,1... | collective-permute-start | bytes 589832 | tf_op jit(solution)/shard_map/ppermute | solution.py:115
  129.9 14.5 %collective-permute-start.9 = (bf16[3,128,256]{2,1,0:T(8,128)(2,1)S(1)}, bf16[3,128,256]{2,1,0:T(8,128)(2,1)S(1)}, u32[]{:S(2)}, u32[]{:S(2)}) collective-permute-start(bf16[3,128,256]{2,1,0:T(8,128)(2,1)S(1)} %add_convert_fusion), channel_id=1, source_target_pairs={{0,480},{32,64},{64,32},{96,128},{128,96},{160,192},{192,160},{224... | collective-permute-start | bytes 589832 | tf_op jit(solution)/shard_map/ppermute | solution.py:119
  133.4 11.1 %collective-permute-start.11 = (bf16[2,128,256]{2,1,0:T(8,128)(2,1)S(1)}, bf16[2,128,256]{2,1,0:T(8,128)(2,1)S(1)}, u32[]{:S(2)}, u32[]{:S(2)}) collective-permute-start(bf16[2,128,256]{2,1,0:T(8,128)(2,1)S(1)} %get-tuple-element.29), channel_id=1, source_target_pairs={{0,96},{32,448},{64,160},{96,0},{128,224},{160,64},{192,288},{224,... | collective-permute-start | bytes 393224 | tf_op jit(solution)/shard_map/ppermute | solution.py:115
  144.7 17.2 %collective-permute-start.10 = (bf16[2,128,256]{2,1,0:T(8,128)(2,1)S(1)}, bf16[2,128,256]{2,1,0:T(8,128)(2,1)S(1)}, u32[]{:S(2)}, u32[]{:S(2)}) collective-permute-start(bf16[2,128,256]{2,1,0:T(8,128)(2,1)S(1)} %get-tuple-element.30), channel_id=1, source_target_pairs={{0,160},{32,384},{64,224},{96,448},{128,288},{160,0},{192,352},{22... | collective-permute-start | bytes 393224 | tf_op jit(solution)/shard_map/ppermute | solution.py:115
  150.5 17.1 %collective-permute-start.12 = (bf16[2,128,256]{2,1,0:T(8,128)(2,1)S(1)}, bf16[2,128,256]{2,1,0:T(8,128)(2,1)S(1)}, u32[]{:S(2)}, u32[]{:S(2)}) collective-permute-start(bf16[2,128,256]{2,1,0:T(8,128)(2,1)S(1)} %get-tuple-element.31), channel_id=1, source_target_pairs={{0,352},{32,192},{64,416},{96,256},{128,480},{160,320},{192,32},{2... | collective-permute-start | bytes 393224 | tf_op jit(solution)/shard_map/ppermute | solution.py:119

commit v9 on v8

--- a/solution.py
+++ b/solution.py
@@ -118,15 +118,16 @@
         pairs = [(i, (i - step if i % 2 == 0 else i + step) % rows) for i in range(rows)]
         return lax.ppermute(x, "row", pairs)
 
-    halves_a, halves_b = [], []
-    for half_a, half_b, next_a, next_b in zip(
-        two_a, (two_b0, two_b1), (one_a0, one_a1), (one_b0, one_b1)
-    ):
-        got_a, got_b = swap_a(half_a, 1), swap_b(half_b, 1)
-        halves_b.append(swap_b(add(next_b, got_a), 1))
-        halves_a.append(swap_a(add(next_a, got_b), 1))
+    two_a0, two_a1 = two_a
+    got_a0, got_b0 = swap_a(two_a0, 1), swap_b(two_b0, 1)
+    got_a1, got_b1 = swap_a(two_a1, 1), swap_b(two_b1, 1)
     opposite = swap_a(opposite, 3)
-    got_a, got_b = jnp.concatenate(halves_a, axis=0), jnp.concatenate(halves_b, axis=0)
+    one_b0, one_a0 = swap_b(add(one_b0, got_a0), 1), swap_a(add(one_a0, got_b0), 1)
+    one_b1 = swap_b(add(one_b1, got_a1), 1)
+    got_b1, opposite = lax.optimization_barrier((got_b1, opposite))
+    one_a1 = swap_a(add(one_a1, got_b1), 1)
+    got_a = jnp.concatenate([one_a0, one_a1], axis=0)
+    got_b = jnp.concatenate([one_b0, one_b1], axis=0)
     mine = add(own[:2], got_a[:2], got_b[:2])
     far_a = add(own[2:4], got_a[4:6], got_b[2:4])
     far_b = add(own[4:6], got_a[2:4], got_b[4:6], opposite)

time: 169 us -> 167 us (0.988)
  waiting for transfers between devices: 26.7 us -> 22.6 us
  starting transfers between devices: 41.2 us -> 43 us
    ppermute x6, waiting for transfers between devices: 15.6 us -> 7.37 us  [swap_a(): return lax.ppermute(x, 'row', pairs)]
    ppermute x5, waiting for transfers between devices: 5.79 us -> 9.93 us  [swap_b(): return lax.ppermute(x, 'row', pairs)]
  transfers between devices with their start and end apart: 13 -> 13, of which waited for: 5 -> 7; matrix products, arithmetic and copies ran while one was open for 0% -> 0% of each run, Pallas kernels for 0% -> 0%
where the time goes in v9:
time: 167 us; the launch traced here: 166 us
  blocking collectives  91.6 us (55%)
  starting transfers between devices  43 us (26%)
  waiting for transfers between devices  22.6 us (14%)
  Pallas kernels  5.85 us (4%)
  other arithmetic  2.01 us (1%)
    all_gather x1, blocking collectives, gather_rows(): got = lax.all_gather(sent, 'row', axis=0, tiled=True)  47.7 us
    all_to_all x1, blocking collectives, on_device(): lax.all_to_all(own, 'col', 0, 0, tiled=True, axis_index_groups=same_core)  24.3 us
    ppermute x6, starting transfers between devices, swap_a(): return lax.ppermute(x, 'row', pairs)  24.2 us
    all_to_all x1, blocking collectives, on_device(): lax.all_to_all(link_copies, 'col', 0, 0, tiled=True, axis_index_groups=sa...  19.6 us
    ppermute x5, starting transfers between devices, swap_b(): return lax.ppermute(x, 'row', pairs)  15 us
    ppermute x5, waiting for transfers between devices, swap_b(): return lax.ppermute(x, 'row', pairs)  9.93 us
    ppermute x6, waiting for transfers between devices, swap_a(): return lax.ppermute(x, 'row', pairs)  7.37 us
  transfers between devices with their start and end apart: 13, of which 7 were waited for; matrix products, arithmetic and copies ran while one was open for 0% of the time, Pallas kernels for 0%

profile of v9, /device:TPU:32, one launch (start us, length us, event | category | flops | bytes accessed | tf_op | source)
XLA Modules:
  0.0 166.5 jit_solution(11496164706150153463)
XLA Ops:
  0.6 0.9 multiply_convert_fusion.1
  1.6 47.7 %all-gather.1 = f16[4096,256]{1,0:T(8,128)(2,1)S(1)} all-gather(f16[256,256]{1,0:T(8,128)(2,1)S(1)} %multiply_convert_fusion.1), channel_id=1, replica_groups=mesh['row'=16,'col'=32] {'row'}, dimensions={0}, use_global_device_ids=true | all-gather | bytes 2228224 | tf_op jit(solution)/shard_map/all_gather | solution.py:234
  49.3 0.6 multiply_convert_fusion
  50.0 0.5 copy-done
  50.4 1.6 link_products.1
  52.0 1.9 %collective-permute-start = (bf16[16,128,256]{2,1,0:T(8,128)(2,1)S(1)}, bf16[16,128,256]{2,1,0:T(8,128)(2,1)S(1)}, u32[]{:S(2)}, u32[]{:S(2)}) collective-permute-start(bf16[16,128,256]{2,1,0:T(8,128)(2,1)S(1)} %get-tuple-element.19), channel_id=1, source_target_pairs={{0,1},{1,0},{2,3},{3,2},{4,5},{5,4},{6,7},{7,6},{8,9},{9,8},{10,11... | collective-permute-start | bytes 3145736 | tf_op jit(solution)/shard_map/ppermute | solution.py:215
  54.0 2.6 %collective-permute-done.b_ref = bf16[16,128,256]{2,1,0:T(8,128)(2,1)S(1)} collective-permute-done((bf16[16,128,256]{2,1,0:T(8,128)(2,1)S(1)}, bf16[16,128,256]{2,1,0:T(8,128)(2,1)S(1)}, u32[]{:S(2)}, u32[]{:S(2)}) %collective-permute-start) | collective-permute-done | bytes 1048608 | tf_op jit(solution)/shard_map/ppermute | solution.py:215
  56.6 0.2 add_two.1
  56.9 24.3 %all_to_all.10.parts_ref = bf16[16,128,256]{2,1,0:T(8,128)(2,1)S(1)} all-to-all(bf16[16,128,256]{2,1,0:T(8,128)(2,1)S(1)} %add_two.1), channel_id=1, replica_groups={{0,2,4,6,8,10,12,14,16,18,20,22,24,26,28,30},{1,3,5,7,9,11,13,15,17,19,..., dimensions={0} | all-to-all | bytes 2097152 | tf_op jit(solution)/shard_map/all_to_all | solution.py:216
  81.2 1.2 link_update.1
  82.3 19.6 %all_to_all.11.own_ref = bf16[16,128,256]{2,1,0:T(8,128)(2,1)S(1)} all-to-all(bf16[16,128,256]{2,1,0:T(8,128)(2,1)S(1)} %get-tuple-element.21), channel_id=1, replica_groups={{0,2,4,6,8,10,12,14,16,18,20,22,24,26,28,30},{1,3,5,7,9,11,13,15,17,19,..., dimensions={0} | all-to-all | bytes 2097152 | tf_op jit(solution)/shard_map/all_to_all | solution.py:220
  101.9 1.9 %collective-permute-start.1 = (bf16[16,128,256]{2,1,0:T(8,128)(2,1)S(1)}, bf16[16,128,256]{2,1,0:T(8,128)(2,1)S(1)}, u32[]{:S(2)}, u32[]{:S(2)}) collective-permute-start(bf16[16,128,256]{2,1,0:T(8,128)(2,1)S(1)} %all_to_all.11.own_ref), channel_id=1, source_target_pairs={{0,1},{1,0},{2,3},{3,2},{4,5},{5,4},{6,7},{7,6},{8,9},{9,8},{10,11... | collective-permute-start | bytes 3145736 | tf_op jit(solution)/shard_map/ppermute | solution.py:221
  103.8 2.6 %collective-permute-done.1.other_ref = bf16[16,128,256]{2,1,0:T(8,128)(2,1)S(1)} collective-permute-done((bf16[16,128,256]{2,1,0:T(8,128)(2,1)S(1)}, bf16[16,128,256]{2,1,0:T(8,128)(2,1)S(1)}, u32[]{:S(2)}, u32[]{:S(2)}) %collective-permute-start.1) | collective-permute-done | bytes 1048608 | tf_op jit(solution)/shard_map/ppermute | solution.py:221
  106.5 1.8 %flow_products.1 = (bf16[6,128,256]{2,1,0:T(8,128)(2,1)S(1)}, bf16[3,128,256]{2,1,0:T(8,128)(2,1)S(1)}, bf16[3,128,256]{2,1,0:T(8,128)(2,1)S(1)}, bf16[3,128,256...) custom-call(s32[2]{0:T(128)S(1)} %pad_add_fusion.me_ref, ...), custom_call_target="tpu_custom_call" | custom-call | tf_op jit(solution)/shard_map/flow_products/pallas_call | solution.py:87
  108.3 2.4 %collective-permute-start.2 = (bf16[3,128,256]{2,1,0:T(8,128)(2,1)S(1)}, bf16[3,128,256]{2,1,0:T(8,128)(2,1)S(1)}, u32[]{:S(2)}, u32[]{:S(2)}) collective-permute-start(bf16[3,128,256]{2,1,0:T(8,128)(2,1)S(1)} %get-tuple-element.24), channel_id=1, source_target_pairs={{0,480},{32,64},{64,32},{96,128},{128,96},{160,192},{192,160},{224... | collective-permute-start | bytes 589832 | tf_op jit(solution)/shard_map/ppermute | solution.py:119
  110.7 5.5 %collective-permute-start.7 = (bf16[2,128,256]{2,1,0:T(8,128)(2,1)S(1)}, bf16[2,128,256]{2,1,0:T(8,128)(2,1)S(1)}, u32[]{:S(2)}, u32[]{:S(2)}) collective-permute-start(bf16[2,128,256]{2,1,0:T(8,128)(2,1)S(1)} %get-tuple-element.29), channel_id=1, source_target_pairs={{0,96},{32,448},{64,160},{96,0},{128,224},{160,64},{192,288},{224,... | collective-permute-start | bytes 393224 | tf_op jit(solution)/shard_map/ppermute | solution.py:115
  116.2 2.0 %collective-permute-start.4 = (bf16[3,128,256]{2,1,0:T(8,128)(2,1)S(1)}, bf16[3,128,256]{2,1,0:T(8,128)(2,1)S(1)}, u32[]{:S(2)}, u32[]{:S(2)}) collective-permute-start(bf16[3,128,256]{2,1,0:T(8,128)(2,1)S(1)} %get-tuple-element.26), channel_id=1, source_target_pairs={{0,32},{32,0},{64,96},{96,64},{128,160},{160,128},{192,224},{224,1... | collective-permute-start | bytes 589832 | tf_op jit(solution)/shard_map/ppermute | solution.py:115
  118.1 2.7 %collective-permute-start.6 = (bf16[3,128,256]{2,1,0:T(8,128)(2,1)S(1)}, bf16[3,128,256]{2,1,0:T(8,128)(2,1)S(1)}, u32[]{:S(2)}, u32[]{:S(2)}) collective-permute-start(bf16[3,128,256]{2,1,0:T(8,128)(2,1)S(1)} %get-tuple-element.28), channel_id=1, source_target_pairs={{0,480},{32,64},{64,32},{96,128},{128,96},{160,192},{192,160},{224... | collective-permute-start | bytes 589832 | tf_op jit(solution)/shard_map/ppermute | solution.py:119
  120.8 3.7 %collective-permute-start.9 = (bf16[3,128,256]{2,1,0:T(8,128)(2,1)S(1)}, bf16[3,128,256]{2,1,0:T(8,128)(2,1)S(1)}, u32[]{:S(2)}, u32[]{:S(2)}) collective-permute-start(bf16[3,128,256]{2,1,0:T(8,128)(2,1)S(1)} %get-tuple-element.32), channel_id=1, source_target_pairs={{0,32},{32,0},{64,96},{96,64},{128,160},{160,128},{192,224},{224,1... | collective-permute-start | bytes 589832 | tf_op jit(solution)/shard_map/ppermute | solution.py:115
  124.6 2.2 %collective-permute-start.3 = (bf16[3,128,256]{2,1,0:T(8,128)(2,1)S(1)}, bf16[3,128,256]{2,1,0:T(8,128)(2,1)S(1)}, u32[]{:S(2)}, u32[]{:S(2)}) collective-permute-start(bf16[3,128,256]{2,1,0:T(8,128)(2,1)S(1)} %add_convert_fusion.3), channel_id=1, source_target_pairs={{0,32},{32,0},{64,96},{96,64},{128,160},{160,128},{192,224},{224,1... | collective-permute-start | bytes 589832 | tf_op jit(solution)/shard_map/ppermute | solution.py:115
  126.8 0.8 collective-permute-done.4
  127.6 2.4 %collective-permute-start.5 = (bf16[3,128,256]{2,1,0:T(8,128)(2,1)S(1)}, bf16[3,128,256]{2,1,0:T(8,128)(2,1)S(1)}, u32[]{:S(2)}, u32[]{:S(2)}) collective-permute-start(bf16[3,128,256]{2,1,0:T(8,128)(2,1)S(1)} %add_convert_fusion.2), channel_id=1, source_target_pairs={{0,480},{32,64},{64,32},{96,128},{128,96},{160,192},{192,160},{224... | collective-permute-start | bytes 589832 | tf_op jit(solution)/shard_map/ppermute | solution.py:119
  130.1 5.2 %collective-permute-start.8 = (bf16[3,128,256]{2,1,0:T(8,128)(2,1)S(1)}, bf16[3,128,256]{2,1,0:T(8,128)(2,1)S(1)}, u32[]{:S(2)}, u32[]{:S(2)}) collective-permute-start(bf16[3,128,256]{2,1,0:T(8,128)(2,1)S(1)} %add_convert_fusion.1), channel_id=1, source_target_pairs={{0,32},{32,0},{64,96},{96,64},{128,160},{160,128},{192,224},{224,1... | collective-permute-start | bytes 589832 | tf_op jit(solution)/shard_map/ppermute | solution.py:115
  135.4 1.9 %collective-permute-start.10 = (bf16[3,128,256]{2,1,0:T(8,128)(2,1)S(1)}, bf16[3,128,256]{2,1,0:T(8,128)(2,1)S(1)}, u32[]{:S(2)}, u32[]{:S(2)}) collective-permute-start(bf16[3,128,256]{2,1,0:T(8,128)(2,1)S(1)} %add_convert_fusion), channel_id=1, source_target_pairs={{0,480},{32,64},{64,32},{96,128},{128,96},{160,192},{192,160},{224... | collective-permute-start | bytes 589832 | tf_op jit(solution)/shard_map/ppermute | solution.py:119
  137.4 1.7 %collective-permute-done.8 = bf16[3,128,256]{2,1,0:T(8,128)(2,1)S(1)} collective-permute-done((bf16[3,128,256]{2,1,0:T(8,128)(2,1)S(1)}, bf16[3,128,256]{2,1,0:T(8,128)(2,1)S(1)}, u32[]{:S(2)}, u32[]{:S(2)}) %collective-permute-start.8) | collective-permute-done | bytes 196640 | tf_op jit(solution)/shard_map/ppermute | solution.py:115
  139.1 3.9 %collective-permute-done.10 = bf16[3,128,256]{2,1,0:T(8,128)(2,1)S(1)} collective-permute-done((bf16[3,128,256]{2,1,0:T(8,128)(2,1)S(1)}, bf16[3,128,256]{2,1,0:T(8,128)(2,1)S(1)}, u32[]{:S(2)}, u32[]{:S(2)}) %collective-permute-start.10) | collective-permute-done | bytes 196640 | tf_op jit(solution)/shard_map/ppermute | solution.py:119
  143.0 0.2 add_convert_fusion.5
  143.2 5.7 %collective-permute-start.11 = (bf16[2,128,256]{2,1,0:T(8,128)(2,1)S(1)}, bf16[2,128,256]{2,1,0:T(8,128)(2,1)S(1)}, u32[]{:S(2)}, u32[]{:S(2)}) collective-permute-start(bf16[2,128,256]{2,1,0:T(8,128)(2,1)S(1)} %get-tuple-element.34), channel_id=1, source_target_pairs={{0,160},{32,384},{64,224},{96,448},{128,288},{160,0},{192,352},{22... | collective-permute-start | bytes 393224 | tf_op jit(solution)/shard_map/ppermute | solution.py:115
  148.8 5.6 %collective-permute-start.12 = (bf16[2,128,256]{2,1,0:T(8,128)(2,1)S(1)}, bf16[2,128,256]{2,1,0:T(8,128)(2,1)S(1)}, u32[]{:S(2)}, u32[]{:S(2)}) collective-permute-start(bf16[2,128,256]{2,1,0:T(8,128)(2,1)S(1)} %get-tuple-element.35), channel_id=1, source_target_pairs={{0,352},{32,192},{64,416},{96,256},{128,480},{160,320},{192,32},{2... | collective-permute-start | bytes 393224 | tf_op jit(solution)/shard_map/ppermute | solution.py:119
  154.4 4.8 %collective-permute-done.11 = bf16[2,128,256]{2,1,0:T(8,128)(2,1)S(1)} collective-permute-done((bf16[2,128,256]{2,1,0:T(8,128)(2,1)S(1)}, bf16[2,128,256]{2,1,0:T(8,128)(2,1)S(1)}, u32[]{:S(2)}, u32[]{:S(2)}) %collective-permute-start.11) | collective-permute-done | bytes 131104 | tf_op jit(solution)/shard_map/ppermute | solution.py:115
  159.3 6.0 %collective-permute-done.12 = bf16[2,128,256]{2,1,0:T(8,128)(2,1)S(1)} collective-permute-done((bf16[2,128,256]{2,1,0:T(8,128)(2,1)S(1)}, bf16[2,128,256]{2,1,0:T(8,128)(2,1)S(1)}, u32[]{:S(2)}, u32[]{:S(2)}) %collective-permute-start.12) | collective-permute-done | bytes 131104 | tf_op jit(solution)/shard_map/ppermute | solution.py:119
  165.4 1.1 flow_update.1
  (39 shorter events, 0.4 us)
Async XLA Ops:
  49.3 1.1 copy-start
  49.3 1.1 copy-start.9
  49.3 1.1 copy-start.10
  49.3 1.1 copy-start.11
  52.0 4.6 %collective-permute-start = (bf16[16,128,256]{2,1,0:T(8,128)(2,1)S(1)}, bf16[16,128,256]{2,1,0:T(8,128)(2,1)S(1)}, u32[]{:S(2)}, u32[]{:S(2)}) collective-permute-start(bf16[16,128,256]{2,1,0:T(8,128)(2,1)S(1)} %get-tuple-element.19), channel_id=1, source_target_pairs={{0,1},{1,0},{2,3},{3,2},{4,5},{5,4},{6,7},{7,6},{8,9},{9,8},{10,11... | collective-permute-start | bytes 3145736 | tf_op jit(solution)/shard_map/ppermute | solution.py:215
  56.6 24.6 %copy-start.2 = (bf16[256,256]{1,0:T(8,128)(2,1)S(1)}, bf16[256,256]{1,0:T(8,128)(2,1)}, u32[]{:S(2)}) copy-start(bf16[256,256]{1,0:T(8,128)(2,1)} %agg_ref.2) | copy-start | bytes 393220
  56.6 24.6 %copy-start.3 = (bf16[256,256]{1,0:T(8,128)(2,1)S(1)}, bf16[256,256]{1,0:T(8,128)(2,1)}, u32[]{:S(2)}) copy-start(bf16[256,256]{1,0:T(8,128)(2,1)} %self_ref.2) | copy-start | bytes 393220
  56.6 24.6 %copy-start.4 = (bf16[256,256]{1,0:T(8,128)(2,1)S(1)}, bf16[256,256]{1,0:T(8,128)(2,1)}, u32[]{:S(2)}) copy-start(bf16[256,256]{1,0:T(8,128)(2,1)} %out_w_ref.2) | copy-start | bytes 393220
  56.6 24.6 %copy-start.8 = (bf16[128,256]{1,0:T(8,128)(2,1)S(1)}, bf16[128,256]{1,0:T(8,128)(2,1)}, u32[]{:S(2)}) copy-start(bf16[128,256]{1,0:T(8,128)(2,1)} %state_ref.2) | copy-start | bytes 196612
  56.6 24.6 %copy-start.12 = (f32[256]{0:T(256)S(1)}, f32[256]{0:T(256)}, u32[]{:S(2)}) copy-start(f32[256]{0:T(256)} %param.20) | copy-start | bytes 3076
  101.9 4.5 %collective-permute-start.1 = (bf16[16,128,256]{2,1,0:T(8,128)(2,1)S(1)}, bf16[16,128,256]{2,1,0:T(8,128)(2,1)S(1)}, u32[]{:S(2)}, u32[]{:S(2)}) collective-permute-start(bf16[16,128,256]{2,1,0:T(8,128)(2,1)S(1)} %all_to_all.11.own_ref), channel_id=1, source_target_pairs={{0,1},{1,0},{2,3},{3,2},{4,5},{5,4},{6,7},{7,6},{8,9},{9,8},{10,11... | collective-permute-start | bytes 3145736 | tf_op jit(solution)/shard_map/ppermute | solution.py:221
  108.3 16.3 %collective-permute-start.2 = (bf16[3,128,256]{2,1,0:T(8,128)(2,1)S(1)}, bf16[3,128,256]{2,1,0:T(8,128)(2,1)S(1)}, u32[]{:S(2)}, u32[]{:S(2)}) collective-permute-start(bf16[3,128,256]{2,1,0:T(8,128)(2,1)S(1)} %get-tuple-element.24), channel_id=1, source_target_pairs={{0,480},{32,64},{64,32},{96,128},{128,96},{160,192},{192,160},{224... | collective-permute-start | bytes 589832 | tf_op jit(solution)/shard_map/ppermute | solution.py:119
  110.7 19.3 %collective-permute-start.7 = (bf16[2,128,256]{2,1,0:T(8,128)(2,1)S(1)}, bf16[2,128,256]{2,1,0:T(8,128)(2,1)S(1)}, u32[]{:S(2)}, u32[]{:S(2)}) collective-permute-start(bf16[2,128,256]{2,1,0:T(8,128)(2,1)S(1)} %get-tuple-element.29), channel_id=1, source_target_pairs={{0,96},{32,448},{64,160},{96,0},{128,224},{160,64},{192,288},{224,... | collective-permute-start | bytes 393224 | tf_op jit(solution)/shard_map/ppermute | solution.py:115
  116.2 11.4 %collective-permute-start.4 = (bf16[3,128,256]{2,1,0:T(8,128)(2,1)S(1)}, bf16[3,128,256]{2,1,0:T(8,128)(2,1)S(1)}, u32[]{:S(2)}, u32[]{:S(2)}) collective-permute-start(bf16[3,128,256]{2,1,0:T(8,128)(2,1)S(1)} %get-tuple-element.26), channel_id=1, source_target_pairs={{0,32},{32,0},{64,96},{96,64},{128,160},{160,128},{192,224},{224,1... | collective-permute-start | bytes 589832 | tf_op jit(solution)/shard_map/ppermute | solution.py:115
  118.1 11.9 %collective-permute-start.6 = (bf16[3,128,256]{2,1,0:T(8,128)(2,1)S(1)}, bf16[3,128,256]{2,1,0:T(8,128)(2,1)S(1)}, u32[]{:S(2)}, u32[]{:S(2)}) collective-permute-start(bf16[3,128,256]{2,1,0:T(8,128)(2,1)S(1)} %get-tuple-element.28), channel_id=1, source_target_pairs={{0,480},{32,64},{64,32},{96,128},{128,96},{160,192},{192,160},{224... | collective-permute-start | bytes 589832 | tf_op jit(solution)/shard_map/ppermute | solution.py:119
  120.8 14.5 %collective-permute-start.9 = (bf16[3,128,256]{2,1,0:T(8,128)(2,1)S(1)}, bf16[3,128,256]{2,1,0:T(8,128)(2,1)S(1)}, u32[]{:S(2)}, u32[]{:S(2)}) collective-permute-start(bf16[3,128,256]{2,1,0:T(8,128)(2,1)S(1)} %get-tuple-element.32), channel_id=1, source_target_pairs={{0,32},{32,0},{64,96},{96,64},{128,160},{160,128},{192,224},{224,1... | collective-permute-start | bytes 589832 | tf_op jit(solution)/shard_map/ppermute | solution.py:115
  124.6 12.8 %collective-permute-start.3 = (bf16[3,128,256]{2,1,0:T(8,128)(2,1)S(1)}, bf16[3,128,256]{2,1,0:T(8,128)(2,1)S(1)}, u32[]{:S(2)}, u32[]{:S(2)}) collective-permute-start(bf16[3,128,256]{2,1,0:T(8,128)(2,1)S(1)} %add_convert_fusion.3), channel_id=1, source_target_pairs={{0,32},{32,0},{64,96},{96,64},{128,160},{160,128},{192,224},{224,1... | collective-permute-start | bytes 589832 | tf_op jit(solution)/shard_map/ppermute | solution.py:115
  127.6 9.7 %collective-permute-start.5 = (bf16[3,128,256]{2,1,0:T(8,128)(2,1)S(1)}, bf16[3,128,256]{2,1,0:T(8,128)(2,1)S(1)}, u32[]{:S(2)}, u32[]{:S(2)}) collective-permute-start(bf16[3,128,256]{2,1,0:T(8,128)(2,1)S(1)} %add_convert_fusion.2), channel_id=1, source_target_pairs={{0,480},{32,64},{64,32},{96,128},{128,96},{160,192},{192,160},{224... | collective-permute-start | bytes 589832 | tf_op jit(solution)/shard_map/ppermute | solution.py:119
  130.0 35.3 %copy-start.1 = (bf16[256,256]{1,0:T(8,128)(2,1)S(1)}, bf16[256,256]{1,0:T(8,128)(2,1)}, u32[]{:S(2)}) copy-start(bf16[256,256]{1,0:T(8,128)(2,1)} %state_ref.3) | copy-start | bytes 393220
  130.0 35.3 %copy-start.5 = (bf16[256,256]{1,0:T(8,128)(2,1)S(1)}, bf16[256,256]{1,0:T(8,128)(2,1)}, u32[]{:S(2)}) copy-start(bf16[256,256]{1,0:T(8,128)(2,1)} %agg_ref.3) | copy-start | bytes 393220
  130.1 35.3 %copy-start.6 = (bf16[256,256]{1,0:T(8,128)(2,1)S(1)}, bf16[256,256]{1,0:T(8,128)(2,1)}, u32[]{:S(2)}) copy-start(bf16[256,256]{1,0:T(8,128)(2,1)} %self_ref.3) | copy-start | bytes 393220
  130.1 35.3 %copy-start.7 = (bf16[256,256]{1,0:T(8,128)(2,1)S(1)}, bf16[256,256]{1,0:T(8,128)(2,1)}, u32[]{:S(2)}) copy-start(bf16[256,256]{1,0:T(8,128)(2,1)} %out_w_ref.3) | copy-start | bytes 393220
  130.1 35.3 %copy-start.13 = (f32[256]{0:T(256)S(1)}, f32[256]{0:T(256)}, u32[]{:S(2)}) copy-start(f32[256]{0:T(256)} %param.24) | copy-start | bytes 3076
  130.1 9.0 %collective-permute-start.8 = (bf16[3,128,256]{2,1,0:T(8,128)(2,1)S(1)}, bf16[3,128,256]{2,1,0:T(8,128)(2,1)S(1)}, u32[]{:S(2)}, u32[]{:S(2)}) collective-permute-start(bf16[3,128,256]{2,1,0:T(8,128)(2,1)S(1)} %add_convert_fusion.1), channel_id=1, source_target_pairs={{0,32},{32,0},{64,96},{96,64},{128,160},{160,128},{192,224},{224,1... | collective-permute-start | bytes 589832 | tf_op jit(solution)/shard_map/ppermute | solution.py:115
  135.4 7.6 %collective-permute-start.10 = (bf16[3,128,256]{2,1,0:T(8,128)(2,1)S(1)}, bf16[3,128,256]{2,1,0:T(8,128)(2,1)S(1)}, u32[]{:S(2)}, u32[]{:S(2)}) collective-permute-start(bf16[3,128,256]{2,1,0:T(8,128)(2,1)S(1)} %add_convert_fusion), channel_id=1, source_target_pairs={{0,480},{32,64},{64,32},{96,128},{128,96},{160,192},{192,160},{224... | collective-permute-start | bytes 589832 | tf_op jit(solution)/shard_map/ppermute | solution.py:119
  143.2 16.1 %collective-permute-start.11 = (bf16[2,128,256]{2,1,0:T(8,128)(2,1)S(1)}, bf16[2,128,256]{2,1,0:T(8,128)(2,1)S(1)}, u32[]{:S(2)}, u32[]{:S(2)}) collective-permute-start(bf16[2,128,256]{2,1,0:T(8,128)(2,1)S(1)} %get-tuple-element.34), channel_id=1, source_target_pairs={{0,160},{32,384},{64,224},{96,448},{128,288},{160,0},{192,352},{22... | collective-permute-start | bytes 393224 | tf_op jit(solution)/shard_map/ppermute | solution.py:115
  148.8 16.4 %collective-permute-start.12 = (bf16[2,128,256]{2,1,0:T(8,128)(2,1)S(1)}, bf16[2,128,256]{2,1,0:T(8,128)(2,1)S(1)}, u32[]{:S(2)}, u32[]{:S(2)}) collective-permute-start(bf16[2,128,256]{2,1,0:T(8,128)(2,1)S(1)} %get-tuple-element.35), channel_id=1, source_target_pairs={{0,352},{32,192},{64,416},{96,256},{128,480},{160,320},{192,32},{2... | collective-permute-start | bytes 393224 | tf_op jit(solution)/shard_map/ppermute | solution.py:119

commit v10 on v7

--- a/solution.py
+++ b/solution.py
@@ -49,7 +49,7 @@
     )(me, flow, link, live, coefs, pieces)
 
 
-ROW_ORDER = (0, 5, -5, 2, 7, -3, -2, -7, 3, 1, 6, -4, -1, -6, 4, 8)
+ROW_ORDER = (0, 3, 6, -3, -6, 1, 4, 7, -2, -5, -1, -4, -7, 2, 5, 8)
 
 
 def flow_products_kernel(
@@ -83,7 +83,7 @@
 
 def flow_products(me, flow, link, live, coefs, own, other, blocks):
     assert blocks == 2 * len(ROW_ORDER)
-    counts = [6] * 5 + [2]
+    counts = [10, 10, 10, 2]
     return pl.pallas_call(
         flow_products_kernel,
         out_shape=[jax.ShapeDtypeStruct((count, BS, H), BF16) for count in counts],
@@ -106,7 +106,9 @@
     return total.astype(BF16)
 
 
-def sum_over_rows(own, two_a, two_b, one_a, one_b, opposite, rows):
+def sum_over_rows(own, for_a, for_b, opposite):
+    rows = len(ROW_ORDER)
+
     def swap_a(x, step):
         pairs = [(i, (i + step if i % 2 == 0 else i - step) % rows) for i in range(rows)]
         return lax.ppermute(x, "row", pairs)
@@ -115,15 +117,16 @@
         pairs = [(i, (i - step if i % 2 == 0 else i + step) % rows) for i in range(rows)]
         return lax.ppermute(x, "row", pairs)
 
-    got_a, got_b = swap_a(two_a, 1), swap_b(two_b, 1)
-    opposite = swap_a(opposite, 3)
-    got_a, got_b, opposite = lax.optimization_barrier((got_a, got_b, opposite))
-    one_b, one_a = add(one_b, got_a), add(one_a, got_b)
-    got_a, got_b = swap_a(one_a, 1), swap_b(one_b, 1)
+    got_a, got_b = swap_a(for_a, 1), swap_b(for_b, 1)
+    opposite = swap_a(opposite, 2)
+    six_a = add(own[4:6], got_a[8:10], got_b[4:6], opposite)
+    six_b = add(own[8:10], got_a[4:6], got_b[8:10])
     mine = add(own[:2], got_a[:2], got_b[:2])
-    far_a = add(own[2:4], got_a[4:6], got_b[2:4])
-    far_b = add(own[4:6], got_a[2:4], got_b[4:6], opposite)
-    got_a, got_b = swap_a(far_a, 5), swap_b(far_b, 5)
+    three_a = own[2:4].astype(F32) + got_a[6:8].astype(F32) + got_b[2:4].astype(F32)
+    three_b = own[6:8].astype(F32) + got_a[2:4].astype(F32) + got_b[6:8].astype(F32)
+    got_a, got_b = swap_a(six_a, 3), swap_b(six_b, 3)
+    three_b, three_a = add(three_b, got_a), add(three_a, got_b)
+    got_a, got_b = swap_a(three_a, 3), swap_b(three_b, 3)
     return jnp.stack([x.reshape(2 * BS, H) for x in (mine, got_a, got_b)])
 
 
@@ -214,7 +217,7 @@
     parts = flow_products(
         me, tile_flow, tile_link, tile_live, coefs, own, other, flow_blocks
     )
-    flow_parts = sum_over_rows(*parts, rows)
+    flow_parts = sum_over_rows(*parts)
     (flow_next,) = update(
         flow_parts, flow_state, flow_gain, flow_agg_weight, flow_self_weight, flow_out_weight, 0
     )

time: 170 us -> 169 us (level)
  the two profiles are of different devices: /device:TPU:32 before, /device:TPU:35 now
where the time goes in v10:
time: 169 us
  blocking collectives  82.3 us (49%)
  starting transfers between devices  40 us (24%)
  waiting for transfers between devices  37.2 us (22%)
  Pallas kernels  5.85 us (3%)
  other arithmetic  1.95 us (1%)
    all_gather x1, blocking collectives, gather_rows(): got = lax.all_gather(sent, 'row', axis=0, tiled=True)  41.2 us
    all_to_all x1, blocking collectives, on_device(): lax.all_to_all(own, 'col', 0, 0, tiled=True, axis_index_groups=same_core)  21.9 us
    ppermute x4, waiting for transfers between devices, swap_a(): return lax.ppermute(x, 'row', pairs)  19.6 us
    all_to_all x1, blocking collectives, on_device(): lax.all_to_all(link_copies, 'col', 0, 0, tiled=True, axis_index_groups=sa...  19.1 us
    ppermute x4, starting transfers between devices, swap_a(): return lax.ppermute(x, 'row', pairs)  18.1 us
    ppermute x3, waiting for transfers between devices, swap_b(): return lax.ppermute(x, 'row', pairs)  13.1 us
    ppermute x1, starting transfers between devices, on_device(): own = add_two(own, lax.ppermute(other, 'col', sibling))  9.08 us
    ppermute x3, starting transfers between devices, swap_b(): return lax.ppermute(x, 'row', pairs)  8.64 us
  transfers between devices with their start and end apart: 9, of which 8 were waited for; matrix products, arithmetic and copies ran while one was open for 0% of the time, Pallas kernels for 0%

profile of v10, /device:TPU:35, one launch (start us, length us, event | category | flops | bytes accessed | tf_op | source)
XLA Modules:
  0.0 168.8 jit_solution(6665852527587229677)
XLA Ops:
  0.6 0.9 multiply_convert_fusion.1
  1.6 41.2 %all-gather.1 = f16[4096,256]{1,0:T(8,128)(2,1)S(1)} all-gather(f16[256,256]{1,0:T(8,128)(2,1)S(1)} %multiply_convert_fusion.1), channel_id=1, replica_groups=mesh['row'=16,'col'=32] {'row'}, dimensions={0}, use_global_device_ids=true | all-gather | bytes 2228224 | tf_op jit(solution)/shard_map/all_gather | solution.py:229
  42.8 0.6 multiply_convert_fusion
  43.4 0.1 pad_add_fusion.me_ref
  43.5 0.5 copy-done
  44.0 1.6 link_products.1
  45.6 9.1 %collective-permute-start = (bf16[16,128,256]{2,1,0:T(8,128)(2,1)S(1)}, bf16[16,128,256]{2,1,0:T(8,128)(2,1)S(1)}, u32[]{:S(2)}, u32[]{:S(2)}) collective-permute-start(bf16[16,128,256]{2,1,0:T(8,128)(2,1)S(1)} %get-tuple-element.11), channel_id=1, source_target_pairs={{0,1},{1,0},{2,3},{3,2},{4,5},{5,4},{6,7},{7,6},{8,9},{9,8},{10,11... | collective-permute-start | bytes 3145736 | tf_op jit(solution)/shard_map/ppermute | solution.py:210
  54.6 2.3 %collective-permute-done.b_ref = bf16[16,128,256]{2,1,0:T(8,128)(2,1)S(1)} collective-permute-done((bf16[16,128,256]{2,1,0:T(8,128)(2,1)S(1)}, bf16[16,128,256]{2,1,0:T(8,128)(2,1)S(1)}, u32[]{:S(2)}, u32[]{:S(2)}) %collective-permute-start) | collective-permute-done | bytes 1048608 | tf_op jit(solution)/shard_map/ppermute | solution.py:210
  56.9 0.2 add_two.1
  57.2 21.9 %all_to_all.10.parts_ref = bf16[16,128,256]{2,1,0:T(8,128)(2,1)S(1)} all-to-all(bf16[16,128,256]{2,1,0:T(8,128)(2,1)S(1)} %add_two.1), channel_id=1, replica_groups={{0,2,4,6,8,10,12,14,16,18,20,22,24,26,28,30},{1,3,5,7,9,11,13,15,17,19,..., dimensions={0} | all-to-all | bytes 2097152 | tf_op jit(solution)/shard_map/all_to_all | solution.py:211
  79.1 1.2 link_update.1
  80.3 19.1 %all_to_all.11.own_ref = bf16[16,128,256]{2,1,0:T(8,128)(2,1)S(1)} all-to-all(bf16[16,128,256]{2,1,0:T(8,128)(2,1)S(1)} %get-tuple-element.13), channel_id=1, replica_groups={{0,2,4,6,8,10,12,14,16,18,20,22,24,26,28,30},{1,3,5,7,9,11,13,15,17,19,..., dimensions={0} | all-to-all | bytes 2097152 | tf_op jit(solution)/shard_map/all_to_all | solution.py:215
  99.4 4.2 %collective-permute-start.1 = (bf16[16,128,256]{2,1,0:T(8,128)(2,1)S(1)}, bf16[16,128,256]{2,1,0:T(8,128)(2,1)S(1)}, u32[]{:S(2)}, u32[]{:S(2)}) collective-permute-start(bf16[16,128,256]{2,1,0:T(8,128)(2,1)S(1)} %all_to_all.11.own_ref), channel_id=1, source_target_pairs={{0,1},{1,0},{2,3},{3,2},{4,5},{5,4},{6,7},{7,6},{8,9},{9,8},{10,11... | collective-permute-start | bytes 3145736 | tf_op jit(solution)/shard_map/ppermute | solution.py:216
  103.6 2.3 %collective-permute-done.1.other_ref = bf16[16,128,256]{2,1,0:T(8,128)(2,1)S(1)} collective-permute-done((bf16[16,128,256]{2,1,0:T(8,128)(2,1)S(1)}, bf16[16,128,256]{2,1,0:T(8,128)(2,1)S(1)}, u32[]{:S(2)}, u32[]{:S(2)}) %collective-permute-start.1) | collective-permute-done | bytes 1048608 | tf_op jit(solution)/shard_map/ppermute | solution.py:216
  105.9 1.8 %flow_products.1 = (bf16[10,128,256]{2,1,0:T(8,128)(2,1)S(1)}, bf16[10,128,256]{2,1,0:T(8,128)(2,1)S(1)}, bf16[10,128,256]{2,1,0:T(8,128)(2,1)S(1)}, bf16[2,128,256]{2,1,0:T(8,128)(2,1)S(1)}) custom-call(s32[2]{0:T(128)S(1)} %pad_add_fusion.me_ref, s32[1,1,24]{2,1,0:T(1,128)S(1)} %copy-done.9, s32[1,1,24]{2,1,0:T(1,128)S(1)} %copy-done.10, ...), custom_call_target="tpu_custom_call" | custom-call | tf_op jit(solution)/shard_map/flow_products/pallas_call | solution.py:87
  107.7 0.0 copy-start.1
  107.7 3.5 %collective-permute-start.2 = (bf16[10,128,256]{2,1,0:T(8,128)(2,1)S(1)}, bf16[10,128,256]{2,1,0:T(8,128)(2,1)S(1)}, u32[]{:S(2)}, u32[]{:S(2)}) collective-permute-start(bf16[10,128,256]{2,1,0:T(8,128)(2,1)S(1)} %get-tuple-element.15), channel_id=1, source_target_pairs={{0,32},{32,0},{64,96},{96,64},{128,160},{160,128},{192,224},{224,1... | collective-permute-start | bytes 1966088 | tf_op jit(solution)/shard_map/ppermute | solution.py:114
  111.2 1.9 %collective-permute-start.3 = (bf16[10,128,256]{2,1,0:T(8,128)(2,1)S(1)}, bf16[10,128,256]{2,1,0:T(8,128)(2,1)S(1)}, u32[]{:S(2)}, u32[]{:S(2)}) collective-permute-start(bf16[10,128,256]{2,1,0:T(8,128)(2,1)S(1)} %get-tuple-element.16), channel_id=1, source_target_pairs={{0,480},{32,64},{64,32},{96,128},{128,96},{160,192},{192,160},{224... | collective-permute-start | bytes 1966088 | tf_op jit(solution)/shard_map/ppermute | solution.py:118
  113.2 4.3 %collective-permute-start.6 = (bf16[2,128,256]{2,1,0:T(8,128)(2,1)S(1)}, bf16[2,128,256]{2,1,0:T(8,128)(2,1)S(1)}, u32[]{:S(2)}, u32[]{:S(2)}) collective-permute-start(bf16[2,128,256]{2,1,0:T(8,128)(2,1)S(1)} %get-tuple-element.17), channel_id=1, source_target_pairs={{0,64},{32,480},{64,128},{96,32},{128,192},{160,96},{192,256},{224... | collective-permute-start | bytes 393224 | tf_op jit(solution)/shard_map/ppermute | solution.py:114
  117.5 11.0 %collective-permute-done.6 = bf16[2,128,256]{2,1,0:T(8,128)(2,1)S(1)} collective-permute-done((bf16[2,128,256]{2,1,0:T(8,128)(2,1)S(1)}, bf16[2,128,256]{2,1,0:T(8,128)(2,1)S(1)}, u32[]{:S(2)}, u32[]{:S(2)}) %collective-permute-start.6) | collective-permute-done | bytes 131104 | tf_op jit(solution)/shard_map/ppermute | solution.py:114
  128.5 3.0 %collective-permute-done.3 = bf16[10,128,256]{2,1,0:T(8,128)(2,1)S(1)} collective-permute-done((bf16[10,128,256]{2,1,0:T(8,128)(2,1)S(1)}, bf16[10,128,256]{2,1,0:T(8,128)(2,1)S(1)}, u32[]{:S(2)}, u32[]{:S(2)}) %collective-permute-start.3) | collective-permute-done | bytes 655392 | tf_op jit(solution)/shard_map/ppermute | solution.py:118
  131.6 0.2 add_convert_fusion.4
  131.7 4.3 %collective-permute-start.7 = (bf16[2,128,256]{2,1,0:T(8,128)(2,1)S(1)}, bf16[2,128,256]{2,1,0:T(8,128)(2,1)S(1)}, u32[]{:S(2)}, u32[]{:S(2)}) collective-permute-start(bf16[2,128,256]{2,1,0:T(8,128)(2,1)S(1)} %get-tuple-element.19), channel_id=1, source_target_pairs={{0,96},{32,448},{64,160},{96,0},{128,224},{160,64},{192,288},{224,... | collective-permute-start | bytes 393224 | tf_op jit(solution)/shard_map/ppermute | solution.py:114
  136.1 3.5 %collective-permute-start.4 = (bf16[2,128,256]{2,1,0:T(8,128)(2,1)S(1)}, bf16[2,128,256]{2,1,0:T(8,128)(2,1)S(1)}, u32[]{:S(2)}, u32[]{:S(2)}) collective-permute-start(bf16[2,128,256]{2,1,0:T(8,128)(2,1)S(1)} %get-tuple-element.20), channel_id=1, source_target_pairs={{0,416},{32,128},{64,480},{96,192},{128,32},{160,256},{192,96},{22... | collective-permute-start | bytes 393224 | tf_op jit(solution)/shard_map/ppermute | solution.py:118
  139.6 5.2 %collective-permute-done.7 = bf16[2,128,256]{2,1,0:T(8,128)(2,1)S(1)} collective-permute-done((bf16[2,128,256]{2,1,0:T(8,128)(2,1)S(1)}, bf16[2,128,256]{2,1,0:T(8,128)(2,1)S(1)}, u32[]{:S(2)}, u32[]{:S(2)}) %collective-permute-start.7) | collective-permute-done | bytes 131104 | tf_op jit(solution)/shard_map/ppermute | solution.py:114
  144.8 2.8 %collective-permute-done.4 = bf16[2,128,256]{2,1,0:T(8,128)(2,1)S(1)} collective-permute-done((bf16[2,128,256]{2,1,0:T(8,128)(2,1)S(1)}, bf16[2,128,256]{2,1,0:T(8,128)(2,1)S(1)}, u32[]{:S(2)}, u32[]{:S(2)}) %collective-permute-start.4) | collective-permute-done | bytes 131104 | tf_op jit(solution)/shard_map/ppermute | solution.py:118
  147.6 0.1 add_convert_fusion.2
  147.7 6.0 %collective-permute-start.5 = (bf16[2,128,256]{2,1,0:T(8,128)(2,1)S(1)}, bf16[2,128,256]{2,1,0:T(8,128)(2,1)S(1)}, u32[]{:S(2)}, u32[]{:S(2)}) collective-permute-start(bf16[2,128,256]{2,1,0:T(8,128)(2,1)S(1)} %get-tuple-element.21), channel_id=1, source_target_pairs={{0,96},{32,448},{64,160},{96,0},{128,224},{160,64},{192,288},{224,... | collective-permute-start | bytes 393224 | tf_op jit(solution)/shard_map/ppermute | solution.py:114
  153.8 3.2 %collective-permute-start.8 = (bf16[2,128,256]{2,1,0:T(8,128)(2,1)S(1)}, bf16[2,128,256]{2,1,0:T(8,128)(2,1)S(1)}, u32[]{:S(2)}, u32[]{:S(2)}) collective-permute-start(bf16[2,128,256]{2,1,0:T(8,128)(2,1)S(1)} %get-tuple-element.22), channel_id=1, source_target_pairs={{0,416},{32,128},{64,480},{96,192},{128,32},{160,256},{192,96},{22... | collective-permute-start | bytes 393224 | tf_op jit(solution)/shard_map/ppermute | solution.py:118
  156.9 3.4 %collective-permute-done.5 = bf16[2,128,256]{2,1,0:T(8,128)(2,1)S(1)} collective-permute-done((bf16[2,128,256]{2,1,0:T(8,128)(2,1)S(1)}, bf16[2,128,256]{2,1,0:T(8,128)(2,1)S(1)}, u32[]{:S(2)}, u32[]{:S(2)}) %collective-permute-start.5) | collective-permute-done | bytes 131104 | tf_op jit(solution)/shard_map/ppermute | solution.py:114
  160.3 7.3 %collective-permute-done.8 = bf16[2,128,256]{2,1,0:T(8,128)(2,1)S(1)} collective-permute-done((bf16[2,128,256]{2,1,0:T(8,128)(2,1)S(1)}, bf16[2,128,256]{2,1,0:T(8,128)(2,1)S(1)}, u32[]{:S(2)}, u32[]{:S(2)}) %collective-permute-start.8) | collective-permute-done | bytes 131104 | tf_op jit(solution)/shard_map/ppermute | solution.py:118
  167.7 1.1 flow_update.1
  (28 shorter events, 0.1 us)
Async XLA Ops:
  42.8 1.1 copy-start
  42.8 1.1 copy-start.9
  42.8 1.1 copy-start.10
  42.8 1.1 copy-start.11
  45.6 11.3 %collective-permute-start = (bf16[16,128,256]{2,1,0:T(8,128)(2,1)S(1)}, bf16[16,128,256]{2,1,0:T(8,128)(2,1)S(1)}, u32[]{:S(2)}, u32[]{:S(2)}) collective-permute-start(bf16[16,128,256]{2,1,0:T(8,128)(2,1)S(1)} %get-tuple-element.11), channel_id=1, source_target_pairs={{0,1},{1,0},{2,3},{3,2},{4,5},{5,4},{6,7},{7,6},{8,9},{9,8},{10,11... | collective-permute-start | bytes 3145736 | tf_op jit(solution)/shard_map/ppermute | solution.py:210
  56.9 22.2 %copy-start.2 = (bf16[256,256]{1,0:T(8,128)(2,1)S(1)}, bf16[256,256]{1,0:T(8,128)(2,1)}, u32[]{:S(2)}) copy-start(bf16[256,256]{1,0:T(8,128)(2,1)} %agg_ref.2) | copy-start | bytes 393220
  56.9 22.2 %copy-start.3 = (bf16[256,256]{1,0:T(8,128)(2,1)S(1)}, bf16[256,256]{1,0:T(8,128)(2,1)}, u32[]{:S(2)}) copy-start(bf16[256,256]{1,0:T(8,128)(2,1)} %self_ref.2) | copy-start | bytes 393220
  56.9 22.2 %copy-start.4 = (bf16[256,256]{1,0:T(8,128)(2,1)S(1)}, bf16[256,256]{1,0:T(8,128)(2,1)}, u32[]{:S(2)}) copy-start(bf16[256,256]{1,0:T(8,128)(2,1)} %out_w_ref.2) | copy-start | bytes 393220
  56.9 22.2 %copy-start.8 = (bf16[128,256]{1,0:T(8,128)(2,1)S(1)}, bf16[128,256]{1,0:T(8,128)(2,1)}, u32[]{:S(2)}) copy-start(bf16[128,256]{1,0:T(8,128)(2,1)} %state_ref.2) | copy-start | bytes 196612
  56.9 22.2 %copy-start.12 = (f32[256]{0:T(256)S(1)}, f32[256]{0:T(256)}, u32[]{:S(2)}) copy-start(f32[256]{0:T(256)} %param.20) | copy-start | bytes 3076
  99.4 6.4 %collective-permute-start.1 = (bf16[16,128,256]{2,1,0:T(8,128)(2,1)S(1)}, bf16[16,128,256]{2,1,0:T(8,128)(2,1)S(1)}, u32[]{:S(2)}, u32[]{:S(2)}) collective-permute-start(bf16[16,128,256]{2,1,0:T(8,128)(2,1)S(1)} %all_to_all.11.own_ref), channel_id=1, source_target_pairs={{0,1},{1,0},{2,3},{3,2},{4,5},{5,4},{6,7},{7,6},{8,9},{9,8},{10,11... | collective-permute-start | bytes 3145736 | tf_op jit(solution)/shard_map/ppermute | solution.py:216
  107.7 60.0 %copy-start.1 = (bf16[256,256]{1,0:T(8,128)(2,1)S(1)}, bf16[256,256]{1,0:T(8,128)(2,1)}, u32[]{:S(2)}) copy-start(bf16[256,256]{1,0:T(8,128)(2,1)} %state_ref.3) | copy-start | bytes 393220
  107.7 60.0 %copy-start.5 = (bf16[256,256]{1,0:T(8,128)(2,1)S(1)}, bf16[256,256]{1,0:T(8,128)(2,1)}, u32[]{:S(2)}) copy-start(bf16[256,256]{1,0:T(8,128)(2,1)} %agg_ref.3) | copy-start | bytes 393220
  107.7 60.0 %copy-start.6 = (bf16[256,256]{1,0:T(8,128)(2,1)S(1)}, bf16[256,256]{1,0:T(8,128)(2,1)}, u32[]{:S(2)}) copy-start(bf16[256,256]{1,0:T(8,128)(2,1)} %self_ref.3) | copy-start | bytes 393220
  107.7 60.0 %copy-start.7 = (bf16[256,256]{1,0:T(8,128)(2,1)S(1)}, bf16[256,256]{1,0:T(8,128)(2,1)}, u32[]{:S(2)}) copy-start(bf16[256,256]{1,0:T(8,128)(2,1)} %out_w_ref.3) | copy-start | bytes 393220
  107.7 60.0 %copy-start.13 = (f32[256]{0:T(256)S(1)}, f32[256]{0:T(256)}, u32[]{:S(2)}) copy-start(f32[256]{0:T(256)} %param.24) | copy-start | bytes 3076
  107.7 20.8 %collective-permute-start.2 = (bf16[10,128,256]{2,1,0:T(8,128)(2,1)S(1)}, bf16[10,128,256]{2,1,0:T(8,128)(2,1)S(1)}, u32[]{:S(2)}, u32[]{:S(2)}) collective-permute-start(bf16[10,128,256]{2,1,0:T(8,128)(2,1)S(1)} %get-tuple-element.15), channel_id=1, source_target_pairs={{0,32},{32,0},{64,96},{96,64},{128,160},{160,128},{192,224},{224,1... | collective-permute-start | bytes 1966088 | tf_op jit(solution)/shard_map/ppermute | solution.py:114
  111.2 20.3 %collective-permute-start.3 = (bf16[10,128,256]{2,1,0:T(8,128)(2,1)S(1)}, bf16[10,128,256]{2,1,0:T(8,128)(2,1)S(1)}, u32[]{:S(2)}, u32[]{:S(2)}) collective-permute-start(bf16[10,128,256]{2,1,0:T(8,128)(2,1)S(1)} %get-tuple-element.16), channel_id=1, source_target_pairs={{0,480},{32,64},{64,32},{96,128},{128,96},{160,192},{192,160},{224... | collective-permute-start | bytes 1966088 | tf_op jit(solution)/shard_map/ppermute | solution.py:118
  113.2 15.4 %collective-permute-start.6 = (bf16[2,128,256]{2,1,0:T(8,128)(2,1)S(1)}, bf16[2,128,256]{2,1,0:T(8,128)(2,1)S(1)}, u32[]{:S(2)}, u32[]{:S(2)}) collective-permute-start(bf16[2,128,256]{2,1,0:T(8,128)(2,1)S(1)} %get-tuple-element.17), channel_id=1, source_target_pairs={{0,64},{32,480},{64,128},{96,32},{128,192},{160,96},{192,256},{224... | collective-permute-start | bytes 393224 | tf_op jit(solution)/shard_map/ppermute | solution.py:114
  131.7 13.1 %collective-permute-start.7 = (bf16[2,128,256]{2,1,0:T(8,128)(2,1)S(1)}, bf16[2,128,256]{2,1,0:T(8,128)(2,1)S(1)}, u32[]{:S(2)}, u32[]{:S(2)}) collective-permute-start(bf16[2,128,256]{2,1,0:T(8,128)(2,1)S(1)} %get-tuple-element.19), channel_id=1, source_target_pairs={{0,96},{32,448},{64,160},{96,0},{128,224},{160,64},{192,288},{224,... | collective-permute-start | bytes 393224 | tf_op jit(solution)/shard_map/ppermute | solution.py:114
  136.1 11.5 %collective-permute-start.4 = (bf16[2,128,256]{2,1,0:T(8,128)(2,1)S(1)}, bf16[2,128,256]{2,1,0:T(8,128)(2,1)S(1)}, u32[]{:S(2)}, u32[]{:S(2)}) collective-permute-start(bf16[2,128,256]{2,1,0:T(8,128)(2,1)S(1)} %get-tuple-element.20), channel_id=1, source_target_pairs={{0,416},{32,128},{64,480},{96,192},{128,32},{160,256},{192,96},{22... | collective-permute-start | bytes 393224 | tf_op jit(solution)/shard_map/ppermute | solution.py:118
  147.7 12.6 %collective-permute-start.5 = (bf16[2,128,256]{2,1,0:T(8,128)(2,1)S(1)}, bf16[2,128,256]{2,1,0:T(8,128)(2,1)S(1)}, u32[]{:S(2)}, u32[]{:S(2)}) collective-permute-start(bf16[2,128,256]{2,1,0:T(8,128)(2,1)S(1)} %get-tuple-element.21), channel_id=1, source_target_pairs={{0,96},{32,448},{64,160},{96,0},{128,224},{160,64},{192,288},{224,... | collective-permute-start | bytes 393224 | tf_op jit(solution)/shard_map/ppermute | solution.py:114
  153.8 13.8 %collective-permute-start.8 = (bf16[2,128,256]{2,1,0:T(8,128)(2,1)S(1)}, bf16[2,128,256]{2,1,0:T(8,128)(2,1)S(1)}, u32[]{:S(2)}, u32[]{:S(2)}) collective-permute-start(bf16[2,128,256]{2,1,0:T(8,128)(2,1)S(1)} %get-tuple-element.22), channel_id=1, source_target_pairs={{0,416},{32,128},{64,480},{96,192},{128,32},{160,256},{192,96},{22... | collective-permute-start | bytes 393224 | tf_op jit(solution)/shard_map/ppermute | solution.py:118

commit v11 on v10

--- a/solution.py
+++ b/solution.py
@@ -49,7 +49,7 @@
     )(me, flow, link, live, coefs, pieces)
 
 
-ROW_ORDER = (0, 3, 6, -3, -6, 1, 4, 7, -2, -5, -1, -4, -7, 2, 5, 8)
+ROW_ORDER = (0, 3, 6, -3, -6, 7, -5, 1, 4, -2, -7, 5, -1, -4, 2, 8)
 
 
 def flow_products_kernel(
@@ -83,7 +83,7 @@
 
 def flow_products(me, flow, link, live, coefs, own, other, blocks):
     assert blocks == 2 * len(ROW_ORDER)
-    counts = [10, 10, 10, 2]
+    counts = [10, 4, 6, 4, 6, 2]
     return pl.pallas_call(
         flow_products_kernel,
         out_shape=[jax.ShapeDtypeStruct((count, BS, H), BF16) for count in counts],
@@ -106,7 +106,7 @@
     return total.astype(BF16)
 
 
-def sum_over_rows(own, for_a, for_b, opposite):
+def sum_over_rows(own, far_a, near_a, far_b, near_b, opposite):
     rows = len(ROW_ORDER)
 
     def swap_a(x, step):
@@ -117,13 +117,14 @@
         pairs = [(i, (i - step if i % 2 == 0 else i + step) % rows) for i in range(rows)]
         return lax.ppermute(x, "row", pairs)
 
-    got_a, got_b = swap_a(for_a, 1), swap_b(for_b, 1)
+    far_a, far_b = swap_a(far_a, 1), swap_b(far_b, 1)
     opposite = swap_a(opposite, 2)
-    six_a = add(own[4:6], got_a[8:10], got_b[4:6], opposite)
-    six_b = add(own[8:10], got_a[4:6], got_b[8:10])
-    mine = add(own[:2], got_a[:2], got_b[:2])
-    three_a = own[2:4].astype(F32) + got_a[6:8].astype(F32) + got_b[2:4].astype(F32)
-    three_b = own[6:8].astype(F32) + got_a[2:4].astype(F32) + got_b[6:8].astype(F32)
+    near_a, near_b = swap_a(near_a, 1), swap_b(near_b, 1)
+    six_a = add(own[4:6], far_a[2:4], far_b[:2], opposite)
+    six_b = add(own[8:10], far_a[:2], far_b[2:4])
+    mine = add(own[:2], near_a[:2], near_b[:2])
+    three_a = own[2:4].astype(F32) + near_a[4:6].astype(F32) + near_b[2:4].astype(F32)
+    three_b = own[6:8].astype(F32) + near_a[2:4].astype(F32) + near_b[4:6].astype(F32)
     got_a, got_b = swap_a(six_a, 3), swap_b(six_b, 3)
     three_b, three_a = add(three_b, got_a), add(three_a, got_b)
     got_a, got_b = swap_a(three_a, 3), swap_b(three_b, 3)

time: 169 us -> 164 us (0.970)
  the two profiles are of different devices: /device:TPU:35 before, /device:TPU:1 now
where the time goes in v11:
time: 164 us; the launch traced here: 163 us
  blocking collectives  86.5 us (53%)
  starting transfers between devices  43.2 us (26%)
  waiting for transfers between devices  24.3 us (15%)
  Pallas kernels  5.85 us (4%)
  other arithmetic  1.96 us (1%)
    all_gather x1, blocking collectives, gather_rows(): got = lax.all_gather(sent, 'row', axis=0, tiled=True)  44.6 us
    all_to_all x1, blocking collectives, on_device(): lax.all_to_all(own, 'col', 0, 0, tiled=True, axis_index_groups=same_core)  22.9 us
    all_to_all x1, blocking collectives, on_device(): lax.all_to_all(link_copies, 'col', 0, 0, tiled=True, axis_index_groups=sa...  19 us
    ppermute x4, starting transfers between devices, swap_b(): return lax.ppermute(x, 'row', pairs)  18.3 us
    ppermute x5, starting transfers between devices, swap_a(): return lax.ppermute(x, 'row', pairs)  12.6 us
    ppermute x5, waiting for transfers between devices, swap_a(): return lax.ppermute(x, 'row', pairs)  10.9 us
    ppermute x4, waiting for transfers between devices, swap_b(): return lax.ppermute(x, 'row', pairs)  8.93 us
    ppermute x1, starting transfers between devices, on_device(): own = add_two(own, lax.ppermute(other, 'col', sibling))  8.14 us
  transfers between devices with their start and end apart: 11, of which 5 were waited for; matrix products, arithmetic and copies ran while one was open for 0% of the time, Pallas kernels for 0%

profile of v11, /device:TPU:1, one launch (start us, length us, event | category | flops | bytes accessed | tf_op | source)
XLA Modules:
  0.0 163.3 jit_solution(3871393492118225539)
XLA Ops:
  0.6 0.9 multiply_convert_fusion.1
  1.6 44.6 %all-gather.1 = f16[4096,256]{1,0:T(8,128)(2,1)S(1)} all-gather(f16[256,256]{1,0:T(8,128)(2,1)S(1)} %multiply_convert_fusion.1), channel_id=1, replica_groups=mesh['row'=16,'col'=32] {'row'}, dimensions={0}, use_global_device_ids=true | all-gather | bytes 2228224 | tf_op jit(solution)/shard_map/all_gather | solution.py:230
  46.2 0.6 multiply_convert_fusion
  46.8 0.1 pad_add_fusion.me_ref
  46.9 0.5 copy-done
  47.3 1.6 link_products.1
  48.9 8.1 %collective-permute-start = (bf16[16,128,256]{2,1,0:T(8,128)(2,1)S(1)}, bf16[16,128,256]{2,1,0:T(8,128)(2,1)S(1)}, u32[]{:S(2)}, u32[]{:S(2)}) collective-permute-start(bf16[16,128,256]{2,1,0:T(8,128)(2,1)S(1)} %get-tuple-element.13), channel_id=1, source_target_pairs={{0,1},{1,0},{2,3},{3,2},{4,5},{5,4},{6,7},{7,6},{8,9},{9,8},{10,11... | collective-permute-start | bytes 3145736 | tf_op jit(solution)/shard_map/ppermute | solution.py:211
  57.1 2.3 %collective-permute-done.b_ref = bf16[16,128,256]{2,1,0:T(8,128)(2,1)S(1)} collective-permute-done((bf16[16,128,256]{2,1,0:T(8,128)(2,1)S(1)}, bf16[16,128,256]{2,1,0:T(8,128)(2,1)S(1)}, u32[]{:S(2)}, u32[]{:S(2)}) %collective-permute-start) | collective-permute-done | bytes 1048608 | tf_op jit(solution)/shard_map/ppermute | solution.py:211
  59.4 0.2 add_two.1
  59.6 22.9 %all_to_all.10.parts_ref = bf16[16,128,256]{2,1,0:T(8,128)(2,1)S(1)} all-to-all(bf16[16,128,256]{2,1,0:T(8,128)(2,1)S(1)} %add_two.1), channel_id=1, replica_groups={{0,2,4,6,8,10,12,14,16,18,20,22,24,26,28,30},{1,3,5,7,9,11,13,15,17,19,..., dimensions={0} | all-to-all | bytes 2097152 | tf_op jit(solution)/shard_map/all_to_all | solution.py:212
  82.5 1.2 link_update.1
  83.7 19.0 %all_to_all.11.own_ref = bf16[16,128,256]{2,1,0:T(8,128)(2,1)S(1)} all-to-all(bf16[16,128,256]{2,1,0:T(8,128)(2,1)S(1)} %get-tuple-element.15), channel_id=1, replica_groups={{0,2,4,6,8,10,12,14,16,18,20,22,24,26,28,30},{1,3,5,7,9,11,13,15,17,19,..., dimensions={0} | all-to-all | bytes 2097152 | tf_op jit(solution)/shard_map/all_to_all | solution.py:216
  102.7 4.2 %collective-permute-start.1 = (bf16[16,128,256]{2,1,0:T(8,128)(2,1)S(1)}, bf16[16,128,256]{2,1,0:T(8,128)(2,1)S(1)}, u32[]{:S(2)}, u32[]{:S(2)}) collective-permute-start(bf16[16,128,256]{2,1,0:T(8,128)(2,1)S(1)} %all_to_all.11.own_ref), channel_id=1, source_target_pairs={{0,1},{1,0},{2,3},{3,2},{4,5},{5,4},{6,7},{7,6},{8,9},{9,8},{10,11... | collective-permute-start | bytes 3145736 | tf_op jit(solution)/shard_map/ppermute | solution.py:217
  107.0 2.3 %collective-permute-done.1.other_ref = bf16[16,128,256]{2,1,0:T(8,128)(2,1)S(1)} collective-permute-done((bf16[16,128,256]{2,1,0:T(8,128)(2,1)S(1)}, bf16[16,128,256]{2,1,0:T(8,128)(2,1)S(1)}, u32[]{:S(2)}, u32[]{:S(2)}) %collective-permute-start.1) | collective-permute-done | bytes 1048608 | tf_op jit(solution)/shard_map/ppermute | solution.py:217
  109.2 1.8 %flow_products.1 = (bf16[10,128,256]{2,1,0:T(8,128)(2,1)S(1)}, bf16[4,128,256]{2,1,0:T(8,128)(2,1)S(1)}, bf16[6,128,256]{2,1,0:T(8,128)(2,1)S(1)}, bf16[4,128,25...) custom-call(s32[2]{0:T(128)S(1)} %pad_add_fusion.me_ref, ...), custom_call_target="tpu_custom_call" | custom-call | tf_op jit(solution)/shard_map/flow_products/pallas_call | solution.py:87
  111.0 0.0 copy-start.6
  111.1 0.0 copy-start.7
  111.1 2.1 %collective-permute-start.4 = (bf16[4,128,256]{2,1,0:T(8,128)(2,1)S(1)}, bf16[4,128,256]{2,1,0:T(8,128)(2,1)S(1)}, u32[]{:S(2)}, u32[]{:S(2)}) collective-permute-start(bf16[4,128,256]{2,1,0:T(8,128)(2,1)S(1)} %get-tuple-element.19), channel_id=1, source_target_pairs={{0,32},{32,0},{64,96},{96,64},{128,160},{160,128},{192,224},{224,1... | collective-permute-start | bytes 786440 | tf_op jit(solution)/shard_map/ppermute | solution.py:114
  113.1 3.3 %collective-permute-start.5 = (bf16[4,128,256]{2,1,0:T(8,128)(2,1)S(1)}, bf16[4,128,256]{2,1,0:T(8,128)(2,1)S(1)}, u32[]{:S(2)}, u32[]{:S(2)}) collective-permute-start(bf16[4,128,256]{2,1,0:T(8,128)(2,1)S(1)} %get-tuple-element.20), channel_id=1, source_target_pairs={{0,480},{32,64},{64,32},{96,128},{128,96},{160,192},{192,160},{224... | collective-permute-start | bytes 786440 | tf_op jit(solution)/shard_map/ppermute | solution.py:118
  116.5 3.1 %collective-permute-start.8 = (bf16[2,128,256]{2,1,0:T(8,128)(2,1)S(1)}, bf16[2,128,256]{2,1,0:T(8,128)(2,1)S(1)}, u32[]{:S(2)}, u32[]{:S(2)}) collective-permute-start(bf16[2,128,256]{2,1,0:T(8,128)(2,1)S(1)} %get-tuple-element.21), channel_id=1, source_target_pairs={{0,64},{32,480},{64,128},{96,32},{128,192},{160,96},{192,256},{224... | collective-permute-start | bytes 393224 | tf_op jit(solution)/shard_map/ppermute | solution.py:114
  119.6 3.1 %collective-permute-start.2 = (bf16[6,128,256]{2,1,0:T(8,128)(2,1)S(1)}, bf16[6,128,256]{2,1,0:T(8,128)(2,1)S(1)}, u32[]{:S(2)}, u32[]{:S(2)}) collective-permute-start(bf16[6,128,256]{2,1,0:T(8,128)(2,1)S(1)} %get-tuple-element.17), channel_id=1, source_target_pairs={{0,32},{32,0},{64,96},{96,64},{128,160},{160,128},{192,224},{224,1... | collective-permute-start | bytes 1179656 | tf_op jit(solution)/shard_map/ppermute | solution.py:114
  122.7 3.3 %collective-permute-start.3 = (bf16[6,128,256]{2,1,0:T(8,128)(2,1)S(1)}, bf16[6,128,256]{2,1,0:T(8,128)(2,1)S(1)}, u32[]{:S(2)}, u32[]{:S(2)}) collective-permute-start(bf16[6,128,256]{2,1,0:T(8,128)(2,1)S(1)} %get-tuple-element.18), channel_id=1, source_target_pairs={{0,480},{32,64},{64,32},{96,128},{128,96},{160,192},{192,160},{224... | collective-permute-start | bytes 1179656 | tf_op jit(solution)/shard_map/ppermute | solution.py:118
  126.1 0.1 add_convert_fusion.3
  126.2 4.4 %collective-permute-start.6 = (bf16[2,128,256]{2,1,0:T(8,128)(2,1)S(1)}, bf16[2,128,256]{2,1,0:T(8,128)(2,1)S(1)}, u32[]{:S(2)}, u32[]{:S(2)}) collective-permute-start(bf16[2,128,256]{2,1,0:T(8,128)(2,1)S(1)} %get-tuple-element.25), channel_id=1, source_target_pairs={{0,416},{32,128},{64,480},{96,192},{128,32},{160,256},{192,96},{22... | collective-permute-start | bytes 393224 | tf_op jit(solution)/shard_map/ppermute | solution.py:118
  130.6 2.3 %collective-permute-start.9 = (bf16[2,128,256]{2,1,0:T(8,128)(2,1)S(1)}, bf16[2,128,256]{2,1,0:T(8,128)(2,1)S(1)}, u32[]{:S(2)}, u32[]{:S(2)}) collective-permute-start(bf16[2,128,256]{2,1,0:T(8,128)(2,1)S(1)} %get-tuple-element.26), channel_id=1, source_target_pairs={{0,96},{32,448},{64,160},{96,0},{128,224},{160,64},{192,288},{224,... | collective-permute-start | bytes 393224 | tf_op jit(solution)/shard_map/ppermute | solution.py:114
  132.9 8.4 %collective-permute-done.6 = bf16[2,128,256]{2,1,0:T(8,128)(2,1)S(1)} collective-permute-done((bf16[2,128,256]{2,1,0:T(8,128)(2,1)S(1)}, bf16[2,128,256]{2,1,0:T(8,128)(2,1)S(1)}, u32[]{:S(2)}, u32[]{:S(2)}) %collective-permute-start.6) | collective-permute-done | bytes 131104 | tf_op jit(solution)/shard_map/ppermute | solution.py:118
  141.4 0.2 add_convert_fusion.4
  141.6 7.3 %collective-permute-start.10 = (bf16[2,128,256]{2,1,0:T(8,128)(2,1)S(1)}, bf16[2,128,256]{2,1,0:T(8,128)(2,1)S(1)}, u32[]{:S(2)}, u32[]{:S(2)}) collective-permute-start(bf16[2,128,256]{2,1,0:T(8,128)(2,1)S(1)} %get-tuple-element.23), channel_id=1, source_target_pairs={{0,416},{32,128},{64,480},{96,192},{128,32},{160,256},{192,96},{22... | collective-permute-start | bytes 393224 | tf_op jit(solution)/shard_map/ppermute | solution.py:118
  148.9 1.9 %collective-permute-start.7 = (bf16[2,128,256]{2,1,0:T(8,128)(2,1)S(1)}, bf16[2,128,256]{2,1,0:T(8,128)(2,1)S(1)}, u32[]{:S(2)}, u32[]{:S(2)}) collective-permute-start(bf16[2,128,256]{2,1,0:T(8,128)(2,1)S(1)} %get-tuple-element.24), channel_id=1, source_target_pairs={{0,96},{32,448},{64,160},{96,0},{128,224},{160,64},{192,288},{224,... | collective-permute-start | bytes 393224 | tf_op jit(solution)/shard_map/ppermute | solution.py:114
  150.8 0.5 collective-permute-done.10
  151.3 10.9 %collective-permute-done.7 = bf16[2,128,256]{2,1,0:T(8,128)(2,1)S(1)} collective-permute-done((bf16[2,128,256]{2,1,0:T(8,128)(2,1)S(1)}, bf16[2,128,256]{2,1,0:T(8,128)(2,1)S(1)}, u32[]{:S(2)}, u32[]{:S(2)}) %collective-permute-start.7) | collective-permute-done | bytes 131104 | tf_op jit(solution)/shard_map/ppermute | solution.py:114
  162.3 1.1 flow_update.1
  (32 shorter events, 0.1 us)
Async XLA Ops:
  46.2 1.1 copy-start
  46.2 1.1 copy-start.9
  46.2 1.1 copy-start.10
  46.2 1.1 copy-start.11
  48.9 10.4 %collective-permute-start = (bf16[16,128,256]{2,1,0:T(8,128)(2,1)S(1)}, bf16[16,128,256]{2,1,0:T(8,128)(2,1)S(1)}, u32[]{:S(2)}, u32[]{:S(2)}) collective-permute-start(bf16[16,128,256]{2,1,0:T(8,128)(2,1)S(1)} %get-tuple-element.13), channel_id=1, source_target_pairs={{0,1},{1,0},{2,3},{3,2},{4,5},{5,4},{6,7},{7,6},{8,9},{9,8},{10,11... | collective-permute-start | bytes 3145736 | tf_op jit(solution)/shard_map/ppermute | solution.py:211
  59.3 23.1 %copy-start.2 = (bf16[256,256]{1,0:T(8,128)(2,1)S(1)}, bf16[256,256]{1,0:T(8,128)(2,1)}, u32[]{:S(2)}) copy-start(bf16[256,256]{1,0:T(8,128)(2,1)} %agg_ref.2) | copy-start | bytes 393220
  59.3 23.2 %copy-start.3 = (bf16[256,256]{1,0:T(8,128)(2,1)S(1)}, bf16[256,256]{1,0:T(8,128)(2,1)}, u32[]{:S(2)}) copy-start(bf16[256,256]{1,0:T(8,128)(2,1)} %self_ref.2) | copy-start | bytes 393220
  59.4 23.2 %copy-start.4 = (bf16[256,256]{1,0:T(8,128)(2,1)S(1)}, bf16[256,256]{1,0:T(8,128)(2,1)}, u32[]{:S(2)}) copy-start(bf16[256,256]{1,0:T(8,128)(2,1)} %out_w_ref.2) | copy-start | bytes 393220
  59.4 23.2 %copy-start.8 = (bf16[128,256]{1,0:T(8,128)(2,1)S(1)}, bf16[128,256]{1,0:T(8,128)(2,1)}, u32[]{:S(2)}) copy-start(bf16[128,256]{1,0:T(8,128)(2,1)} %state_ref.2) | copy-start | bytes 196612
  59.4 23.2 %copy-start.12 = (f32[256]{0:T(256)S(1)}, f32[256]{0:T(256)}, u32[]{:S(2)}) copy-start(f32[256]{0:T(256)} %param.20) | copy-start | bytes 3076
  102.7 6.5 %collective-permute-start.1 = (bf16[16,128,256]{2,1,0:T(8,128)(2,1)S(1)}, bf16[16,128,256]{2,1,0:T(8,128)(2,1)S(1)}, u32[]{:S(2)}, u32[]{:S(2)}) collective-permute-start(bf16[16,128,256]{2,1,0:T(8,128)(2,1)S(1)} %all_to_all.11.own_ref), channel_id=1, source_target_pairs={{0,1},{1,0},{2,3},{3,2},{4,5},{5,4},{6,7},{7,6},{8,9},{9,8},{10,11... | collective-permute-start | bytes 3145736 | tf_op jit(solution)/shard_map/ppermute | solution.py:217
  111.0 51.2 %copy-start.1 = (bf16[256,256]{1,0:T(8,128)(2,1)S(1)}, bf16[256,256]{1,0:T(8,128)(2,1)}, u32[]{:S(2)}) copy-start(bf16[256,256]{1,0:T(8,128)(2,1)} %state_ref.3) | copy-start | bytes 393220
  111.0 51.2 %copy-start.5 = (bf16[256,256]{1,0:T(8,128)(2,1)S(1)}, bf16[256,256]{1,0:T(8,128)(2,1)}, u32[]{:S(2)}) copy-start(bf16[256,256]{1,0:T(8,128)(2,1)} %agg_ref.3) | copy-start | bytes 393220
  111.0 51.2 %copy-start.6 = (bf16[256,256]{1,0:T(8,128)(2,1)S(1)}, bf16[256,256]{1,0:T(8,128)(2,1)}, u32[]{:S(2)}) copy-start(bf16[256,256]{1,0:T(8,128)(2,1)} %self_ref.3) | copy-start | bytes 393220
  111.1 51.2 %copy-start.7 = (bf16[256,256]{1,0:T(8,128)(2,1)S(1)}, bf16[256,256]{1,0:T(8,128)(2,1)}, u32[]{:S(2)}) copy-start(bf16[256,256]{1,0:T(8,128)(2,1)} %out_w_ref.3) | copy-start | bytes 393220
  111.1 51.2 %copy-start.13 = (f32[256]{0:T(256)S(1)}, f32[256]{0:T(256)}, u32[]{:S(2)}) copy-start(f32[256]{0:T(256)} %param.24) | copy-start | bytes 3076
  111.1 15.0 %collective-permute-start.4 = (bf16[4,128,256]{2,1,0:T(8,128)(2,1)S(1)}, bf16[4,128,256]{2,1,0:T(8,128)(2,1)S(1)}, u32[]{:S(2)}, u32[]{:S(2)}) collective-permute-start(bf16[4,128,256]{2,1,0:T(8,128)(2,1)S(1)} %get-tuple-element.19), channel_id=1, source_target_pairs={{0,32},{32,0},{64,96},{96,64},{128,160},{160,128},{192,224},{224,1... | collective-permute-start | bytes 786440 | tf_op jit(solution)/shard_map/ppermute | solution.py:114
  113.1 13.0 %collective-permute-start.5 = (bf16[4,128,256]{2,1,0:T(8,128)(2,1)S(1)}, bf16[4,128,256]{2,1,0:T(8,128)(2,1)S(1)}, u32[]{:S(2)}, u32[]{:S(2)}) collective-permute-start(bf16[4,128,256]{2,1,0:T(8,128)(2,1)S(1)} %get-tuple-element.20), channel_id=1, source_target_pairs={{0,480},{32,64},{64,32},{96,128},{128,96},{160,192},{192,160},{224... | collective-permute-start | bytes 786440 | tf_op jit(solution)/shard_map/ppermute | solution.py:118
  116.5 9.6 %collective-permute-start.8 = (bf16[2,128,256]{2,1,0:T(8,128)(2,1)S(1)}, bf16[2,128,256]{2,1,0:T(8,128)(2,1)S(1)}, u32[]{:S(2)}, u32[]{:S(2)}) collective-permute-start(bf16[2,128,256]{2,1,0:T(8,128)(2,1)S(1)} %get-tuple-element.21), channel_id=1, source_target_pairs={{0,64},{32,480},{64,128},{96,32},{128,192},{160,96},{192,256},{224... | collective-permute-start | bytes 393224 | tf_op jit(solution)/shard_map/ppermute | solution.py:114
  119.6 21.8 %collective-permute-start.2 = (bf16[6,128,256]{2,1,0:T(8,128)(2,1)S(1)}, bf16[6,128,256]{2,1,0:T(8,128)(2,1)S(1)}, u32[]{:S(2)}, u32[]{:S(2)}) collective-permute-start(bf16[6,128,256]{2,1,0:T(8,128)(2,1)S(1)} %get-tuple-element.17), channel_id=1, source_target_pairs={{0,32},{32,0},{64,96},{96,64},{128,160},{160,128},{192,224},{224,1... | collective-permute-start | bytes 1179656 | tf_op jit(solution)/shard_map/ppermute | solution.py:114
  122.7 18.6 %collective-permute-start.3 = (bf16[6,128,256]{2,1,0:T(8,128)(2,1)S(1)}, bf16[6,128,256]{2,1,0:T(8,128)(2,1)S(1)}, u32[]{:S(2)}, u32[]{:S(2)}) collective-permute-start(bf16[6,128,256]{2,1,0:T(8,128)(2,1)S(1)} %get-tuple-element.18), channel_id=1, source_target_pairs={{0,480},{32,64},{64,32},{96,128},{128,96},{160,192},{192,160},{224... | collective-permute-start | bytes 1179656 | tf_op jit(solution)/shard_map/ppermute | solution.py:118
  126.2 15.1 %collective-permute-start.6 = (bf16[2,128,256]{2,1,0:T(8,128)(2,1)S(1)}, bf16[2,128,256]{2,1,0:T(8,128)(2,1)S(1)}, u32[]{:S(2)}, u32[]{:S(2)}) collective-permute-start(bf16[2,128,256]{2,1,0:T(8,128)(2,1)S(1)} %get-tuple-element.25), channel_id=1, source_target_pairs={{0,416},{32,128},{64,480},{96,192},{128,32},{160,256},{192,96},{22... | collective-permute-start | bytes 393224 | tf_op jit(solution)/shard_map/ppermute | solution.py:118
  130.6 10.7 %collective-permute-start.9 = (bf16[2,128,256]{2,1,0:T(8,128)(2,1)S(1)}, bf16[2,128,256]{2,1,0:T(8,128)(2,1)S(1)}, u32[]{:S(2)}, u32[]{:S(2)}) collective-permute-start(bf16[2,128,256]{2,1,0:T(8,128)(2,1)S(1)} %get-tuple-element.26), channel_id=1, source_target_pairs={{0,96},{32,448},{64,160},{96,0},{128,224},{160,64},{192,288},{224,... | collective-permute-start | bytes 393224 | tf_op jit(solution)/shard_map/ppermute | solution.py:114
  141.6 9.7 %collective-permute-start.10 = (bf16[2,128,256]{2,1,0:T(8,128)(2,1)S(1)}, bf16[2,128,256]{2,1,0:T(8,128)(2,1)S(1)}, u32[]{:S(2)}, u32[]{:S(2)}) collective-permute-start(bf16[2,128,256]{2,1,0:T(8,128)(2,1)S(1)} %get-tuple-element.23), channel_id=1, source_target_pairs={{0,416},{32,128},{64,480},{96,192},{128,32},{160,256},{192,96},{22... | collective-permute-start | bytes 393224 | tf_op jit(solution)/shard_map/ppermute | solution.py:118
  148.9 13.3 %collective-permute-start.7 = (bf16[2,128,256]{2,1,0:T(8,128)(2,1)S(1)}, bf16[2,128,256]{2,1,0:T(8,128)(2,1)S(1)}, u32[]{:S(2)}, u32[]{:S(2)}) collective-permute-start(bf16[2,128,256]{2,1,0:T(8,128)(2,1)S(1)} %get-tuple-element.24), channel_id=1, source_target_pairs={{0,96},{32,448},{64,160},{96,0},{128,224},{160,64},{192,288},{224,... | collective-permute-start | bytes 393224 | tf_op jit(solution)/shard_map/ppermute | solution.py:114

commit v12 on v11

--- a/solution.py
+++ b/solution.py
@@ -17,33 +17,31 @@
 
 
 def link_products_kernel(
-    me_ref, flow_ref, link_ref, live_ref, coefs_ref, pieces_ref, own_ref, other_ref, acc_ref
+    side, me_ref, flow_ref, link_ref, live_ref, coefs_ref, pieces_ref, out_ref, acc_ref
 ):
-    blocks = acc_ref.shape[0] - 1
-    half = blocks // 2
+    half = acc_ref.shape[0] - 1
     acc_ref[...] = jnp.zeros_like(acc_ref)
     for slot in range(coefs_ref.shape[0]):
         block = link_ref[0, 0, slot]
-        place = ((block + me_ref[1]) % 2) * half + block // 2
-        place = jnp.where(live_ref[0, 0, slot] == 1, place, blocks)
+        here = jnp.logical_and(live_ref[0, 0, slot] == 1, (block + me_ref[1]) % 2 == side)
+        place = jnp.where(here, block // 2, half)
         acc_ref[place] += lax.dot_general(
             coefs_ref[slot],
             pieces_ref[flow_ref[0, 0, slot]],
             (((0,), (0,)), ((), ())),
             preferred_element_type=F32,
         )
-    own_ref[...] = acc_ref[:half].astype(BF16)
-    other_ref[...] = acc_ref[half : 2 * half].astype(BF16)
-
-
-def link_products(me, flow, link, live, coefs, pieces, blocks):
+    out_ref[...] = acc_ref[:half].astype(BF16)
+
+
+def link_products(side, me, flow, link, live, coefs, pieces, blocks):
     shape = jax.ShapeDtypeStruct((blocks // 2, BS, H), BF16)
     return pl.pallas_call(
-        link_products_kernel,
-        out_shape=[shape, shape],
+        functools.partial(link_products_kernel, side),
+        out_shape=shape,
         in_specs=[SMEM, SMEM, SMEM, SMEM, VMEM, VMEM],
-        out_specs=[VMEM, VMEM],
-        scratch_shapes=[pltpu.VMEM((blocks + 1, BS, H), F32)],
+        out_specs=VMEM,
+        scratch_shapes=[pltpu.VMEM((blocks // 2 + 1, BS, H), F32)],
         compiler_params=PARAMS,
         name="link_products",
     )(me, flow, link, live, coefs, pieces)
@@ -204,9 +202,12 @@
     same_core = [[2 * i + core for i in range(pairs)] for core in range(2)]
 
     flow_group = gather_rows(flow_state)
-    own, other = link_products(
-        me, tile_flow, tile_link, tile_live, coefs,
-        flow_group.reshape(flow_blocks, BS, H), cols,
+    other, own = (
+        link_products(
+            side, me, tile_flow, tile_link, tile_live, coefs,
+            flow_group.reshape(flow_blocks, BS, H), cols,
+        )
+        for side in (1, 0)
     )
     own = add_two(own, lax.ppermute(other, "col", sibling))
     link_parts = lax.all_to_all(own, "col", 0, 0, tiled=True, axis_index_groups=same_core)

time: 164 us -> 162 us (0.988)
  waiting for transfers between devices: 24.3 us -> 20.3 us
  transfers between devices with their start and end apart: 11 -> 11, of which waited for: 5 -> 5; matrix products, arithmetic and copies ran while one was open for 0% -> 0% of each run, Pallas kernels for 0% -> 1%
where the time goes in v12:
time: 162 us
  blocking collectives  86.5 us (53%)
  starting transfers between devices  44.6 us (28%)
  waiting for transfers between devices  20.3 us (13%)
  Pallas kernels  6.98 us (4%)
  other arithmetic  1.97 us (1%)
    all_gather x1, blocking collectives, gather_rows(): got = lax.all_gather(sent, 'row', axis=0, tiled=True)  44.6 us
    all_to_all x1, blocking collectives, on_device(): lax.all_to_all(own, 'col', 0, 0, tiled=True, axis_index_groups=same_core)  22.9 us
    ppermute x4, starting transfers between devices, swap_b(): return lax.ppermute(x, 'row', pairs)  19.6 us
    all_to_all x1, blocking collectives, on_device(): lax.all_to_all(link_copies, 'col', 0, 0, tiled=True, axis_index_groups=sa...  19 us
    ppermute x5, starting transfers between devices, swap_a(): return lax.ppermute(x, 'row', pairs)  12.6 us
    ppermute x5, waiting for transfers between devices, swap_a(): return lax.ppermute(x, 'row', pairs)  9.61 us
    ppermute x1, starting transfers between devices, on_device(): own = add_two(own, lax.ppermute(other, 'col', sibling))  8.15 us
    ppermute x4, waiting for transfers between devices, swap_b(): return lax.ppermute(x, 'row', pairs)  7.56 us
  transfers between devices with their start and end apart: 11, of which 5 were waited for; matrix products, arithmetic and copies ran while one was open for 0% of the time, Pallas kernels for 1%

profile of v12, /device:TPU:1, one launch (start us, length us, event | category | flops | bytes accessed | tf_op | source)
XLA Modules:
  0.0 161.8 jit_solution(5507516444636369099)
XLA Ops:
  0.6 0.9 multiply_convert_fusion.1
  1.6 44.6 %all-gather.1 = f16[4096,256]{1,0:T(8,128)(2,1)S(1)} all-gather(f16[256,256]{1,0:T(8,128)(2,1)S(1)} %multiply_convert_fusion.1), channel_id=1, replica_groups=mesh['row'=16,'col'=32] {'row'}, dimensions={0}, use_global_device_ids=true | all-gather | bytes 2228224 | tf_op jit(solution)/shard_map/all_gather | solution.py:231
  46.2 0.6 multiply_convert_fusion
  46.8 0.1 pad_add_fusion.me_ref
  46.9 0.5 copy-done
  47.3 1.4 link_products.3
  48.7 8.1 %collective-permute-start = (bf16[16,128,256]{2,1,0:T(8,128)(2,1)S(1)}, bf16[16,128,256]{2,1,0:T(8,128)(2,1)S(1)}, u32[]{:S(2)}, u32[]{:S(2)}) collective-permute-start(bf16[16,128,256]{2,1,0:T(8,128)(2,1)S(1)} %link_products.3), channel_id=1, source_target_pairs={{0,1},{1,0},{2,3},{3,2},{4,5},{5,4},{6,7},{7,6},{8,9},{9,8},{10,11... | collective-permute-start | bytes 3145736 | tf_op jit(solution)/shard_map/ppermute | solution.py:212
  56.9 1.4 link_products.2.a_ref
  58.2 0.0 copy-start.2
  58.3 0.8 collective-permute-done.b_ref
  59.1 0.2 add_two.1
  59.4 22.9 %all_to_all.10.parts_ref = bf16[16,128,256]{2,1,0:T(8,128)(2,1)S(1)} all-to-all(bf16[16,128,256]{2,1,0:T(8,128)(2,1)S(1)} %add_two.1), channel_id=1, replica_groups={{0,2,4,6,8,10,12,14,16,18,20,22,24,26,28,30},{1,3,5,7,9,11,13,15,17,19,..., dimensions={0} | all-to-all | bytes 2097152 | tf_op jit(solution)/shard_map/all_to_all | solution.py:213
  82.3 1.2 link_update.1
  83.4 19.0 %all_to_all.11.own_ref = bf16[16,128,256]{2,1,0:T(8,128)(2,1)S(1)} all-to-all(bf16[16,128,256]{2,1,0:T(8,128)(2,1)S(1)} %get-tuple-element.11), channel_id=1, replica_groups={{0,2,4,6,8,10,12,14,16,18,20,22,24,26,28,30},{1,3,5,7,9,11,13,15,17,19,..., dimensions={0} | all-to-all | bytes 2097152 | tf_op jit(solution)/shard_map/all_to_all | solution.py:217
  102.5 4.2 %collective-permute-start.1 = (bf16[16,128,256]{2,1,0:T(8,128)(2,1)S(1)}, bf16[16,128,256]{2,1,0:T(8,128)(2,1)S(1)}, u32[]{:S(2)}, u32[]{:S(2)}) collective-permute-start(bf16[16,128,256]{2,1,0:T(8,128)(2,1)S(1)} %all_to_all.11.own_ref), channel_id=1, source_target_pairs={{0,1},{1,0},{2,3},{3,2},{4,5},{5,4},{6,7},{7,6},{8,9},{9,8},{10,11... | collective-permute-start | bytes 3145736 | tf_op jit(solution)/shard_map/ppermute | solution.py:218
  106.7 2.3 %collective-permute-done.1.other_ref = bf16[16,128,256]{2,1,0:T(8,128)(2,1)S(1)} collective-permute-done((bf16[16,128,256]{2,1,0:T(8,128)(2,1)S(1)}, bf16[16,128,256]{2,1,0:T(8,128)(2,1)S(1)}, u32[]{:S(2)}, u32[]{:S(2)}) %collective-permute-start.1) | collective-permute-done | bytes 1048608 | tf_op jit(solution)/shard_map/ppermute | solution.py:218
  109.0 1.8 %flow_products.1 = (bf16[10,128,256]{2,1,0:T(8,128)(2,1)S(1)}, bf16[4,128,256]{2,1,0:T(8,128)(2,1)S(1)}, bf16[6,128,256]{2,1,0:T(8,128)(2,1)S(1)}, bf16[4,128,25...) custom-call(s32[2]{0:T(128)S(1)} %pad_add_fusion.me_ref, ...), custom_call_target="tpu_custom_call" | custom-call | tf_op jit(solution)/shard_map/flow_products/pallas_call | solution.py:85
  110.8 2.1 %collective-permute-start.4 = (bf16[4,128,256]{2,1,0:T(8,128)(2,1)S(1)}, bf16[4,128,256]{2,1,0:T(8,128)(2,1)S(1)}, u32[]{:S(2)}, u32[]{:S(2)}) collective-permute-start(bf16[4,128,256]{2,1,0:T(8,128)(2,1)S(1)} %get-tuple-element.15), channel_id=1, source_target_pairs={{0,32},{32,0},{64,96},{96,64},{128,160},{160,128},{192,224},{224,1... | collective-permute-start | bytes 786440 | tf_op jit(solution)/shard_map/ppermute | solution.py:112
  112.9 3.3 %collective-permute-start.5 = (bf16[4,128,256]{2,1,0:T(8,128)(2,1)S(1)}, bf16[4,128,256]{2,1,0:T(8,128)(2,1)S(1)}, u32[]{:S(2)}, u32[]{:S(2)}) collective-permute-start(bf16[4,128,256]{2,1,0:T(8,128)(2,1)S(1)} %get-tuple-element.16), channel_id=1, source_target_pairs={{0,480},{32,64},{64,32},{96,128},{128,96},{160,192},{192,160},{224... | collective-permute-start | bytes 786440 | tf_op jit(solution)/shard_map/ppermute | solution.py:116
  116.2 3.1 %collective-permute-start.8 = (bf16[2,128,256]{2,1,0:T(8,128)(2,1)S(1)}, bf16[2,128,256]{2,1,0:T(8,128)(2,1)S(1)}, u32[]{:S(2)}, u32[]{:S(2)}) collective-permute-start(bf16[2,128,256]{2,1,0:T(8,128)(2,1)S(1)} %get-tuple-element.17), channel_id=1, source_target_pairs={{0,64},{32,480},{64,128},{96,32},{128,192},{160,96},{192,256},{224... | collective-permute-start | bytes 393224 | tf_op jit(solution)/shard_map/ppermute | solution.py:112
  119.4 3.1 %collective-permute-start.2 = (bf16[6,128,256]{2,1,0:T(8,128)(2,1)S(1)}, bf16[6,128,256]{2,1,0:T(8,128)(2,1)S(1)}, u32[]{:S(2)}, u32[]{:S(2)}) collective-permute-start(bf16[6,128,256]{2,1,0:T(8,128)(2,1)S(1)} %get-tuple-element.13), channel_id=1, source_target_pairs={{0,32},{32,0},{64,96},{96,64},{128,160},{160,128},{192,224},{224,1... | collective-permute-start | bytes 1179656 | tf_op jit(solution)/shard_map/ppermute | solution.py:112
  122.5 3.3 %collective-permute-start.3 = (bf16[6,128,256]{2,1,0:T(8,128)(2,1)S(1)}, bf16[6,128,256]{2,1,0:T(8,128)(2,1)S(1)}, u32[]{:S(2)}, u32[]{:S(2)}) collective-permute-start(bf16[6,128,256]{2,1,0:T(8,128)(2,1)S(1)} %get-tuple-element.14), channel_id=1, source_target_pairs={{0,480},{32,64},{64,32},{96,128},{128,96},{160,192},{192,160},{224... | collective-permute-start | bytes 1179656 | tf_op jit(solution)/shard_map/ppermute | solution.py:116
  125.9 0.1 add_convert_fusion.3
  126.0 4.4 %collective-permute-start.6 = (bf16[2,128,256]{2,1,0:T(8,128)(2,1)S(1)}, bf16[2,128,256]{2,1,0:T(8,128)(2,1)S(1)}, u32[]{:S(2)}, u32[]{:S(2)}) collective-permute-start(bf16[2,128,256]{2,1,0:T(8,128)(2,1)S(1)} %get-tuple-element.21), channel_id=1, source_target_pairs={{0,416},{32,128},{64,480},{96,192},{128,32},{160,256},{192,96},{22... | collective-permute-start | bytes 393224 | tf_op jit(solution)/shard_map/ppermute | solution.py:116
  130.4 2.3 %collective-permute-start.9 = (bf16[2,128,256]{2,1,0:T(8,128)(2,1)S(1)}, bf16[2,128,256]{2,1,0:T(8,128)(2,1)S(1)}, u32[]{:S(2)}, u32[]{:S(2)}) collective-permute-start(bf16[2,128,256]{2,1,0:T(8,128)(2,1)S(1)} %get-tuple-element.22), channel_id=1, source_target_pairs={{0,96},{32,448},{64,160},{96,0},{128,224},{160,64},{192,288},{224,... | collective-permute-start | bytes 393224 | tf_op jit(solution)/shard_map/ppermute | solution.py:112
  132.7 7.0 %collective-permute-done.6 = bf16[2,128,256]{2,1,0:T(8,128)(2,1)S(1)} collective-permute-done((bf16[2,128,256]{2,1,0:T(8,128)(2,1)S(1)}, bf16[2,128,256]{2,1,0:T(8,128)(2,1)S(1)}, u32[]{:S(2)}, u32[]{:S(2)}) %collective-permute-start.6) | collective-permute-done | bytes 131104 | tf_op jit(solution)/shard_map/ppermute | solution.py:116
  139.8 0.2 add_convert_fusion.4
  140.0 8.6 %collective-permute-start.10 = (bf16[2,128,256]{2,1,0:T(8,128)(2,1)S(1)}, bf16[2,128,256]{2,1,0:T(8,128)(2,1)S(1)}, u32[]{:S(2)}, u32[]{:S(2)}) collective-permute-start(bf16[2,128,256]{2,1,0:T(8,128)(2,1)S(1)} %get-tuple-element.19), channel_id=1, source_target_pairs={{0,416},{32,128},{64,480},{96,192},{128,32},{160,256},{192,96},{22... | collective-permute-start | bytes 393224 | tf_op jit(solution)/shard_map/ppermute | solution.py:116
  148.6 1.9 %collective-permute-start.7 = (bf16[2,128,256]{2,1,0:T(8,128)(2,1)S(1)}, bf16[2,128,256]{2,1,0:T(8,128)(2,1)S(1)}, u32[]{:S(2)}, u32[]{:S(2)}) collective-permute-start(bf16[2,128,256]{2,1,0:T(8,128)(2,1)S(1)} %get-tuple-element.20), channel_id=1, source_target_pairs={{0,96},{32,448},{64,160},{96,0},{128,224},{160,64},{192,288},{224,... | collective-permute-start | bytes 393224 | tf_op jit(solution)/shard_map/ppermute | solution.py:112
  150.5 0.5 collective-permute-done.10
  151.0 9.6 %collective-permute-done.7 = bf16[2,128,256]{2,1,0:T(8,128)(2,1)S(1)} collective-permute-done((bf16[2,128,256]{2,1,0:T(8,128)(2,1)S(1)}, bf16[2,128,256]{2,1,0:T(8,128)(2,1)S(1)}, u32[]{:S(2)}, u32[]{:S(2)}) %collective-permute-start.7) | collective-permute-done | bytes 131104 | tf_op jit(solution)/shard_map/ppermute | solution.py:112
  160.8 1.1 flow_update.1
  (33 shorter events, 0.1 us)
Async XLA Ops:
  46.2 1.1 copy-start
  46.2 1.1 copy-start.9
  46.2 1.1 copy-start.10
  46.2 1.1 copy-start.11
  48.7 10.4 %collective-permute-start = (bf16[16,128,256]{2,1,0:T(8,128)(2,1)S(1)}, bf16[16,128,256]{2,1,0:T(8,128)(2,1)S(1)}, u32[]{:S(2)}, u32[]{:S(2)}) collective-permute-start(bf16[16,128,256]{2,1,0:T(8,128)(2,1)S(1)} %link_products.3), channel_id=1, source_target_pairs={{0,1},{1,0},{2,3},{3,2},{4,5},{5,4},{6,7},{7,6},{8,9},{9,8},{10,11... | collective-permute-start | bytes 3145736 | tf_op jit(solution)/shard_map/ppermute | solution.py:212
  58.2 24.0 %copy-start.2 = (bf16[256,256]{1,0:T(8,128)(2,1)S(1)}, bf16[256,256]{1,0:T(8,128)(2,1)}, u32[]{:S(2)}) copy-start(bf16[256,256]{1,0:T(8,128)(2,1)} %agg_ref.2) | copy-start | bytes 393220
  58.2 24.0 %copy-start.3 = (bf16[256,256]{1,0:T(8,128)(2,1)S(1)}, bf16[256,256]{1,0:T(8,128)(2,1)}, u32[]{:S(2)}) copy-start(bf16[256,256]{1,0:T(8,128)(2,1)} %self_ref.2) | copy-start | bytes 393220
  58.2 24.0 %copy-start.4 = (bf16[256,256]{1,0:T(8,128)(2,1)S(1)}, bf16[256,256]{1,0:T(8,128)(2,1)}, u32[]{:S(2)}) copy-start(bf16[256,256]{1,0:T(8,128)(2,1)} %out_w_ref.2) | copy-start | bytes 393220
  58.3 24.0 %copy-start.8 = (bf16[128,256]{1,0:T(8,128)(2,1)S(1)}, bf16[128,256]{1,0:T(8,128)(2,1)}, u32[]{:S(2)}) copy-start(bf16[128,256]{1,0:T(8,128)(2,1)} %state_ref.2) | copy-start | bytes 196612
  58.3 24.0 %copy-start.12 = (f32[256]{0:T(256)S(1)}, f32[256]{0:T(256)}, u32[]{:S(2)}) copy-start(f32[256]{0:T(256)} %param.20) | copy-start | bytes 3076
  102.5 6.5 %collective-permute-start.1 = (bf16[16,128,256]{2,1,0:T(8,128)(2,1)S(1)}, bf16[16,128,256]{2,1,0:T(8,128)(2,1)S(1)}, u32[]{:S(2)}, u32[]{:S(2)}) collective-permute-start(bf16[16,128,256]{2,1,0:T(8,128)(2,1)S(1)} %all_to_all.11.own_ref), channel_id=1, source_target_pairs={{0,1},{1,0},{2,3},{3,2},{4,5},{5,4},{6,7},{7,6},{8,9},{9,8},{10,11... | collective-permute-start | bytes 3145736 | tf_op jit(solution)/shard_map/ppermute | solution.py:218
  110.8 49.9 %copy-start.1 = (bf16[256,256]{1,0:T(8,128)(2,1)S(1)}, bf16[256,256]{1,0:T(8,128)(2,1)}, u32[]{:S(2)}) copy-start(bf16[256,256]{1,0:T(8,128)(2,1)} %state_ref.3) | copy-start | bytes 393220
  110.8 49.9 %copy-start.5 = (bf16[256,256]{1,0:T(8,128)(2,1)S(1)}, bf16[256,256]{1,0:T(8,128)(2,1)}, u32[]{:S(2)}) copy-start(bf16[256,256]{1,0:T(8,128)(2,1)} %agg_ref.3) | copy-start | bytes 393220
  110.8 49.9 %copy-start.6 = (bf16[256,256]{1,0:T(8,128)(2,1)S(1)}, bf16[256,256]{1,0:T(8,128)(2,1)}, u32[]{:S(2)}) copy-start(bf16[256,256]{1,0:T(8,128)(2,1)} %self_ref.3) | copy-start | bytes 393220
  110.8 49.9 %copy-start.7 = (bf16[256,256]{1,0:T(8,128)(2,1)S(1)}, bf16[256,256]{1,0:T(8,128)(2,1)}, u32[]{:S(2)}) copy-start(bf16[256,256]{1,0:T(8,128)(2,1)} %out_w_ref.3) | copy-start | bytes 393220
  110.8 49.9 %copy-start.13 = (f32[256]{0:T(256)S(1)}, f32[256]{0:T(256)}, u32[]{:S(2)}) copy-start(f32[256]{0:T(256)} %param.24) | copy-start | bytes 3076
  110.8 15.0 %collective-permute-start.4 = (bf16[4,128,256]{2,1,0:T(8,128)(2,1)S(1)}, bf16[4,128,256]{2,1,0:T(8,128)(2,1)S(1)}, u32[]{:S(2)}, u32[]{:S(2)}) collective-permute-start(bf16[4,128,256]{2,1,0:T(8,128)(2,1)S(1)} %get-tuple-element.15), channel_id=1, source_target_pairs={{0,32},{32,0},{64,96},{96,64},{128,160},{160,128},{192,224},{224,1... | collective-permute-start | bytes 786440 | tf_op jit(solution)/shard_map/ppermute | solution.py:112
  112.9 13.0 %collective-permute-start.5 = (bf16[4,128,256]{2,1,0:T(8,128)(2,1)S(1)}, bf16[4,128,256]{2,1,0:T(8,128)(2,1)S(1)}, u32[]{:S(2)}, u32[]{:S(2)}) collective-permute-start(bf16[4,128,256]{2,1,0:T(8,128)(2,1)S(1)} %get-tuple-element.16), channel_id=1, source_target_pairs={{0,480},{32,64},{64,32},{96,128},{128,96},{160,192},{192,160},{224... | collective-permute-start | bytes 786440 | tf_op jit(solution)/shard_map/ppermute | solution.py:116
  116.2 9.6 %collective-permute-start.8 = (bf16[2,128,256]{2,1,0:T(8,128)(2,1)S(1)}, bf16[2,128,256]{2,1,0:T(8,128)(2,1)S(1)}, u32[]{:S(2)}, u32[]{:S(2)}) collective-permute-start(bf16[2,128,256]{2,1,0:T(8,128)(2,1)S(1)} %get-tuple-element.17), channel_id=1, source_target_pairs={{0,64},{32,480},{64,128},{96,32},{128,192},{160,96},{192,256},{224... | collective-permute-start | bytes 393224 | tf_op jit(solution)/shard_map/ppermute | solution.py:112
  119.4 20.4 %collective-permute-start.2 = (bf16[6,128,256]{2,1,0:T(8,128)(2,1)S(1)}, bf16[6,128,256]{2,1,0:T(8,128)(2,1)S(1)}, u32[]{:S(2)}, u32[]{:S(2)}) collective-permute-start(bf16[6,128,256]{2,1,0:T(8,128)(2,1)S(1)} %get-tuple-element.13), channel_id=1, source_target_pairs={{0,32},{32,0},{64,96},{96,64},{128,160},{160,128},{192,224},{224,1... | collective-permute-start | bytes 1179656 | tf_op jit(solution)/shard_map/ppermute | solution.py:112
  122.5 17.2 %collective-permute-start.3 = (bf16[6,128,256]{2,1,0:T(8,128)(2,1)S(1)}, bf16[6,128,256]{2,1,0:T(8,128)(2,1)S(1)}, u32[]{:S(2)}, u32[]{:S(2)}) collective-permute-start(bf16[6,128,256]{2,1,0:T(8,128)(2,1)S(1)} %get-tuple-element.14), channel_id=1, source_target_pairs={{0,480},{32,64},{64,32},{96,128},{128,96},{160,192},{192,160},{224... | collective-permute-start | bytes 1179656 | tf_op jit(solution)/shard_map/ppermute | solution.py:116
  126.0 13.8 %collective-permute-start.6 = (bf16[2,128,256]{2,1,0:T(8,128)(2,1)S(1)}, bf16[2,128,256]{2,1,0:T(8,128)(2,1)S(1)}, u32[]{:S(2)}, u32[]{:S(2)}) collective-permute-start(bf16[2,128,256]{2,1,0:T(8,128)(2,1)S(1)} %get-tuple-element.21), channel_id=1, source_target_pairs={{0,416},{32,128},{64,480},{96,192},{128,32},{160,256},{192,96},{22... | collective-permute-start | bytes 393224 | tf_op jit(solution)/shard_map/ppermute | solution.py:116
  130.4 9.4 %collective-permute-start.9 = (bf16[2,128,256]{2,1,0:T(8,128)(2,1)S(1)}, bf16[2,128,256]{2,1,0:T(8,128)(2,1)S(1)}, u32[]{:S(2)}, u32[]{:S(2)}) collective-permute-start(bf16[2,128,256]{2,1,0:T(8,128)(2,1)S(1)} %get-tuple-element.22), channel_id=1, source_target_pairs={{0,96},{32,448},{64,160},{96,0},{128,224},{160,64},{192,288},{224,... | collective-permute-start | bytes 393224 | tf_op jit(solution)/shard_map/ppermute | solution.py:112
  140.0 11.1 %collective-permute-start.10 = (bf16[2,128,256]{2,1,0:T(8,128)(2,1)S(1)}, bf16[2,128,256]{2,1,0:T(8,128)(2,1)S(1)}, u32[]{:S(2)}, u32[]{:S(2)}) collective-permute-start(bf16[2,128,256]{2,1,0:T(8,128)(2,1)S(1)} %get-tuple-element.19), channel_id=1, source_target_pairs={{0,416},{32,128},{64,480},{96,192},{128,32},{160,256},{192,96},{22... | collective-permute-start | bytes 393224 | tf_op jit(solution)/shard_map/ppermute | solution.py:116
  148.6 12.0 %collective-permute-start.7 = (bf16[2,128,256]{2,1,0:T(8,128)(2,1)S(1)}, bf16[2,128,256]{2,1,0:T(8,128)(2,1)S(1)}, u32[]{:S(2)}, u32[]{:S(2)}) collective-permute-start(bf16[2,128,256]{2,1,0:T(8,128)(2,1)S(1)} %get-tuple-element.20), channel_id=1, source_target_pairs={{0,96},{32,448},{64,160},{96,0},{128,224},{160,64},{192,288},{224,... | collective-permute-start | bytes 393224 | tf_op jit(solution)/shard_map/ppermute | solution.py:112
